TPU v7x, 256 devices: a whole 4x4x8 slice. The times are simulated.
256 devices in a mesh: group: 2 (over core), dp: 16 (over x, z_hi), mp: 8 (over y, z_lo).
Axes of the slice: x: 4, y: 4, z: 8 (z_hi: 4, z_lo: 2; z = z_hi * 2 + z_lo), core: 2. Of those that a mesh axis runs over, the one named last changes fastest.
Arguments:
- noise_seeds: int32 [32], P(('group', 'dp')), may hold values from 0 to 16777215
- timestep_ids: int32 [32], P(('group', 'dp')), may hold values from 0 to 999
- gen_up: bfloat16 [3072, 6144], P(('group', 'dp'), 'mp'), may hold values from -0.109375 to 0.109375
- gen_down: bfloat16 [6144, 3072], P('mp', ('group', 'dp')), may hold values from -0.08930431 to 0.08930431
- score_qkv: bfloat16 [2, 3, 3072, 3072], P('group', None, None, 'mp'), may hold values from -0.109375 to 0.109375
- score_out: bfloat16 [2, 3072, 3072], P('group', 'mp'), may hold values from -0.109375 to 0.109375
Outputs:
- latents: bfloat16 [32, 256, 3072], P(('group', 'dp'), None, 'mp')
- score_gap: bfloat16 [32, 256, 3072], P(('group', 'dp'), None, 'mp')
- grad_up: bfloat16 [3072, 6144], P(('group', 'dp'), 'mp')
- grad_down: bfloat16 [6144, 3072], P('mp', ('group', 'dp'))
All inputs are finite; a program needn't handle non-finite values.
Results may differ from a plain program's by a relative error of at most 0.03.
Values may be sent and summed in bfloat16 or wider, within the bound.
No kernel may reach another device: no remote copies, remote signals or barrier semaphores. Data moves between devices by JAX's collectives and lax.ppermute only.
A program may use at most 128 MiB of HBM per device.

v0:
```python
import jax
import jax.numpy as jnp
from jax import lax
from jax.experimental import pallas as pl
from jax.experimental.pallas import tpu as pltpu
from jax.sharding import Mesh
from jax.sharding import PartitionSpec as P


D = 3072
FF_LOCAL = 768
HEAD_DIM = 128
SEQ = 256
STEPS = 1000
BATCH = 32
SHARD = 96
BLOCK = 384
SAMPLES = ("group", "x", "zh")
MODEL = ("y", "zl")

NORM_EPS = 1e-06
ROOT_THREE = 1.7320508
GELU_SCALE = 0.7978845608


def hop(value, axis, step):
    n = lax.axis_size(axis)
    return lax.ppermute(value, axis, [(i, (i + step) % n) for i in range(n)])


def wide(value):
    return value.astype(jnp.float32)


def narrow(value):
    return value.astype(jnp.bfloat16)


def direct_gather(block, axis):
    return [block] + [hop(block, axis, -k) for k in (1, 2, 3)]


def ring_gather(block, axis):
    half = block.shape[0] // 2
    left = hop(block, axis, 1)
    right = hop(block, axis, -1)
    far_top = hop(left[:half], axis, 1)
    far_bottom = hop(right[half:], axis, -1)
    return [block, right, far_top, far_bottom, left]


def direct_scatter(parts, axis):
    return wide(parts[0]) + sum(wide(hop(parts[k], axis, k)) for k in (1, 3, 2))


def ring_scatter(parts, axis):
    own, right, far, left = parts
    half = own.shape[0] // 2
    for_right = hop(far[:half], axis, 1)
    for_left = hop(far[half:], axis, -1)
    right = jnp.concatenate([narrow(wide(right[:half]) + wide(for_right)), right[half:]])
    left = jnp.concatenate([left[:half], narrow(wide(left[half:]) + wide(for_left))])
    from_left = hop(right, axis, 1)
    from_right = hop(left, axis, -1)
    return wide(own) + wide(from_left) + wide(from_right)


def exchange(parts):
    return lax.all_to_all(parts, MODEL, 0, 0, tiled=True)


def pick(stack, index):
    return lax.dynamic_index_in_dim(stack, index, 0, keepdims=False)


def finish(mixing):
    mixing = mixing ^ mixing >> 15
    mixing = mixing * 1274126177
    mixing = mixing ^ mixing >> 13
    mixing = mixing * 1911520717
    mixing = mixing ^ mixing >> 16
    level = (mixing >> 7 & 65535).astype(jnp.float32)
    return ((level + 0.5) * (2.0 / 65536.0) - 1.0) * ROOT_THREE


def dot(left, right, left_dim=1, right_dim=0):
    return lax.dot_general(
        left, right, (((left_dim,), (right_dim,)), ((), ())), preferred_element_type=jnp.float32
    )


VMEM = pl.BlockSpec(memory_space=pltpu.VMEM)
SMEM = pl.BlockSpec(memory_space=pltpu.SMEM)
HBM = pl.BlockSpec(memory_space=pl.ANY)


def array(*shape, kind=jnp.bfloat16):
    return jax.ShapeDtypeStruct(shape, kind)


def local_call(kernel, ins, outs, flops, moved, scratch=(), limit=40):
    return pl.pallas_call(
        kernel,
        out_shape=outs,
        in_specs=ins,
        out_specs=jax.tree.map(lambda _: VMEM, outs),
        scratch_shapes=scratch,
        compiler_params=pltpu.CompilerParams(vmem_limit_bytes=limit << 20),
        cost_estimate=pl.CostEstimate(flops=flops, bytes_accessed=moved, transcendentals=0),
    )


def lane_chunk(c):
    return pl.ds(pl.multiple_of(c * 256, 256), 256)


def row_tile(i):
    return pl.ds(pl.multiple_of(i * 16, 16), 16)


def noise_kernel(seed_ref, feature_ref, own_ref, crossed_ref):
    start = seed_ref[0] * 747796405

    def tile(i, _):
        tokens = lax.broadcasted_iota(jnp.int32, (16, D), 0) + i * 16
        noise = finish(start + tokens * 1103515245 + feature_ref[...])
        scale = lax.rsqrt(jnp.mean(noise * noise, axis=-1, keepdims=True) + NORM_EPS)
        normed = narrow(noise * scale)
        own_ref[row_tile(i), :] = normed[:, : D // 2]
        crossed_ref[row_tile(i), :] = normed[:, D // 2 :]
        return 0

    lax.fori_loop(0, SEQ // 16, tile, 0)


def up_kernel(own_ref, crossed_ref, n0, n1, n2, n3, r0, r1, far_top, far_bottom, r3, here, away):
    blocks = ((n0, (r0,)), (n1, (r1,)), (n2, (far_top, far_bottom)), (n3, (r3,)))

    def columns(c, _):
        lanes = lane_chunk(c)
        weights = [
            jnp.concatenate([near[:SHARD, lanes]] + [piece[:, lanes] for piece in rest])
            for near, rest in blocks
        ]
        for normed, total in ((own_ref, here), (crossed_ref, away)):
            total[:, lanes] = sum(
                dot(normed[:, k * BLOCK : (k + 1) * BLOCK], block)
                for k, block in enumerate(weights)
            )
        return 0

    lax.fori_loop(0, FF_LOCAL // 256, columns, 0)


def hidden_kernel(here, arrived, before_ref, hidden_ref):
    def tile(i, _):
        rows = row_tile(i)
        value = here[rows, :] + arrived[rows, :]
        before_ref[rows, :] = value
        bend = jnp.tanh(GELU_SCALE * (value + 0.044715 * (value * value * value)))
        hidden_ref[rows, :] = narrow(0.5 * value * (1.0 + bend))
        return 0

    lax.fori_loop(0, SEQ // 16, tile, 0)


def down_kernel(
    at_ref, hidden_ref, crossed_ref, n0, n1, n2, n3, r0, r1, far_top, far_bottom, r3,
    down_ref, parts_ref, away_ref,
):
    group, x, zh = at_ref[0], at_ref[1], at_ref[2]
    for dx, (near, rest) in enumerate(((n0, r0), (n1, r1), (n2, None), (n3, r3))):
        spot = (x + dx) & 3
        for dz in range(4):
            base = pl.multiple_of(((zh + dz) & 3) * SHARD, 32)
            rows = pl.ds(base, SHARD)
            if dz == 0:
                down_ref[spot, rows, :] = near[SHARD:, :]
            elif rest is not None:
                down_ref[spot, rows, :] = rest[(dz - 1) * SHARD : dz * SHARD, :]
            elif dz == 1:
                down_ref[spot, rows, :] = far_top[:SHARD, :]
            elif dz == 2:
                half = SHARD // 2
                down_ref[spot, pl.ds(base, half), :] = far_top[SHARD:, :]
                low = pl.multiple_of(base + half, 16)
                down_ref[spot, pl.ds(low, half), :] = far_bottom[:half, :]
            else:
                down_ref[spot, rows, :] = far_bottom[SHARD // 2 :, :]

    def block(k, _):
        weights = down_ref[k]
        parts_ref[group * 4 + k] = narrow(dot(hidden_ref[...], weights, 1, 1))
        away_ref[k] = narrow(dot(crossed_ref[...], weights, 1, 1))
        return 0

    lax.fori_loop(0, 4, block, 0)


def score_kernel(
    sign_ref, noisy_ref, own_hbm, other_hbm, out_own_hbm, out_other_hbm, gap_ref,
    qkv_w, out_w, normed_ref, qkv_ref, mix_ref, qkv_sem, out_sem,
):
    loads = []
    for net, (source, out_source) in enumerate(
        ((own_hbm, out_own_hbm), (other_hbm, out_other_hbm))
    ):
        for k in range(3):
            loads.append(
                pltpu.make_async_copy(
                    source.at[k], qkv_w.at[net * 3 + k], qkv_sem.at[net * 3 + k]
                )
            )
        loads.append(pltpu.make_async_copy(out_source, out_w.at[net], out_sem.at[net]))
    for k in (0, 1, 2, 4, 5, 6, 3, 7):
        loads[k].start()

    def norm(i, _):
        rows = row_tile(i)
        blocks = [wide(noisy_ref[j, rows, :]) for j in range(8)]
        total = sum(jnp.sum(block * block, axis=-1, keepdims=True) for block in blocks)
        scale = lax.rsqrt(total * (1.0 / D) + NORM_EPS)
        for j in range(8):
            normed_ref[rows, j * BLOCK : (j + 1) * BLOCK] = narrow(blocks[j] * scale)
        return 0

    lax.fori_loop(0, SEQ // 16, norm, 0)

    def network(net, _):
        for own in range(2):

            @pl.when(net == own)
            def _():
                for k in range(3):
                    loads[own * 4 + k].wait()

        def project(k, _):
            qkv_ref[k] = narrow(dot(normed_ref[...], qkv_w[net * 3 + k]))
            return 0

        lax.fori_loop(0, 3, project, 0)
        sign = jnp.where(net == 0, sign_ref[0], -sign_ref[0])

        def attend(head, _):
            lanes = pl.ds(pl.multiple_of(head * HEAD_DIM, HEAD_DIM), HEAD_DIM)
            scores = dot(qkv_ref[0, :, lanes], qkv_ref[1, :, lanes], 1, 1) * HEAD_DIM ** (-0.5)
            expo = jnp.exp(scores)
            probs = narrow(expo / jnp.sum(expo, axis=-1, keepdims=True))
            attended = dot(probs, qkv_ref[2, :, lanes])
            mix_ref[net, :, lanes] = narrow(wide(narrow(attended)) * sign)
            return 0

        lax.fori_loop(0, BLOCK // HEAD_DIM, attend, 0)
        return 0

    lax.fori_loop(0, 2, network, 0)
    loads[3].wait()
    loads[7].wait()

    def emit(j, _):
        columns = pl.ds(pl.multiple_of(j * 2 * BLOCK, 2 * BLOCK), 2 * BLOCK)
        both = narrow(
            dot(mix_ref[0], out_w[0, :, columns]) + dot(mix_ref[1], out_w[1, :, columns])
        )
        gap_ref[2 * j] = both[:, :BLOCK]
        gap_ref[2 * j + 1] = both[:, BLOCK:]
        return 0

    lax.fori_loop(0, 4, emit, 0)


def slope_kernel(at_ref, gap_ref, crossed_ref, down_ref, here, away):
    group = at_ref[0]

    def columns(c, _):
        lanes = lane_chunk(c)
        here[:, lanes] = sum(dot(gap_ref[group * 4 + k], down_ref[k, :, lanes]) for k in range(4))
        away[:, lanes] = sum(dot(crossed_ref[k], down_ref[k, :, lanes]) for k in range(4))
        return 0

    lax.fori_loop(0, FF_LOCAL // 256, columns, 0)


def change_kernel(here, arrived, before_ref, change_ref):
    def tile(i, _):
        rows = row_tile(i)
        value = before_ref[rows, :]
        square = value * value
        bend = jnp.tanh(GELU_SCALE * (value + 0.044715 * square * value))
        turn = 0.5 * (1.0 + bend) + 0.5 * value * (1.0 - bend * bend) * GELU_SCALE * (
            1.0 + 3.0 * 0.044715 * square
        )
        change_ref[rows, :] = narrow((here[rows, :] + arrived[rows, :]) * turn)
        return 0

    lax.fori_loop(0, SEQ // 16, tile, 0)


def down_grad_kernel(at_ref, gap_ref, gap_crossed_ref, hidden_ref, hidden_crossed_ref, grad_ref):
    group, x = at_ref[0], at_ref[1]

    def block(k, _):
        spot = (x + k) & 3
        grad_ref[k] = narrow(
            (
                dot(gap_ref[group * 4 + spot], hidden_ref[...], 0, 0)
                + dot(gap_crossed_ref[spot], hidden_crossed_ref[...], 0, 0)
            )
            * (1.0 / BATCH)
        )
        return 0

    lax.fori_loop(0, 4, block, 0)


def up_grad_kernel(own_ref, own_crossed_ref, change_ref, change_crossed_ref, grad_ref):
    def block(k, _):
        lanes = pl.ds(pl.multiple_of(k * BLOCK, BLOCK), BLOCK)
        grad_ref[k] = narrow(
            (
                dot(own_ref[:, lanes], change_ref[...], 0, 0)
                + dot(own_crossed_ref[:, lanes], change_crossed_ref[...], 0, 0)
            )
            * (1.0 / BATCH)
        )
        return 0

    lax.fori_loop(0, 4, block, 0)


def latent_kernel(ids_ref, shift_ref, feature_ref, parts_ref, latent_ref, noisy_ref):
    start = ids_ref[0] * 747796405
    shift = shift_ref[0]

    def tile(i, _):
        rows = row_tile(i)
        tokens = lax.broadcasted_iota(jnp.int32, (16, BLOCK), 0) + i * 16
        mixing = start + tokens * 1103515245 + feature_ref[...]
        mixed = sum(wide(parts_ref[j, rows, :]) for j in range(8))
        latent = narrow(finish(mixing) + mixed)
        latent_ref[rows, :] = latent
        noisy = narrow((1.0 - shift) * wide(latent) + shift * finish(mixing + 374761393))
        for j in range(8):
            noisy_ref[j, rows, :] = noisy
        return 0

    lax.fori_loop(0, SEQ // 16, tile, 0)


def gap_kernel(parts_ref, gap_ref, copies_ref):
    def tile(i, _):
        rows = row_tile(i)
        gap = narrow(sum(wide(parts_ref[j, rows, :]) for j in range(8)))
        gap_ref[rows, :] = gap
        for j in range(8):
            copies_ref[j, rows, :] = gap
        return 0

    lax.fori_loop(0, SEQ // 16, tile, 0)


def swap(value):
    return hop(value, "group", 1)


def step(noise_seeds, timestep_ids, gen_up, gen_down, score_qkv, score_out):
    group, x, zh = (lax.axis_index(a) for a in SAMPLES)
    y, zl = (lax.axis_index(a) for a in MODEL)

    at = jnp.stack([group, x, zh])
    half_d = array(SEQ, D // 2)
    before_kind = array(SEQ, FF_LOCAL, kind=jnp.float32)
    hidden_kind = array(SEQ, FF_LOCAL)
    grad_kind = array(4, BLOCK, FF_LOCAL)
    matmul = 1_200_000_000

    down_shard = gen_down.T
    up_z = direct_gather(gen_up, "zh")
    near = direct_gather(jnp.concatenate([gen_up, down_shard]), "x")
    up_cat = jnp.concatenate(up_z[1:])
    up_rest = ring_gather(up_cat, "x")
    down_z = direct_gather(down_shard, "zh")
    down_rest = ring_gather(jnp.concatenate(down_z[1:]), "x")
    qkv_own, out_own = score_qkv[0], score_out[0]
    qkv_other, out_other = swap(qkv_own), swap(out_own)

    index = lax.iota(jnp.int32, D)
    feature = (
        (((index // 1536) ^ group) * 4 + ((index // BLOCK + x) & 3)) * 4
        + ((index // SHARD + zh) & 3)
    ) * SHARD + index % SHARD
    normed, normed_away = local_call(
        noise_kernel, [SMEM, VMEM], (half_d, half_d), 30_000_000, 1_600_000
    )(noise_seeds, (feature * 668265263)[None])
    normed_crossed = swap(normed_away)
    here, away = local_call(
        up_kernel, [VMEM] * 11, (before_kind, before_kind), matmul, 5_000_000
    )(normed, normed_crossed, *near, *up_rest)
    before, hidden = local_call(
        hidden_kernel, [VMEM] * 2, (before_kind, hidden_kind), 3_000_000, 2_800_000
    )(here, swap(away))
    hidden_crossed = swap(hidden)
    down_all, parts, parts_away = local_call(
        down_kernel,
        [SMEM] + [VMEM] * 11,
        (grad_kind, array(8, SEQ, BLOCK), array(4, SEQ, BLOCK)),
        matmul,
        8_000_000,
    )(at, hidden, hidden_crossed, *near, *down_rest)
    parts = lax.dynamic_update_slice_in_dim(parts, swap(parts_away), (1 - group) * 4, 0)

    local = lax.iota(jnp.int32, BLOCK) + (y * 2 + zl) * BLOCK
    shift = (timestep_ids[0].astype(jnp.float32) + 0.5) / STEPS
    eight_kind = array(8, SEQ, BLOCK)
    latent, noisy = local_call(
        latent_kernel, [SMEM, SMEM, VMEM, VMEM], (array(SEQ, BLOCK), eight_kind), 9_000_000, 4_000_000
    )(noise_seeds, shift[None], (local * 668265263)[None], exchange(parts))
    noisy_all = exchange(noisy)
    sign = wide(2 * group - 1)[None]
    gap_parts = local_call(
        score_kernel,
        [SMEM, VMEM] + [HBM] * 4,
        array(8, SEQ, BLOCK),
        5_000_000_000,
        20_000_000,
        scratch=[
            pltpu.VMEM((6, D, BLOCK), jnp.bfloat16),
            pltpu.VMEM((2, BLOCK, D), jnp.bfloat16),
            pltpu.VMEM((SEQ, D), jnp.bfloat16),
            pltpu.VMEM((3, SEQ, BLOCK), jnp.bfloat16),
            pltpu.VMEM((2, SEQ, BLOCK), jnp.bfloat16),
            pltpu.SemaphoreType.DMA((6,)),
            pltpu.SemaphoreType.DMA((2,)),
        ],
    )(sign, noisy_all, qkv_own, qkv_other, out_own, out_other)
    gap, gap_copies = local_call(
        gap_kernel, [VMEM], (array(SEQ, BLOCK), eight_kind), 1_000_000, 4_000_000
    )(exchange(gap_parts))
    gap_all = exchange(gap_copies)
    gap_crossed = swap(lax.dynamic_slice_in_dim(gap_all, (1 - group) * 4, 4, 0))
    down_grads = local_call(down_grad_kernel, [SMEM] + [VMEM] * 4, grad_kind, matmul, 5_000_000)(
        at, gap_all, gap_crossed, hidden, hidden_crossed
    )
    down_sum = narrow(ring_scatter([down_grads[k] for k in range(4)], "x"))
    down_sum = down_sum.reshape(4, SHARD, FF_LOCAL)
    grad_down = narrow(direct_scatter([pick(down_sum, (zh + dz) & 3) for dz in range(4)], "zh")).T

    here, away = local_call(
        slope_kernel, [SMEM] + [VMEM] * 3, (before_kind, before_kind), matmul, 6_000_000
    )(at, gap_all, gap_crossed, down_all)
    change = local_call(change_kernel, [VMEM] * 3, hidden_kind, 5_000_000, 2_800_000)(
        here, swap(away), before
    )
    up_grads = local_call(up_grad_kernel, [VMEM] * 4, grad_kind, matmul, 5_000_000)(
        normed, normed_crossed, change, swap(change)
    )
    up_sum = narrow(ring_scatter([up_grads[k] for k in range(4)], "x"))
    up_sum = up_sum.reshape(4, SHARD, FF_LOCAL)
    grad_up = narrow(direct_scatter([up_sum[dz] for dz in range(4)], "zh"))
    return (latent[None], gap[None], grad_up, grad_down)


def solution(mesh):
    split = Mesh(
        mesh.devices.reshape(mesh.shape["group"], 4, 4, 4, 2), ("group", "x", "zh", "y", "zl")
    )
    in_specs = (
        P(SAMPLES),
        P(SAMPLES),
        P(SAMPLES, MODEL),
        P(MODEL, SAMPLES),
        P("group", None, None, MODEL),
        P("group", MODEL, None),
    )
    out_specs = (
        P(SAMPLES, None, MODEL),
        P(SAMPLES, None, MODEL),
        P(SAMPLES, MODEL),
        P(MODEL, SAMPLES),
    )
    return jax.shard_map(step, mesh=split, in_specs=in_specs, out_specs=out_specs, check_vma=False)
```

profile of v0, /device:TPU:2, one launch (start us, length us, event | category | flops | bytes accessed | tf_op | source)
XLA Modules:
  0.0 298.1 jit_solution(10169215055338495532)
XLA Ops:
  0.6 6.4 %collective-permute-start.4 = (bf16[96,768]{1,0:T(8,128)(2,1)}, bf16[96,768]{1,0:T(8,128)(2,1)S(1)}, u32[]{:S(2)}, u32[]{:S(2)}) collective-permute-start(bf16[96,768]{1,0:T(8,128)(2,1)} %param.8), channel_id=1, source_target_pairs={{0,24},{8,0},{16,8},{24,16},{1,25},{9,1},{17,9},{25,17},{2,26},{10... | collective-permute-start | bytes 442376 | tf_op jit(solution)/shard_map/ppermute | solution.py:28
  8.0 2.8 collective-permute-start.6
  11.6 3.5 %shard_map.93 = (bf16[256,1536]{1,0:T(8,128)(2,1)S(1)}, bf16[256,1536]{1,0:T(8,128)(2,1)S(1)}) custom-call(s32[1]{0:T(128)S(6)} %copy.15.seed_ref.ids_ref, s32[1,3072]{1,0:T(1,128)S(1)} %fusion.11.feature_ref), custom_call_target="tpu_custom_call" | custom-call | flops 30000000 | bytes 1600000 | tf_op jit(solution)/shard_map/pallas_call | solution.py:392
  15.2 4.8 %collective-permute-done.4 = bf16[96,768]{1,0:T(8,128)(2,1)S(1)} collective-permute-done((bf16[96,768]{1,0:T(8,128)(2,1)}, bf16[96,768]{1,0:T(8,128)(2,1)S(1)}, u32[]{:S(2)}, u32[]{:S(2)}) %collective-permute-start.4) | collective-permute-done | bytes 147488 | tf_op jit(solution)/shard_map/ppermute | solution.py:28
  26.9 9.1 %collective-permute-done.8.r3 = bf16[288,768]{1,0:T(8,128)(2,1)S(1)} collective-permute-done((bf16[288,768]{1,0:T(8,128)(2,1)S(1)}, bf16[288,768]{1,0:T(8,128)(2,1)S(1)}, u32[]{:S(2)}, u32[]{:S(2)}) %collective-permute-start.8) | collective-permute-done | bytes 442400 | tf_op jit(solution)/shard_map/ppermute | solution.py:28
  35.9 3.0 collective-permute-start.3
  39.1 4.9 %collective-permute-done.1.n1 = bf16[192,768]{1,0:T(8,128)(2,1)S(1)} collective-permute-done((bf16[192,768]{1,0:T(8,128)(2,1)S(1)}, bf16[192,768]{1,0:T(8,128)(2,1)S(1)}, u32[]{:S(2)}, u32[]{:S(2)}) %collective-permute-start.1) | collective-permute-done | bytes 294944 | tf_op jit(solution)/shard_map/ppermute | solution.py:28
  44.0 4.1 %collective-permute-done.2.n2 = bf16[192,768]{1,0:T(8,128)(2,1)S(1)} collective-permute-done((bf16[192,768]{1,0:T(8,128)(2,1)S(1)}, bf16[192,768]{1,0:T(8,128)(2,1)S(1)}, u32[]{:S(2)}, u32[]{:S(2)}) %collective-permute-start.2) | collective-permute-done | bytes 294944 | tf_op jit(solution)/shard_map/ppermute | solution.py:28
  52.7 4.2 %collective-permute-start.13 = (bf16[96,768]{1,0:T(8,128)(2,1)S(1)}, bf16[96,768]{1,0:T(8,128)(2,1)S(1)}, u32[]{:S(2)}, u32[]{:S(2)}) collective-permute-start(bf16[96,768]{1,0:T(8,128)(2,1)S(1)} %bitcast.72), channel_id=1, source_target_pairs={{0,24},{8,0},{16,8},{24,16},{1,25},{9,1},{17,9},{25,17},{2,26},{10... | collective-permute-start | bytes 442376 | tf_op jit(solution)/shard_map/ppermute | solution.py:28
  56.9 2.6 collective-permute-start.14
  61.8 7.7 %collective-permute-done.13 = bf16[96,768]{1,0:T(8,128)(2,1)S(1)} collective-permute-done((bf16[96,768]{1,0:T(8,128)(2,1)S(1)}, bf16[96,768]{1,0:T(8,128)(2,1)S(1)}, u32[]{:S(2)}, u32[]{:S(2)}) %collective-permute-start.13) | collective-permute-done | bytes 147488 | tf_op jit(solution)/shard_map/ppermute | solution.py:28
  73.6 8.4 %collective-permute-done.17.r3 = bf16[288,768]{1,0:T(8,128)(2,1)S(1)} collective-permute-done((bf16[288,768]{1,0:T(8,128)(2,1)S(1)}, bf16[288,768]{1,0:T(8,128)(2,1)S(1)}, u32[]{:S(2)}, u32[]{:S(2)}) %collective-permute-start.17) | collective-permute-done | bytes 442400 | tf_op jit(solution)/shard_map/ppermute | solution.py:28
  85.4 4.4 %collective-permute-done.18.far_top = bf16[144,768]{1,0:T(8,128)(2,1)S(1)} collective-permute-done((bf16[144,768]{1,0:T(8,128)(2,1)S(1)}, bf16[144,768]{1,0:T(8,128)(2,1)S(1)}, u32[]{:S(2)}, u32[]{:S(2)}) %collective-permute-start.18) | collective-permute-done | bytes 221216 | tf_op jit(solution)/shard_map/ppermute | solution.py:28
  90.4 4.0 %shard_map.96 = (bf16[4,384,768]{2,1,0:T(8,128)(2,1)S(1)}, bf16[8,256,384]{2,1,0:T(8,128)(2,1)}, bf16[4,256,384]{2,1,0:T(8,128)(2,1)S(1)}) custom-call(s32[3]{0:T(128)S(1)} %pad_add_fusion.at_ref, bf16[256,768]{1,0:T(8,128)(2,1)S(1)} %get-tuple-element.23.hidden_ref, bf16[256,768]{1,0:T(8,128)(2,1)S(1)} %collective-permute-done.12.crossed_ref.hidden_crossed_ref, ...), custom_call_target="tpu_custom_call" | custom-call | flops 1200000000 | bytes 8000000 | tf_op jit(solution)/shard_map/pallas_call | solution.py:403
  99.1 10.2 %all-to-all-start = ((bf16[8,256,384]{2,1,0:T(8,128)(2,1)}), bf16[8,256,384]{2,1,0:T(8,128)(2,1)S(1)}, u32[]{:S(2)}, u32[]{:S(2)}) async-start(bf16[8,256,384]{2,1,0:T(8,128)(2,1)} %constant_dynamic-update-slice_fusion.6), calls=%async_computation | async-start | bytes 3145728 | tf_op jit(solution)/shard_map/all_to_all | solution.py:69
  109.9 21.0 %all-to-all-done.parts_ref = bf16[8,256,384]{2,1,0:T(8,128)(2,1)S(1)} async-done(((bf16[8,256,384]{2,1,0:T(8,128)(2,1)}), bf16[8,256,384]{2,1,0:T(8,128)(2,1)S(1)}, u32[]{:S(2)}, u32[]{:S(2)}) %all-to-all-start) | async-done | bytes 1572896 | tf_op jit(solution)/shard_map/all_to_all | solution.py:69
  133.7 3.6 %all-to-all-start.1 = ((bf16[8,256,384]{2,1,0:T(8,128)(2,1)}), bf16[8,256,384]{2,1,0:T(8,128)(2,1)S(1)}, u32[]{:S(2)}, u32[]{:S(2)}) async-start(bf16[8,256,384]{2,1,0:T(8,128)(2,1)} %copy-done.6), calls=%async_computation.1 | async-start | bytes 3145728 | tf_op jit(solution)/shard_map/all_to_all | solution.py:69
  137.4 4.9 %collective-permute-done.22.out_other_hbm = bf16[384,3072]{1,0:T(8,128)(2,1)} collective-permute-done((bf16[384,3072]{1,0:T(8,128)(2,1)}, bf16[384,3072]{1,0:T(8,128)(2,1)}, u32[]{:S(2)}, u32[]{:S(2)}) %collective-permute-start.22) | collective-permute-done | bytes 2359328 | tf_op jit(solution)/shard_map/ppermute | solution.py:28
  142.3 15.8 %all-to-all-done.1.noisy_ref = bf16[8,256,384]{2,1,0:T(8,128)(2,1)S(1)} async-done(((bf16[8,256,384]{2,1,0:T(8,128)(2,1)}), bf16[8,256,384]{2,1,0:T(8,128)(2,1)S(1)}, u32[]{:S(2)}, u32[]{:S(2)}) %all-to-all-start.1) | async-done | bytes 1572896 | tf_op jit(solution)/shard_map/all_to_all | solution.py:69
  159.8 13.9 %shard_map.98 = bf16[8,256,384]{2,1,0:T(8,128)(2,1)S(1)} custom-call(f32[1]{0:T(128)} %bitcast.5.sign_ref, bf16[8,256,384]{2,1,0:T(8,128)(2,1)S(1)} %all-to-all-done.1.noisy_ref, bf16[3,3072,384]{2,1,0:T(8,128)(2,1)} %bitcast.6.own_hbm, bf16[3,3072,384]{2,1,0:T(8,128)(2,1)} %collective-permute-done.21.other_hbm, bf16[384,3072]{1,0:T(8,128)(2,1)S(1)} %bitcast.68, ...), custom_call_target="tpu_custom_call" | custom-call | flops 5000000000 | bytes 20000000 | tf_op jit(solution)/shard_map/pallas_call | solution.py:420
  173.7 24.2 %all_to_all.20.parts_ref = bf16[8,256,384]{2,1,0:T(8,128)(2,1)S(1)} all-to-all(bf16[8,256,384]{2,1,0:T(8,128)(2,1)S(1)} %shard_map.98), channel_id=1, replica_groups=mesh['group'=2,'x'=4,'zh'=4,'y'=4,'zl'=2] {'y','zl'}, dimensions={0} | all-to-all | bytes 3145728 | tf_op jit(solution)/shard_map/all_to_all | solution.py:69
  198.9 22.9 %all_to_all.21.gap_ref = bf16[8,256,384]{2,1,0:T(8,128)(2,1)S(1)} all-to-all(bf16[8,256,384]{2,1,0:T(8,128)(2,1)S(1)} %get-tuple-element.29), channel_id=1, replica_groups=mesh['group'=2,'x'=4,'zh'=4,'y'=4,'zl'=2] {'y','zl'}, dimensions={0} | all-to-all | bytes 3145728 | tf_op jit(solution)/shard_map/all_to_all | solution.py:69
  224.3 2.7 shard_map.100
  230.3 2.6 shard_map.103
  237.6 2.7 collective-permute-start.26
  255.9 8.8 %collective-permute-done.36 = bf16[384,768]{1,0:T(8,128)(2,1)} collective-permute-done((bf16[384,768]{1,0:T(8,128)(2,1)}, bf16[384,768]{1,0:T(8,128)(2,1)}, u32[]{:S(2)}, u32[]{:S(2)}) %collective-permute-start.36) | collective-permute-done | bytes 589856 | tf_op jit(solution)/shard_map/ppermute | solution.py:28
  267.7 4.8 %collective-permute-start.39 = (bf16[96,768]{1,0:T(8,128)(2,1)S(1)}, bf16[96,768]{1,0:T(8,128)(2,1)S(1)}, u32[]{:S(2)}, u32[]{:S(2)}) collective-permute-start(bf16[96,768]{1,0:T(8,128)(2,1)S(1)} %get-tuple-element.47), channel_id=1, source_target_pairs={{0,16},{8,24},{16,0},{24,8},{1,17},{9,25},{17,1},{25,9},{2,18},{10... | collective-permute-start | bytes 442376 | tf_op jit(solution)/shard_map/ppermute | solution.py:28
  273.0 2.5 collective-permute-start.37
  278.2 4.8 %collective-permute-start.32 = (bf16[96,768]{1,0:T(8,128)(2,1)S(1)}, bf16[96,768]{1,0:T(8,128)(2,1)S(1)}, u32[]{:S(2)}, u32[]{:S(2)}) collective-permute-start(bf16[96,768]{1,0:T(8,128)(2,1)S(1)} %get-tuple-element.50), channel_id=1, source_target_pairs={{0,16},{8,24},{16,0},{24,8},{1,17},{9,25},{17,1},{25,9},{2,18},{10... | collective-permute-start | bytes 442376 | tf_op jit(solution)/shard_map/ppermute | solution.py:28
  283.5 2.5 collective-permute-start.30
  286.7 7.3 %collective-permute-done.32 = bf16[96,768]{1,0:T(8,128)(2,1)S(1)} collective-permute-done((bf16[96,768]{1,0:T(8,128)(2,1)S(1)}, bf16[96,768]{1,0:T(8,128)(2,1)S(1)}, u32[]{:S(2)}, u32[]{:S(2)}) %collective-permute-start.32) | collective-permute-done | bytes 147488 | tf_op jit(solution)/shard_map/ppermute | solution.py:28
  294.0 3.4 %collective-permute-done.30 = bf16[96,768]{1,0:T(8,128)(2,1)S(1)} collective-permute-done((bf16[96,768]{1,0:T(8,128)(2,1)S(1)}, bf16[96,768]{1,0:T(8,128)(2,1)S(1)}, u32[]{:S(2)}, u32[]{:S(2)}) %collective-permute-start.30) | collective-permute-done | bytes 147488 | tf_op jit(solution)/shard_map/ppermute | solution.py:28
  (115 shorter events, 67.6 us)
Async XLA Ops:
  0.6 19.3 %collective-permute-start.4 = (bf16[96,768]{1,0:T(8,128)(2,1)}, bf16[96,768]{1,0:T(8,128)(2,1)S(1)}, u32[]{:S(2)}, u32[]{:S(2)}) collective-permute-start(bf16[96,768]{1,0:T(8,128)(2,1)} %param.8), channel_id=1, source_target_pairs={{0,24},{8,0},{16,8},{24,16},{1,25},{9,1},{17,9},{25,17},{2,26},{10... | collective-permute-start | bytes 442376 | tf_op jit(solution)/shard_map/ppermute | solution.py:28
  7.0 13.7 %collective-permute-start.5 = (bf16[96,768]{1,0:T(8,128)(2,1)}, bf16[96,768]{1,0:T(8,128)(2,1)S(1)}, u32[]{:S(2)}, u32[]{:S(2)}) collective-permute-start(bf16[96,768]{1,0:T(8,128)(2,1)} %param.8), channel_id=1, source_target_pairs={{0,16},{8,24},{16,0},{24,8},{1,17},{9,25},{17,1},{25,9},{2,18},{10... | collective-permute-start | bytes 442376 | tf_op jit(solution)/shard_map/ppermute | solution.py:28
  8.0 12.7 %collective-permute-start.6 = (bf16[96,768]{1,0:T(8,128)(2,1)}, bf16[96,768]{1,0:T(8,128)(2,1)S(1)}, u32[]{:S(2)}, u32[]{:S(2)}) collective-permute-start(bf16[96,768]{1,0:T(8,128)(2,1)} %param.8), channel_id=1, source_target_pairs={{0,8},{8,16},{16,24},{24,0},{1,9},{9,17},{17,25},{25,1},{2,10},{10... | collective-permute-start | bytes 442376 | tf_op jit(solution)/shard_map/ppermute | solution.py:28
  15.1 33.1 %collective-permute-start = (bf16[256,1536]{1,0:T(8,128)(2,1)S(1)}, bf16[256,1536]{1,0:T(8,128)(2,1)S(1)}, u32[]{:S(2)}, u32[]{:S(2)}) collective-permute-start(bf16[256,1536]{1,0:T(8,128)(2,1)S(1)} %get-tuple-element.20), channel_id=1, source_target_pairs={{0,128},{128,0},{1,129},{129,1},{2,130},{130,2},{3,131},{131,3},{4... | collective-permute-start | bytes 2359304 | tf_op jit(solution)/shard_map/ppermute | solution.py:28
  20.7 15.2 %collective-permute-start.8 = (bf16[288,768]{1,0:T(8,128)(2,1)S(1)}, bf16[288,768]{1,0:T(8,128)(2,1)S(1)}, u32[]{:S(2)}, u32[]{:S(2)}) collective-permute-start(bf16[288,768]{1,0:T(8,128)(2,1)S(1)} %constant_dynamic-update-slice_fusion.r0), channel_id=1, source_target_pairs={{0,32},{32,64},{64,96},{96,0},{1,33},{33,65},{65,97},{97,1},{2,34}... | collective-permute-start | bytes 1327112 | tf_op jit(solution)/shard_map/ppermute | solution.py:28
  22.3 16.7 %collective-permute-start.7 = (bf16[288,768]{1,0:T(8,128)(2,1)S(1)}, bf16[288,768]{1,0:T(8,128)(2,1)S(1)}, u32[]{:S(2)}, u32[]{:S(2)}) collective-permute-start(bf16[288,768]{1,0:T(8,128)(2,1)S(1)} %constant_dynamic-update-slice_fusion.r0), channel_id=1, source_target_pairs={{0,96},{32,0},{64,32},{96,64},{1,97},{33,1},{65,33},{97,65},{2,98}... | collective-permute-start | bytes 1327112 | tf_op jit(solution)/shard_map/ppermute | solution.py:28
  23.8 20.2 %collective-permute-start.1 = (bf16[192,768]{1,0:T(8,128)(2,1)S(1)}, bf16[192,768]{1,0:T(8,128)(2,1)S(1)}, u32[]{:S(2)}, u32[]{:S(2)}) collective-permute-start(bf16[192,768]{1,0:T(8,128)(2,1)S(1)} %pad_maximum_fusion.4.n0), channel_id=1, source_target_pairs={{0,96},{32,0},{64,32},{96,64},{1,97},{33,1},{65,33},{97,65},{2,98}... | collective-permute-start | bytes 884744 | tf_op jit(solution)/shard_map/ppermute | solution.py:28
  25.6 22.5 %collective-permute-start.2 = (bf16[192,768]{1,0:T(8,128)(2,1)S(1)}, bf16[192,768]{1,0:T(8,128)(2,1)S(1)}, u32[]{:S(2)}, u32[]{:S(2)}) collective-permute-start(bf16[192,768]{1,0:T(8,128)(2,1)S(1)} %pad_maximum_fusion.4.n0), channel_id=1, source_target_pairs={{0,64},{32,96},{64,0},{96,32},{1,65},{33,97},{65,1},{97,33},{2,66}... | collective-permute-start | bytes 884744 | tf_op jit(solution)/shard_map/ppermute | solution.py:28
  35.9 12.2 %collective-permute-start.3 = (bf16[192,768]{1,0:T(8,128)(2,1)S(1)}, bf16[192,768]{1,0:T(8,128)(2,1)S(1)}, u32[]{:S(2)}, u32[]{:S(2)}) collective-permute-start(bf16[192,768]{1,0:T(8,128)(2,1)S(1)} %pad_maximum_fusion.4.n0), channel_id=1, source_target_pairs={{0,32},{32,64},{64,96},{96,0},{1,33},{33,65},{65,97},{97,1},{2,34}... | collective-permute-start | bytes 884744 | tf_op jit(solution)/shard_map/ppermute | solution.py:28
  52.6 20.0 %collective-permute-start.11 = (f32[256,768]{1,0:T(8,128)S(1)}, f32[256,768]{1,0:T(8,128)S(1)}, u32[]{:S(2)}, u32[]{:S(2)}) collective-permute-start(f32[256,768]{1,0:T(8,128)S(1)} %get-tuple-element.22), channel_id=1, source_target_pairs={{0,128},{128,0},{1,129},{129,1},{2,130},{130,2},{3,131},{131,3},{4... | collective-permute-start | bytes 2359304 | tf_op jit(solution)/shard_map/ppermute | solution.py:28
  52.7 16.9 %collective-permute-start.13 = (bf16[96,768]{1,0:T(8,128)(2,1)S(1)}, bf16[96,768]{1,0:T(8,128)(2,1)S(1)}, u32[]{:S(2)}, u32[]{:S(2)}) collective-permute-start(bf16[96,768]{1,0:T(8,128)(2,1)S(1)} %bitcast.72), channel_id=1, source_target_pairs={{0,24},{8,0},{16,8},{24,16},{1,25},{9,1},{17,9},{25,17},{2,26},{10... | collective-permute-start | bytes 442376 | tf_op jit(solution)/shard_map/ppermute | solution.py:28
  56.9 13.5 %collective-permute-start.14 = (bf16[96,768]{1,0:T(8,128)(2,1)S(1)}, bf16[96,768]{1,0:T(8,128)(2,1)S(1)}, u32[]{:S(2)}, u32[]{:S(2)}) collective-permute-start(bf16[96,768]{1,0:T(8,128)(2,1)S(1)} %bitcast.73), channel_id=1, source_target_pairs={{0,16},{8,24},{16,0},{24,8},{1,17},{9,25},{17,1},{25,9},{2,18},{10... | collective-permute-start | bytes 442376 | tf_op jit(solution)/shard_map/ppermute | solution.py:28
  59.5 10.9 %collective-permute-start.15 = (bf16[96,768]{1,0:T(8,128)(2,1)S(1)}, bf16[96,768]{1,0:T(8,128)(2,1)S(1)}, u32[]{:S(2)}, u32[]{:S(2)}) collective-permute-start(bf16[96,768]{1,0:T(8,128)(2,1)S(1)} %bitcast.74), channel_id=1, source_target_pairs={{0,8},{8,16},{16,24},{24,0},{1,9},{9,17},{17,25},{25,1},{2,10},{10... | collective-permute-start | bytes 442376 | tf_op jit(solution)/shard_map/ppermute | solution.py:28
  70.4 11.5 %collective-permute-start.17 = (bf16[288,768]{1,0:T(8,128)(2,1)S(1)}, bf16[288,768]{1,0:T(8,128)(2,1)S(1)}, u32[]{:S(2)}, u32[]{:S(2)}) collective-permute-start(bf16[288,768]{1,0:T(8,128)(2,1)S(1)} %constant_dynamic-update-slice_fusion.3.r0), channel_id=1, source_target_pairs={{0,32},{32,64},{64,96},{96,0},{1,33},{33,65},{65,97},{97,1},{2,34}... | collective-permute-start | bytes 1327112 | tf_op jit(solution)/shard_map/ppermute | solution.py:28
  71.8 12.4 %collective-permute-start.16 = (bf16[288,768]{1,0:T(8,128)(2,1)S(1)}, bf16[288,768]{1,0:T(8,128)(2,1)S(1)}, u32[]{:S(2)}, u32[]{:S(2)}) collective-permute-start(bf16[288,768]{1,0:T(8,128)(2,1)S(1)} %constant_dynamic-update-slice_fusion.3.r0), channel_id=1, source_target_pairs={{0,96},{32,0},{64,32},{96,64},{1,97},{33,1},{65,33},{97,65},{2,98}... | collective-permute-start | bytes 1327112 | tf_op jit(solution)/shard_map/ppermute | solution.py:28
  72.5 69.8 %collective-permute-start.21 = (bf16[3,3072,384]{2,1,0:T(8,128)(2,1)}, bf16[3,3072,384]{2,1,0:T(8,128)(2,1)}, u32[]{:S(2)}, u32[]{:S(2)}) collective-permute-start(bf16[3,3072,384]{2,1,0:T(8,128)(2,1)} %bitcast.6.own_hbm), channel_id=1, source_target_pairs={{0,128},{128,0},{1,129},{129,1},{2,130},{130,2},{3,131},{131,3},{4... | collective-permute-start | bytes 21233672 | tf_op jit(solution)/shard_map/ppermute | solution.py:28
  73.0 17.4 %collective-permute-start.12 = (bf16[256,768]{1,0:T(8,128)(2,1)S(1)}, bf16[256,768]{1,0:T(8,128)(2,1)S(1)}, u32[]{:S(2)}, u32[]{:S(2)}) collective-permute-start(bf16[256,768]{1,0:T(8,128)(2,1)S(1)} %get-tuple-element.23.hidden_ref), channel_id=1, source_target_pairs={{0,128},{128,0},{1,129},{129,1},{2,130},{130,2},{3,131},{131,3},{4... | collective-permute-start | bytes 1179656 | tf_op jit(solution)/shard_map/ppermute | solution.py:28
  99.1 31.8 %all-to-all-start = ((bf16[8,256,384]{2,1,0:T(8,128)(2,1)}), bf16[8,256,384]{2,1,0:T(8,128)(2,1)S(1)}, u32[]{:S(2)}, u32[]{:S(2)}) async-start(bf16[8,256,384]{2,1,0:T(8,128)(2,1)} %constant_dynamic-update-slice_fusion.6), calls=%async_computation | async-start | bytes 3145728 | tf_op jit(solution)/shard_map/all_to_all | solution.py:69
  133.7 24.3 %all-to-all-start.1 = ((bf16[8,256,384]{2,1,0:T(8,128)(2,1)}), bf16[8,256,384]{2,1,0:T(8,128)(2,1)S(1)}, u32[]{:S(2)}, u32[]{:S(2)}) async-start(bf16[8,256,384]{2,1,0:T(8,128)(2,1)} %copy-done.6), calls=%async_computation.1 | async-start | bytes 3145728 | tf_op jit(solution)/shard_map/all_to_all | solution.py:69
  234.8 10.8 %collective-permute-start.35 = (bf16[192,768]{1,0:T(8,128)(2,1)S(1)}, bf16[192,768]{1,0:T(8,128)(2,1)S(1)}, u32[]{:S(2)}, u32[]{:S(2)}) collective-permute-start(bf16[192,768]{1,0:T(8,128)(2,1)S(1)} %get-tuple-element.37), channel_id=1, source_target_pairs={{0,96},{32,0},{64,32},{96,64},{1,97},{33,1},{65,33},{97,65},{2,98}... | collective-permute-start | bytes 884744 | tf_op jit(solution)/shard_map/ppermute | solution.py:28
  237.6 12.0 %collective-permute-start.26 = (bf16[192,768]{1,0:T(8,128)(2,1)S(1)}, bf16[192,768]{1,0:T(8,128)(2,1)S(1)}, u32[]{:S(2)}, u32[]{:S(2)}) collective-permute-start(bf16[192,768]{1,0:T(8,128)(2,1)S(1)} %get-tuple-element.42), channel_id=1, source_target_pairs={{0,32},{32,64},{64,96},{96,0},{1,33},{33,65},{65,97},{97,1},{2,34}... | collective-permute-start | bytes 884744 | tf_op jit(solution)/shard_map/ppermute | solution.py:28
  240.2 11.7 %collective-permute-start.28 = (bf16[192,768]{1,0:T(8,128)(2,1)S(1)}, bf16[192,768]{1,0:T(8,128)(2,1)S(1)}, u32[]{:S(2)}, u32[]{:S(2)}) collective-permute-start(bf16[192,768]{1,0:T(8,128)(2,1)S(1)} %get-tuple-element.43), channel_id=1, source_target_pairs={{0,96},{32,0},{64,32},{96,64},{1,97},{33,1},{65,33},{97,65},{2,98}... | collective-permute-start | bytes 884744 | tf_op jit(solution)/shard_map/ppermute | solution.py:28
  246.6 18.1 %collective-permute-start.36 = (bf16[384,768]{1,0:T(8,128)(2,1)}, bf16[384,768]{1,0:T(8,128)(2,1)}, u32[]{:S(2)}, u32[]{:S(2)}) collective-permute-start(bf16[384,768]{1,0:T(8,128)(2,1)} %pad_maximum_fusion.3), channel_id=1, source_target_pairs={{0,96},{32,0},{64,32},{96,64},{1,97},{33,1},{65,33},{97,65},{2,98}... | collective-permute-start | bytes 1769480 | tf_op jit(solution)/shard_map/ppermute | solution.py:28
  248.3 17.7 %collective-permute-start.34 = (bf16[384,768]{1,0:T(8,128)(2,1)}, bf16[384,768]{1,0:T(8,128)(2,1)}, u32[]{:S(2)}, u32[]{:S(2)}) collective-permute-start(bf16[384,768]{1,0:T(8,128)(2,1)} %pad_maximum_fusion.2), channel_id=1, source_target_pairs={{0,32},{32,64},{64,96},{96,0},{1,33},{33,65},{65,97},{97,1},{2,34}... | collective-permute-start | bytes 1769480 | tf_op jit(solution)/shard_map/ppermute | solution.py:28
  253.0 23.8 %collective-permute-start.29 = (bf16[384,768]{1,0:T(8,128)(2,1)}, bf16[384,768]{1,0:T(8,128)(2,1)}, u32[]{:S(2)}, u32[]{:S(2)}) collective-permute-start(bf16[384,768]{1,0:T(8,128)(2,1)} %pad_maximum_fusion.1), channel_id=1, source_target_pairs={{0,96},{32,0},{64,32},{96,64},{1,97},{33,1},{65,33},{97,65},{2,98}... | collective-permute-start | bytes 1769480 | tf_op jit(solution)/shard_map/ppermute | solution.py:28
  254.2 22.6 %collective-permute-start.27 = (bf16[384,768]{1,0:T(8,128)(2,1)}, bf16[384,768]{1,0:T(8,128)(2,1)}, u32[]{:S(2)}, u32[]{:S(2)}) collective-permute-start(bf16[384,768]{1,0:T(8,128)(2,1)} %pad_maximum_fusion), channel_id=1, source_target_pairs={{0,32},{32,64},{64,96},{96,0},{1,33},{33,65},{65,97},{97,1},{2,34}... | collective-permute-start | bytes 1769480 | tf_op jit(solution)/shard_map/ppermute | solution.py:28
  267.7 15.8 %collective-permute-start.39 = (bf16[96,768]{1,0:T(8,128)(2,1)S(1)}, bf16[96,768]{1,0:T(8,128)(2,1)S(1)}, u32[]{:S(2)}, u32[]{:S(2)}) collective-permute-start(bf16[96,768]{1,0:T(8,128)(2,1)S(1)} %get-tuple-element.47), channel_id=1, source_target_pairs={{0,16},{8,24},{16,0},{24,8},{1,17},{9,25},{17,1},{25,9},{2,18},{10... | collective-permute-start | bytes 442376 | tf_op jit(solution)/shard_map/ppermute | solution.py:28
  272.5 13.5 %collective-permute-start.38 = (bf16[96,768]{1,0:T(8,128)(2,1)S(1)}, bf16[96,768]{1,0:T(8,128)(2,1)S(1)}, u32[]{:S(2)}, u32[]{:S(2)}) collective-permute-start(bf16[96,768]{1,0:T(8,128)(2,1)S(1)} %get-tuple-element.48), channel_id=1, source_target_pairs={{0,24},{8,0},{16,8},{24,16},{1,25},{9,1},{17,9},{25,17},{2,26},{10... | collective-permute-start | bytes 442376 | tf_op jit(solution)/shard_map/ppermute | solution.py:28
  273.0 13.0 %collective-permute-start.37 = (bf16[96,768]{1,0:T(8,128)(2,1)S(1)}, bf16[96,768]{1,0:T(8,128)(2,1)S(1)}, u32[]{:S(2)}, u32[]{:S(2)}) collective-permute-start(bf16[96,768]{1,0:T(8,128)(2,1)S(1)} %get-tuple-element.46), channel_id=1, source_target_pairs={{0,8},{8,16},{16,24},{24,0},{1,9},{9,17},{17,25},{25,1},{2,10},{10... | collective-permute-start | bytes 442376 | tf_op jit(solution)/shard_map/ppermute | solution.py:28
  278.2 15.8 %collective-permute-start.32 = (bf16[96,768]{1,0:T(8,128)(2,1)S(1)}, bf16[96,768]{1,0:T(8,128)(2,1)S(1)}, u32[]{:S(2)}, u32[]{:S(2)}) collective-permute-start(bf16[96,768]{1,0:T(8,128)(2,1)S(1)} %get-tuple-element.50), channel_id=1, source_target_pairs={{0,16},{8,24},{16,0},{24,8},{1,17},{9,25},{17,1},{25,9},{2,18},{10... | collective-permute-start | bytes 442376 | tf_op jit(solution)/shard_map/ppermute | solution.py:28
  283.0 11.0 %collective-permute-start.31 = (bf16[96,768]{1,0:T(8,128)(2,1)S(1)}, bf16[96,768]{1,0:T(8,128)(2,1)S(1)}, u32[]{:S(2)}, u32[]{:S(2)}) collective-permute-start(bf16[96,768]{1,0:T(8,128)(2,1)S(1)} %get-tuple-element.51), channel_id=1, source_target_pairs={{0,24},{8,0},{16,8},{24,16},{1,25},{9,1},{17,9},{25,17},{2,26},{10... | collective-permute-start | bytes 442376 | tf_op jit(solution)/shard_map/ppermute | solution.py:28
  283.5 13.9 %collective-permute-start.30 = (bf16[96,768]{1,0:T(8,128)(2,1)S(1)}, bf16[96,768]{1,0:T(8,128)(2,1)S(1)}, u32[]{:S(2)}, u32[]{:S(2)}) collective-permute-start(bf16[96,768]{1,0:T(8,128)(2,1)S(1)} %get-tuple-element.49), channel_id=1, source_target_pairs={{0,8},{8,16},{16,24},{24,0},{1,9},{9,17},{17,25},{25,1},{2,10},{10... | collective-permute-start | bytes 442376 | tf_op jit(solution)/shard_map/ppermute | solution.py:28
  (20 other events, 116.7 us)
where the time goes:
time: 299 us; the launch traced here: 298 us
  waiting for transfers between devices  126 us (42%)
  starting transfers between devices  73.2 us (24%)
  blocking collectives  47.1 us (16%)
  Pallas kernels  34.6 us (12%)
  other arithmetic  9.5 us (3%)
  local copies, waits for them, and re-layouts  5.73 us (2%)
    ppermute x40, waiting for transfers between devices, hop(): return lax.ppermute(value, axis, [(i, (i + step) % n) for i in range(n)])  88.9 us
    ppermute x40, starting transfers between devices, hop(): return lax.ppermute(value, axis, [(i, (i + step) % n) for i in range(n)])  59.5 us
    all_to_all x2, blocking collectives, exchange(): return lax.all_to_all(parts, MODEL, 0, 0, tiled=True)  47.1 us
    all_to_all x2, waiting for transfers between devices, exchange(): return lax.all_to_all(parts, MODEL, 0, 0, tiled=True)  36.8 us
    pallas_call x1, Pallas kernels, step(): local_call(score_kernel, [SMEM, VMEM] + [HBM] * 4, array(8, SEQ, BLOCK),...  13.9 us
    all_to_all x2, starting transfers between devices, exchange(): return lax.all_to_all(parts, MODEL, 0, 0, tiled=True)  13.7 us
  transfers between devices with their start and end apart: 42, of which 27 were waited for; matrix products, arithmetic and copies ran while one was open for 3% of the time, Pallas kernels for 5%

commit v1 on v0

--- a/solution.py
+++ b/solution.py
@@ -53,24 +53,22 @@
     return wide(parts[0]) + sum(wide(hop(parts[k], axis, k)) for k in (1, 3, 2))
 
 
-def ring_scatter(parts, axis):
-    own, right, far, left = parts
-    half = own.shape[0] // 2
-    for_right = hop(far[:half], axis, 1)
-    for_left = hop(far[half:], axis, -1)
-    right = jnp.concatenate([narrow(wide(right[:half]) + wide(for_right)), right[half:]])
-    left = jnp.concatenate([left[:half], narrow(wide(left[half:]) + wide(for_left))])
+def ring_scatter(grads, far_top, far_bottom, shift, axis):
+    for_right = hop(far_top, axis, 1)
+    for_left = hop(far_bottom, axis, -1)
+    part = array(BLOCK, FF_LOCAL)
+    right, left = local_call(merge_kernel, [VMEM] * 3, (part, part), 500_000, 3_000_000)(
+        grads, for_right, for_left
+    )
     from_left = hop(right, axis, 1)
     from_right = hop(left, axis, -1)
-    return wide(own) + wide(from_left) + wide(from_right)
+    return local_call(
+        sum_kernel, [SMEM] + [VMEM] * 3, (array(SHARD, FF_LOCAL),) * 4, 500_000, 3_000_000
+    )(shift[None], grads, from_left, from_right)
 
 
 def exchange(parts):
     return lax.all_to_all(parts, MODEL, 0, 0, tiled=True)
-
-
-def pick(stack, index):
-    return lax.dynamic_index_in_dim(stack, index, 0, keepdims=False)
 
 
 def finish(mixing):
@@ -91,19 +89,19 @@
 
 VMEM = pl.BlockSpec(memory_space=pltpu.VMEM)
 SMEM = pl.BlockSpec(memory_space=pltpu.SMEM)
-HBM = pl.BlockSpec(memory_space=pl.ANY)
+HBM = pl.BlockSpec(memory_space=pltpu.HBM)
 
 
 def array(*shape, kind=jnp.bfloat16):
     return jax.ShapeDtypeStruct(shape, kind)
 
 
-def local_call(kernel, ins, outs, flops, moved, scratch=(), limit=40):
+def local_call(kernel, ins, outs, flops, moved, scratch=(), limit=40, to=None):
     return pl.pallas_call(
         kernel,
         out_shape=outs,
         in_specs=ins,
-        out_specs=jax.tree.map(lambda _: VMEM, outs),
+        out_specs=to or jax.tree.map(lambda _: VMEM, outs),
         scratch_shapes=scratch,
         compiler_params=pltpu.CompilerParams(vmem_limit_bytes=limit << 20),
         cost_estimate=pl.CostEstimate(flops=flops, bytes_accessed=moved, transcendentals=0),
@@ -164,57 +162,96 @@
     lax.fori_loop(0, SEQ // 16, tile, 0)
 
 
-def down_kernel(
-    at_ref, hidden_ref, crossed_ref, n0, n1, n2, n3, r0, r1, far_top, far_bottom, r3,
+def merge_kernel(grads_ref, for_right, for_left, right_ref, left_ref):
+    half = BLOCK // 2
+
+    def tile(i, _):
+        rows = row_tile(i)
+        low = pl.ds(pl.multiple_of(half + i * 16, 16), 16)
+        right_ref[rows, :] = narrow(wide(grads_ref[1, rows, :]) + wide(for_right[rows, :]))
+        right_ref[low, :] = grads_ref[1, low, :]
+        left_ref[rows, :] = grads_ref[3, rows, :]
+        left_ref[low, :] = narrow(wide(grads_ref[3, low, :]) + wide(for_left[rows, :]))
+        return 0
+
+    lax.fori_loop(0, half // 16, tile, 0)
+
+
+def sum_kernel(shift_ref, grads_ref, from_left, from_right, *shards):
+    for dz, shard in enumerate(shards):
+        base = ((shift_ref[0] + dz) & 3) * SHARD
+
+        def tile(i, _):
+            rows = pl.ds(pl.multiple_of(base + i * 16, 16), 16)
+            shard[row_tile(i), :] = narrow(
+                wide(grads_ref[0, rows, :]) + wide(from_left[rows, :]) + wide(from_right[rows, :])
+            )
+            return 0
+
+        lax.fori_loop(0, SHARD // 16, tile, 0)
+
+
+EARLY = (0, 1, 3)
+
+
+def down_early_kernel(
+    at_ref, hidden_ref, crossed_ref, n0, n1, n3, r0, r1, r3, down_ref, here_ref, away_ref
+):
+    for i, (near, rest) in enumerate(((n0, r0), (n1, r1), (n3, r3))):
+        for dz in range(4):
+            rows = pl.ds(pl.multiple_of(((at_ref[2] + dz) & 3) * SHARD, 32), SHARD)
+            down_ref[i, rows, :] = (
+                near[SHARD:, :] if dz == 0 else rest[(dz - 1) * SHARD : dz * SHARD, :]
+            )
+
+    def block(i, _):
+        here_ref[i] = narrow(dot(hidden_ref[...], down_ref[i], 1, 1))
+        away_ref[i] = narrow(dot(crossed_ref[...], down_ref[i], 1, 1))
+        return 0
+
+    lax.fori_loop(0, 3, block, 0)
+
+
+def down_far_kernel(
+    at_ref, hidden_ref, crossed_ref, n2, far_top, far_bottom, here_ref, arrived_ref,
     down_ref, parts_ref, away_ref,
 ):
     group, x, zh = at_ref[0], at_ref[1], at_ref[2]
-    for dx, (near, rest) in enumerate(((n0, r0), (n1, r1), (n2, None), (n3, r3))):
-        spot = (x + dx) & 3
-        for dz in range(4):
-            base = pl.multiple_of(((zh + dz) & 3) * SHARD, 32)
-            rows = pl.ds(base, SHARD)
-            if dz == 0:
-                down_ref[spot, rows, :] = near[SHARD:, :]
-            elif rest is not None:
-                down_ref[spot, rows, :] = rest[(dz - 1) * SHARD : dz * SHARD, :]
-            elif dz == 1:
-                down_ref[spot, rows, :] = far_top[:SHARD, :]
-            elif dz == 2:
-                half = SHARD // 2
-                down_ref[spot, pl.ds(base, half), :] = far_top[SHARD:, :]
-                low = pl.multiple_of(base + half, 16)
-                down_ref[spot, pl.ds(low, half), :] = far_bottom[:half, :]
-            else:
-                down_ref[spot, rows, :] = far_bottom[SHARD // 2 :, :]
-
-    def block(k, _):
-        weights = down_ref[k]
-        parts_ref[group * 4 + k] = narrow(dot(hidden_ref[...], weights, 1, 1))
-        away_ref[k] = narrow(dot(crossed_ref[...], weights, 1, 1))
-        return 0
-
-    lax.fori_loop(0, 4, block, 0)
+    half = SHARD // 2
+    for dz, pieces in enumerate(
+        (
+            (n2[SHARD : SHARD + half, :], n2[SHARD + half :, :]),
+            (far_top[:half, :], far_top[half:SHARD, :]),
+            (far_top[SHARD:, :], far_bottom[:half, :]),
+            (far_bottom[half:SHARD, :], far_bottom[SHARD:, :]),
+        )
+    ):
+        base = ((zh + dz) & 3) * SHARD
+        for k, piece in enumerate(pieces):
+            down_ref[pl.ds(pl.multiple_of(base + k * half, 16), half), :] = piece
+    away_ref[...] = narrow(dot(crossed_ref[...], down_ref[...], 1, 1))
+    parts_ref[group * 4 + ((x + 2) & 3)] = narrow(dot(hidden_ref[...], down_ref[...], 1, 1))
+    for i, dx in enumerate(EARLY):
+        parts_ref[group * 4 + ((x + dx) & 3)] = here_ref[i]
+        parts_ref[(1 - group) * 4 + ((x + dx) & 3)] = arrived_ref[i]
+
+
+def fetch_kernel(own_hbm, other_hbm, out_own_hbm, out_other_hbm, qkv_w, out_w, sems):
+    loads = [
+        pltpu.make_async_copy(own_hbm, qkv_w.at[:3], sems.at[0]),
+        pltpu.make_async_copy(other_hbm, qkv_w.at[3:], sems.at[1]),
+        pltpu.make_async_copy(out_own_hbm, out_w.at[0], sems.at[2]),
+        pltpu.make_async_copy(out_other_hbm, out_w.at[1], sems.at[3]),
+    ]
+    for load in loads:
+        load.start()
+    for load in loads:
+        load.wait()
 
 
 def score_kernel(
-    sign_ref, noisy_ref, own_hbm, other_hbm, out_own_hbm, out_other_hbm, gap_ref,
-    qkv_w, out_w, normed_ref, qkv_ref, mix_ref, qkv_sem, out_sem,
+    sign_ref, noisy_ref, qkv_w, out_w, gap_ref, normed_ref, qkv_ref, mix_ref
 ):
-    loads = []
-    for net, (source, out_source) in enumerate(
-        ((own_hbm, out_own_hbm), (other_hbm, out_other_hbm))
-    ):
-        for k in range(3):
-            loads.append(
-                pltpu.make_async_copy(
-                    source.at[k], qkv_w.at[net * 3 + k], qkv_sem.at[net * 3 + k]
-                )
-            )
-        loads.append(pltpu.make_async_copy(out_source, out_w.at[net], out_sem.at[net]))
-    for k in (0, 1, 2, 4, 5, 6, 3, 7):
-        loads[k].start()
-
     def norm(i, _):
         rows = row_tile(i)
         blocks = [wide(noisy_ref[j, rows, :]) for j in range(8)]
@@ -227,13 +264,6 @@
     lax.fori_loop(0, SEQ // 16, norm, 0)
 
     def network(net, _):
-        for own in range(2):
-
-            @pl.when(net == own)
-            def _():
-                for k in range(3):
-                    loads[own * 4 + k].wait()
-
         def project(k, _):
             qkv_ref[k] = narrow(dot(normed_ref[...], qkv_w[net * 3 + k]))
             return 0
@@ -254,8 +284,6 @@
         return 0
 
     lax.fori_loop(0, 2, network, 0)
-    loads[3].wait()
-    loads[7].wait()
 
     def emit(j, _):
         columns = pl.ds(pl.multiple_of(j * 2 * BLOCK, 2 * BLOCK), 2 * BLOCK)
@@ -269,13 +297,15 @@
     lax.fori_loop(0, 4, emit, 0)
 
 
-def slope_kernel(at_ref, gap_ref, crossed_ref, down_ref, here, away):
-    group = at_ref[0]
+def slope_kernel(at_ref, gap_ref, crossed_ref, early_ref, far_ref, here, away):
+    group, x = at_ref[0], at_ref[1]
+    spots = [(x + dx) & 3 for dx in (*EARLY, 2)]
 
     def columns(c, _):
         lanes = lane_chunk(c)
-        here[:, lanes] = sum(dot(gap_ref[group * 4 + k], down_ref[k, :, lanes]) for k in range(4))
-        away[:, lanes] = sum(dot(crossed_ref[k], down_ref[k, :, lanes]) for k in range(4))
+        weights = [early_ref[i, :, lanes] for i in range(3)] + [far_ref[:, lanes]]
+        here[:, lanes] = sum(dot(gap_ref[group * 4 + k], w) for k, w in zip(spots, weights))
+        away[:, lanes] = sum(dot(crossed_ref[k], w) for k, w in zip(spots, weights))
         return 0
 
     lax.fori_loop(0, FF_LOCAL // 256, columns, 0)
@@ -296,7 +326,7 @@
     lax.fori_loop(0, SEQ // 16, tile, 0)
 
 
-def down_grad_kernel(at_ref, gap_ref, gap_crossed_ref, hidden_ref, hidden_crossed_ref, grad_ref):
+def down_grad_kernel(at_ref, gap_ref, gap_crossed_ref, hidden_ref, hidden_crossed_ref, grad_ref, top, low):
     group, x = at_ref[0], at_ref[1]
 
     def block(k, _):
@@ -311,9 +341,11 @@
         return 0
 
     lax.fori_loop(0, 4, block, 0)
-
-
-def up_grad_kernel(own_ref, own_crossed_ref, change_ref, change_crossed_ref, grad_ref):
+    top[...] = grad_ref[2, : BLOCK // 2]
+    low[...] = grad_ref[2, BLOCK // 2 :]
+
+
+def up_grad_kernel(own_ref, own_crossed_ref, change_ref, change_crossed_ref, grad_ref, top, low):
     def block(k, _):
         lanes = pl.ds(pl.multiple_of(k * BLOCK, BLOCK), BLOCK)
         grad_ref[k] = narrow(
@@ -326,6 +358,8 @@
         return 0
 
     lax.fori_loop(0, 4, block, 0)
+    top[...] = grad_ref[2, : BLOCK // 2]
+    low[...] = grad_ref[2, BLOCK // 2 :]
 
 
 def latent_kernel(ids_ref, shift_ref, feature_ref, parts_ref, latent_ref, noisy_ref):
@@ -400,63 +434,89 @@
         hidden_kernel, [VMEM] * 2, (before_kind, hidden_kind), 3_000_000, 2_800_000
     )(here, swap(away))
     hidden_crossed = swap(hidden)
-    down_all, parts, parts_away = local_call(
-        down_kernel,
-        [SMEM] + [VMEM] * 11,
-        (grad_kind, array(8, SEQ, BLOCK), array(4, SEQ, BLOCK)),
-        matmul,
-        8_000_000,
-    )(at, hidden, hidden_crossed, *near, *down_rest)
-    parts = lax.dynamic_update_slice_in_dim(parts, swap(parts_away), (1 - group) * 4, 0)
+    three = array(3, SEQ, BLOCK)
+    down_early, parts_here, parts_away = local_call(
+        down_early_kernel,
+        [SMEM] + [VMEM] * 8,
+        (array(3, BLOCK, FF_LOCAL), three, three),
+        900_000_000,
+        6_000_000,
+    )(
+        at,
+        hidden,
+        hidden_crossed,
+        *(near[k] for k in EARLY),
+        *(down_rest[k] for k in (0, 1, 4)),
+    )
+    eight_kind = array(8, SEQ, BLOCK)
+    down_far, parts, part_away = local_call(
+        down_far_kernel,
+        [SMEM] + [VMEM] * 7,
+        (array(BLOCK, FF_LOCAL), eight_kind, array(SEQ, BLOCK)),
+        300_000_000,
+        4_000_000,
+    )(at, hidden, hidden_crossed, near[2], down_rest[2], down_rest[3], parts_here, swap(parts_away))
+    parts = lax.dynamic_update_index_in_dim(
+        parts, swap(part_away), (1 - group) * 4 + ((x + 2) & 3), 0
+    )
 
     local = lax.iota(jnp.int32, BLOCK) + (y * 2 + zl) * BLOCK
     shift = (timestep_ids[0].astype(jnp.float32) + 0.5) / STEPS
-    eight_kind = array(8, SEQ, BLOCK)
     latent, noisy = local_call(
-        latent_kernel, [SMEM, SMEM, VMEM, VMEM], (array(SEQ, BLOCK), eight_kind), 9_000_000, 4_000_000
+        latent_kernel,
+        [SMEM, SMEM, VMEM, VMEM],
+        (array(SEQ, BLOCK), eight_kind),
+        9_000_000,
+        4_000_000,
+        limit=16,
     )(noise_seeds, shift[None], (local * 668265263)[None], exchange(parts))
     noisy_all = exchange(noisy)
+    qkv_both, out_both = local_call(
+        fetch_kernel,
+        [HBM] * 4,
+        (array(6, D, BLOCK), array(2, BLOCK, D)),
+        1_000_000,
+        38_000_000,
+        scratch=[pltpu.SemaphoreType.DMA((4,))],
+        limit=44,
+    )(qkv_own, qkv_other, out_own, out_other)
     sign = wide(2 * group - 1)[None]
     gap_parts = local_call(
         score_kernel,
-        [SMEM, VMEM] + [HBM] * 4,
+        [SMEM] + [VMEM] * 3,
         array(8, SEQ, BLOCK),
         5_000_000_000,
         20_000_000,
         scratch=[
-            pltpu.VMEM((6, D, BLOCK), jnp.bfloat16),
-            pltpu.VMEM((2, BLOCK, D), jnp.bfloat16),
             pltpu.VMEM((SEQ, D), jnp.bfloat16),
             pltpu.VMEM((3, SEQ, BLOCK), jnp.bfloat16),
             pltpu.VMEM((2, SEQ, BLOCK), jnp.bfloat16),
-            pltpu.SemaphoreType.DMA((6,)),
-            pltpu.SemaphoreType.DMA((2,)),
         ],
-    )(sign, noisy_all, qkv_own, qkv_other, out_own, out_other)
+        limit=42,
+    )(sign, noisy_all, qkv_both, out_both)
     gap, gap_copies = local_call(
         gap_kernel, [VMEM], (array(SEQ, BLOCK), eight_kind), 1_000_000, 4_000_000
     )(exchange(gap_parts))
     gap_all = exchange(gap_copies)
     gap_crossed = swap(lax.dynamic_slice_in_dim(gap_all, (1 - group) * 4, 4, 0))
-    down_grads = local_call(down_grad_kernel, [SMEM] + [VMEM] * 4, grad_kind, matmul, 5_000_000)(
+    grad_kinds = (grad_kind, array(BLOCK // 2, FF_LOCAL), array(BLOCK // 2, FF_LOCAL))
+    down_grads = local_call(down_grad_kernel, [SMEM] + [VMEM] * 4, grad_kinds, matmul, 5_000_000)(
         at, gap_all, gap_crossed, hidden, hidden_crossed
     )
-    down_sum = narrow(ring_scatter([down_grads[k] for k in range(4)], "x"))
-    down_sum = down_sum.reshape(4, SHARD, FF_LOCAL)
-    grad_down = narrow(direct_scatter([pick(down_sum, (zh + dz) & 3) for dz in range(4)], "zh")).T
+    down_shards = ring_scatter(*down_grads, zh, "x")
+    grad_down = narrow(direct_scatter(down_shards, "zh")).T
 
     here, away = local_call(
-        slope_kernel, [SMEM] + [VMEM] * 3, (before_kind, before_kind), matmul, 6_000_000
-    )(at, gap_all, gap_crossed, down_all)
+        slope_kernel, [SMEM] + [VMEM] * 4, (before_kind, before_kind), matmul, 6_000_000
+    )(at, gap_all, gap_crossed, down_early, down_far)
     change = local_call(change_kernel, [VMEM] * 3, hidden_kind, 5_000_000, 2_800_000)(
         here, swap(away), before
     )
-    up_grads = local_call(up_grad_kernel, [VMEM] * 4, grad_kind, matmul, 5_000_000)(
+    up_grads = local_call(up_grad_kernel, [VMEM] * 4, grad_kinds, matmul, 5_000_000)(
         normed, normed_crossed, change, swap(change)
     )
-    up_sum = narrow(ring_scatter([up_grads[k] for k in range(4)], "x"))
-    up_sum = up_sum.reshape(4, SHARD, FF_LOCAL)
-    grad_up = narrow(direct_scatter([up_sum[dz] for dz in range(4)], "zh"))
+    up_shards = ring_scatter(*up_grads, jnp.int32(0), "x")
+    grad_up = narrow(direct_scatter(up_shards, "zh"))
     return (latent[None], gap[None], grad_up, grad_down)
 
 

time: 299 us -> 312 us (1.043); the launches traced: 298 us -> 308 us
  blocking collectives: 47.1 us -> 25.8 us
  Pallas kernels: 34.6 us -> 51.1 us
  waiting for transfers between devices: 126 us -> 135 us
  other arithmetic: 9.5 us -> 2.66 us
  starting transfers between devices: 73.2 us -> 79.5 us
  local copies, waits for them, and re-layouts: 5.73 us -> 11.1 us
    all_to_all x2 -> x1, blocking collectives: 47.1 us -> 25.8 us  [exchange(): return lax.all_to_all(parts, MODEL, 0, 0, tiled=True)]
    pallas_call x5 -> x11, Pallas kernels: 25.2 us -> 41.7 us  [the longest x1 17.6 us: step(): local_call(score_kernel, [SMEM] + [VMEM] * 3, array(8, SEQ, BLOCK), 50000...]
    ppermute x40 -> x41, starting transfers between devices: 59.5 us -> 67.6 us  [hop(): return lax.ppermute(value, axis, [(i, (i + step) % n) for i in range(n)])]
    unnamed x24 -> x40, local copies, waits for them, and re-layouts: 4.38 us -> 10.3 us
    all_to_all x2 -> x3, waiting for transfers between devices: 36.8 us -> 42.6 us  [exchange(): return lax.all_to_all(parts, MODEL, 0, 0, tiled=True)]
    ppermute x40 -> x41, waiting for transfers between devices: 88.9 us -> 92.8 us  [hop(): return lax.ppermute(value, axis, [(i, (i + step) % n) for i in range(n)])]
    concatenate x4 -> x0, other arithmetic: 3.48 us -> none  [the longest x2 1.74 us: ring_scatter(): jnp.concatenate([narrow(wide(right[:half]) + wide(for_right)), right[half...]
    convert_element_type x5 -> x1, other arithmetic: 4.12 us -> 0.74 us  [narrow(): return value.astype(jnp.bfloat16)]
  transfers between devices with their start and end apart: 42 -> 44, of which waited for: 27 -> 30; matrix products, arithmetic and copies ran while one was open for 3% -> 1% of each run, Pallas kernels for 5% -> 9%
where the time goes in v1:
time: 312 us; the launch traced here: 308 us
  waiting for transfers between devices  135 us (43%)
  starting transfers between devices  79.5 us (25%)
  Pallas kernels  51.1 us (16%)
  blocking collectives  25.8 us (8%)
  local copies, waits for them, and re-layouts  11.1 us (4%)
    ppermute x41, waiting for transfers between devices, hop(): return lax.ppermute(value, axis, [(i, (i + step) % n) for i in range(n)])  92.8 us
    ppermute x41, starting transfers between devices, hop(): return lax.ppermute(value, axis, [(i, (i + step) % n) for i in range(n)])  67.6 us
    all_to_all x3, waiting for transfers between devices, exchange(): return lax.all_to_all(parts, MODEL, 0, 0, tiled=True)  42.6 us
    all_to_all x1, blocking collectives, exchange(): return lax.all_to_all(parts, MODEL, 0, 0, tiled=True)  25.8 us
    pallas_call x1, Pallas kernels, step(): local_call(score_kernel, [SMEM] + [VMEM] * 3, array(8, SEQ, BLOCK), 50000...  17.6 us
    all_to_all x3, starting transfers between devices, exchange(): return lax.all_to_all(parts, MODEL, 0, 0, tiled=True)  11.9 us
    pallas_call x1, Pallas kernels, step(): local_call(fetch_kernel, [HBM] * 4, (array(6, D, BLOCK), array(2, BLOCK,...  10.8 us
    unnamed x40, local copies, waits for them, and re-layouts  10.3 us
  transfers between devices with their start and end apart: 44, of which 30 were waited for; matrix products, arithmetic and copies ran while one was open for 1% of the time, Pallas kernels for 9%

profile of v1, /device:TPU:2, one launch (start us, length us, event | category | flops | bytes accessed | tf_op | source)
XLA Modules:
  0.0 307.8 jit_solution(13550071123278812240)
XLA Ops:
  0.6 6.4 %collective-permute-start.4 = (bf16[96,768]{1,0:T(8,128)(2,1)}, bf16[96,768]{1,0:T(8,128)(2,1)S(1)}, u32[]{:S(2)}, u32[]{:S(2)}) collective-permute-start(bf16[96,768]{1,0:T(8,128)(2,1)} %param.8), channel_id=1, source_target_pairs={{0,24},{8,0},{16,8},{24,16},{1,25},{9,1},{17,9},{25,17},{2,26},{10... | collective-permute-start | bytes 442376 | tf_op jit(solution)/shard_map/ppermute | solution.py:28
  7.0 3.8 %collective-permute-start.5 = (bf16[96,768]{1,0:T(8,128)(2,1)}, bf16[96,768]{1,0:T(8,128)(2,1)S(1)}, u32[]{:S(2)}, u32[]{:S(2)}) collective-permute-start(bf16[96,768]{1,0:T(8,128)(2,1)} %param.8), channel_id=1, source_target_pairs={{0,16},{8,24},{16,0},{24,8},{1,17},{9,25},{17,1},{25,9},{2,18},{10... | collective-permute-start | bytes 442376 | tf_op jit(solution)/shard_map/ppermute | solution.py:28
  11.6 3.5 %shard_map.93 = (bf16[256,1536]{1,0:T(8,128)(2,1)S(1)}, bf16[256,1536]{1,0:T(8,128)(2,1)S(1)}) custom-call(s32[1]{0:T(128)S(6)} %copy.15.seed_ref.ids_ref, s32[1,3072]{1,0:T(1,128)S(1)} %fusion.2.feature_ref), custom_call_target="tpu_custom_call" | custom-call | flops 30000000 | bytes 1600000 | tf_op jit(solution)/shard_map/pallas_call | solution.py:426
  15.2 3.7 %collective-permute-done.4 = bf16[96,768]{1,0:T(8,128)(2,1)S(1)} collective-permute-done((bf16[96,768]{1,0:T(8,128)(2,1)}, bf16[96,768]{1,0:T(8,128)(2,1)S(1)}, u32[]{:S(2)}, u32[]{:S(2)}) %collective-permute-start.4) | collective-permute-done | bytes 147488 | tf_op jit(solution)/shard_map/ppermute | solution.py:28
  28.5 6.1 %collective-permute-done.8.r3 = bf16[288,768]{1,0:T(8,128)(2,1)S(1)} collective-permute-done((bf16[288,768]{1,0:T(8,128)(2,1)S(1)}, bf16[288,768]{1,0:T(8,128)(2,1)S(1)}, u32[]{:S(2)}, u32[]{:S(2)}) %collective-permute-start.8) | collective-permute-done | bytes 442400 | tf_op jit(solution)/shard_map/ppermute | solution.py:28
  36.4 3.0 collective-permute-done.7.r1
  39.4 4.4 %collective-permute-done.3.n3 = bf16[192,768]{1,0:T(8,128)(2,1)S(1)} collective-permute-done((bf16[192,768]{1,0:T(8,128)(2,1)S(1)}, bf16[192,768]{1,0:T(8,128)(2,1)S(1)}, u32[]{:S(2)}, u32[]{:S(2)}) %collective-permute-start.3) | collective-permute-done | bytes 294944 | tf_op jit(solution)/shard_map/ppermute | solution.py:28
  52.6 6.4 %collective-permute-start.13 = (bf16[96,768]{1,0:T(8,128)(2,1)S(1)}, bf16[96,768]{1,0:T(8,128)(2,1)S(1)}, u32[]{:S(2)}, u32[]{:S(2)}) collective-permute-start(bf16[96,768]{1,0:T(8,128)(2,1)S(1)} %bitcast.16), channel_id=1, source_target_pairs={{0,24},{8,0},{16,8},{24,16},{1,25},{9,1},{17,9},{25,17},{2,26},{10... | collective-permute-start | bytes 442376 | tf_op jit(solution)/shard_map/ppermute | solution.py:28
  59.0 4.0 %collective-permute-start.14 = (bf16[96,768]{1,0:T(8,128)(2,1)S(1)}, bf16[96,768]{1,0:T(8,128)(2,1)S(1)}, u32[]{:S(2)}, u32[]{:S(2)}) collective-permute-start(bf16[96,768]{1,0:T(8,128)(2,1)S(1)} %bitcast.17), channel_id=1, source_target_pairs={{0,16},{8,24},{16,0},{24,8},{1,17},{9,25},{17,1},{25,9},{2,18},{10... | collective-permute-start | bytes 442376 | tf_op jit(solution)/shard_map/ppermute | solution.py:28
  63.0 4.7 %collective-permute-done.13 = bf16[96,768]{1,0:T(8,128)(2,1)S(1)} collective-permute-done((bf16[96,768]{1,0:T(8,128)(2,1)S(1)}, bf16[96,768]{1,0:T(8,128)(2,1)S(1)}, u32[]{:S(2)}, u32[]{:S(2)}) %collective-permute-start.13) | collective-permute-done | bytes 147488 | tf_op jit(solution)/shard_map/ppermute | solution.py:28
  67.7 6.0 %collective-permute-done.14 = bf16[96,768]{1,0:T(8,128)(2,1)S(1)} collective-permute-done((bf16[96,768]{1,0:T(8,128)(2,1)S(1)}, bf16[96,768]{1,0:T(8,128)(2,1)S(1)}, u32[]{:S(2)}, u32[]{:S(2)}) %collective-permute-start.14) | collective-permute-done | bytes 147488 | tf_op jit(solution)/shard_map/ppermute | solution.py:28
  80.7 7.9 %collective-permute-done.18.r1 = bf16[288,768]{1,0:T(8,128)(2,1)S(1)} collective-permute-done((bf16[288,768]{1,0:T(8,128)(2,1)S(1)}, bf16[288,768]{1,0:T(8,128)(2,1)S(1)}, u32[]{:S(2)}, u32[]{:S(2)}) %collective-permute-start.18) | collective-permute-done | bytes 442400 | tf_op jit(solution)/shard_map/ppermute | solution.py:28
  95.7 5.6 %collective-permute-done.19.far_bottom = bf16[144,768]{1,0:T(8,128)(2,1)S(1)} collective-permute-done((bf16[144,768]{1,0:T(8,128)(2,1)S(1)}, bf16[144,768]{1,0:T(8,128)(2,1)S(1)}, u32[]{:S(2)}, u32[]{:S(2)}) %collective-permute-start.19) | collective-permute-done | bytes 221216 | tf_op jit(solution)/shard_map/ppermute | solution.py:28
  108.2 4.7 %all-to-all-start = ((bf16[8,256,384]{2,1,0:T(8,128)(2,1)}), bf16[8,256,384]{2,1,0:T(8,128)(2,1)S(1)}, u32[]{:S(2)}, u32[]{:S(2)}) async-start(bf16[8,256,384]{2,1,0:T(8,128)(2,1)} %bitcast_dynamic-update-slice_fusion), calls=%async_computation | async-start | bytes 3145728 | tf_op jit(solution)/shard_map/all_to_all | solution.py:71
  113.6 21.0 %all-to-all-done.parts_ref = bf16[8,256,384]{2,1,0:T(8,128)(2,1)S(1)} async-done(((bf16[8,256,384]{2,1,0:T(8,128)(2,1)}), bf16[8,256,384]{2,1,0:T(8,128)(2,1)S(1)}, u32[]{:S(2)}, u32[]{:S(2)}) %all-to-all-start) | async-done | bytes 1572896 | tf_op jit(solution)/shard_map/all_to_all | solution.py:71
  137.5 3.6 %all-to-all-start.1 = ((bf16[8,256,384]{2,1,0:T(8,128)(2,1)}), bf16[8,256,384]{2,1,0:T(8,128)(2,1)S(1)}, u32[]{:S(2)}, u32[]{:S(2)}) async-start(bf16[8,256,384]{2,1,0:T(8,128)(2,1)} %copy-done.3), calls=%async_computation.1 | async-start | bytes 3145728 | tf_op jit(solution)/shard_map/all_to_all | solution.py:71
  141.2 4.9 %collective-permute-done.23.out_other_hbm = bf16[384,3072]{1,0:T(8,128)(2,1)} collective-permute-done((bf16[384,3072]{1,0:T(8,128)(2,1)}, bf16[384,3072]{1,0:T(8,128)(2,1)}, u32[]{:S(2)}, u32[]{:S(2)}) %collective-permute-start.23) | collective-permute-done | bytes 2359328 | tf_op jit(solution)/shard_map/ppermute | solution.py:28
  147.7 10.8 %shard_map.99 = (bf16[6,3072,384]{2,1,0:T(8,128)(2,1)}, bf16[2,384,3072]{2,1,0:T(8,128)(2,1)S(1)}) custom-call(bf16[3,3072,384]{2,1,0:T(8,128)(2,1)} %bitcast.7.own_hbm, bf16[3,3072,384]{2,1,0:T(8,128)(2,1)} %collective-permute-done.22.other_hbm, bf16[384,3072]{1,0:T(8,128)(2,1)S(1)} %bitcast.14, bf16[384,3072]{1,0:T(8,128)(2,1)} %collective-permute-done.23.out_other_hbm), custom_call_target="tpu_custom_call" | custom-call | flops 1000000 | bytes 38000000 | tf_op jit(solution)/shard_map/pallas_call | solution.py:474
  164.1 17.6 %shard_map.100 = bf16[8,256,384]{2,1,0:T(8,128)(2,1)S(1)} custom-call(f32[1]{0:T(128)} %bitcast.6.sign_ref, bf16[8,256,384]{2,1,0:T(8,128)(2,1)S(1)} %all-to-all-done.1.noisy_ref, bf16[6,3072,384]{2,1,0:T(8,128)(2,1)} %get-tuple-element.53.qkv_w, bf16[2,384,3072]{2,1,0:T(8,128)(2,1)S(1)} %copy-done.1), custom_call_target="tpu_custom_call" | custom-call | flops 5000000000 | bytes 20000000 | tf_op jit(solution)/shard_map/pallas_call | solution.py:484
  181.7 25.8 %all_to_all.20.parts_ref = bf16[8,256,384]{2,1,0:T(8,128)(2,1)S(1)} all-to-all(bf16[8,256,384]{2,1,0:T(8,128)(2,1)S(1)} %shard_map.100), channel_id=1, replica_groups=mesh['group'=2,'x'=4,'zh'=4,'y'=4,'zl'=2] {'y','zl'}, dimensions={0} | all-to-all | bytes 3145728 | tf_op jit(solution)/shard_map/all_to_all | solution.py:71
  209.7 3.6 %all-to-all-start.3 = ((bf16[8,256,384]{2,1,0:T(8,128)(2,1)}), bf16[8,256,384]{2,1,0:T(8,128)(2,1)S(1)}, u32[]{:S(2)}, u32[]{:S(2)}) async-start(bf16[8,256,384]{2,1,0:T(8,128)(2,1)} %copy-done.4), calls=%async_computation.3 | async-start | bytes 3145728 | tf_op jit(solution)/shard_map/all_to_all | solution.py:71
  213.3 20.4 %all-to-all-done.3.gap_ref = bf16[8,256,384]{2,1,0:T(8,128)(2,1)S(1)} async-done(((bf16[8,256,384]{2,1,0:T(8,128)(2,1)}), bf16[8,256,384]{2,1,0:T(8,128)(2,1)S(1)}, u32[]{:S(2)}, u32[]{:S(2)}) %all-to-all-start.3) | async-done | bytes 1572896 | tf_op jit(solution)/shard_map/all_to_all | solution.py:71
  236.1 2.7 shard_map.102
  245.1 2.7 collective-permute-start.35
  250.0 3.0 collective-permute-start.28
  255.6 2.7 collective-permute-start.36
  259.0 2.7 collective-permute-done.27.for_right
  261.9 2.7 collective-permute-start.29
  265.3 9.0 %collective-permute-done.36.from_left = bf16[384,768]{1,0:T(8,128)(2,1)S(1)} collective-permute-done((bf16[384,768]{1,0:T(8,128)(2,1)S(1)}, bf16[384,768]{1,0:T(8,128)(2,1)S(1)}, u32[]{:S(2)}, u32[]{:S(2)}) %collective-permute-start.36) | collective-permute-done | bytes 589856 | tf_op jit(solution)/shard_map/ppermute | solution.py:28
  280.3 4.9 %collective-permute-start.40 = (bf16[96,768]{1,0:T(8,128)(2,1)S(1)}, bf16[96,768]{1,0:T(8,128)(2,1)S(1)}, u32[]{:S(2)}, u32[]{:S(2)}) collective-permute-start(bf16[96,768]{1,0:T(8,128)(2,1)S(1)} %get-tuple-element.79), channel_id=1, source_target_pairs={{0,16},{8,24},{16,0},{24,8},{1,17},{9,25},{17,1},{25,9},{2,18},{10... | collective-permute-start | bytes 442376 | tf_op jit(solution)/shard_map/ppermute | solution.py:28
  291.3 4.9 %collective-permute-start.33 = (bf16[96,768]{1,0:T(8,128)(2,1)S(1)}, bf16[96,768]{1,0:T(8,128)(2,1)S(1)}, u32[]{:S(2)}, u32[]{:S(2)}) collective-permute-start(bf16[96,768]{1,0:T(8,128)(2,1)S(1)} %get-tuple-element.70), channel_id=1, source_target_pairs={{0,16},{8,24},{16,0},{24,8},{1,17},{9,25},{17,1},{25,9},{2,18},{10... | collective-permute-start | bytes 442376 | tf_op jit(solution)/shard_map/ppermute | solution.py:28
  297.0 10.1 %collective-permute-done.32 = bf16[96,768]{1,0:T(8,128)(2,1)S(1)} collective-permute-done((bf16[96,768]{1,0:T(8,128)(2,1)S(1)}, bf16[96,768]{1,0:T(8,128)(2,1)S(1)}, u32[]{:S(2)}, u32[]{:S(2)}) %collective-permute-start.32) | collective-permute-done | bytes 147488 | tf_op jit(solution)/shard_map/ppermute | solution.py:28
  (128 shorter events, 82.2 us)
Async XLA Ops:
  0.6 18.2 %collective-permute-start.4 = (bf16[96,768]{1,0:T(8,128)(2,1)}, bf16[96,768]{1,0:T(8,128)(2,1)S(1)}, u32[]{:S(2)}, u32[]{:S(2)}) collective-permute-start(bf16[96,768]{1,0:T(8,128)(2,1)} %param.8), channel_id=1, source_target_pairs={{0,24},{8,0},{16,8},{24,16},{1,25},{9,1},{17,9},{25,17},{2,26},{10... | collective-permute-start | bytes 442376 | tf_op jit(solution)/shard_map/ppermute | solution.py:28
  7.0 14.4 %collective-permute-start.6 = (bf16[96,768]{1,0:T(8,128)(2,1)}, bf16[96,768]{1,0:T(8,128)(2,1)S(1)}, u32[]{:S(2)}, u32[]{:S(2)}) collective-permute-start(bf16[96,768]{1,0:T(8,128)(2,1)} %param.8), channel_id=1, source_target_pairs={{0,8},{8,16},{16,24},{24,0},{1,9},{9,17},{17,25},{25,1},{2,10},{10... | collective-permute-start | bytes 442376 | tf_op jit(solution)/shard_map/ppermute | solution.py:28
  7.0 13.0 %collective-permute-start.5 = (bf16[96,768]{1,0:T(8,128)(2,1)}, bf16[96,768]{1,0:T(8,128)(2,1)S(1)}, u32[]{:S(2)}, u32[]{:S(2)}) collective-permute-start(bf16[96,768]{1,0:T(8,128)(2,1)} %param.8), channel_id=1, source_target_pairs={{0,16},{8,24},{16,0},{24,8},{1,17},{9,25},{17,1},{25,9},{2,18},{10... | collective-permute-start | bytes 442376 | tf_op jit(solution)/shard_map/ppermute | solution.py:28
  15.1 32.2 %collective-permute-start = (bf16[256,1536]{1,0:T(8,128)(2,1)S(1)}, bf16[256,1536]{1,0:T(8,128)(2,1)S(1)}, u32[]{:S(2)}, u32[]{:S(2)}) collective-permute-start(bf16[256,1536]{1,0:T(8,128)(2,1)S(1)} %get-tuple-element.43), channel_id=1, source_target_pairs={{0,128},{128,0},{1,129},{129,1},{2,130},{130,2},{3,131},{131,3},{4... | collective-permute-start | bytes 2359304 | tf_op jit(solution)/shard_map/ppermute | solution.py:28
  21.5 13.1 %collective-permute-start.8 = (bf16[288,768]{1,0:T(8,128)(2,1)S(1)}, bf16[288,768]{1,0:T(8,128)(2,1)S(1)}, u32[]{:S(2)}, u32[]{:S(2)}) collective-permute-start(bf16[288,768]{1,0:T(8,128)(2,1)S(1)} %constant_dynamic-update-slice_fusion.r0), channel_id=1, source_target_pairs={{0,32},{32,64},{64,96},{96,0},{1,33},{33,65},{65,97},{97,1},{2,34}... | collective-permute-start | bytes 1327112 | tf_op jit(solution)/shard_map/ppermute | solution.py:28
  23.0 16.3 %collective-permute-start.7 = (bf16[288,768]{1,0:T(8,128)(2,1)S(1)}, bf16[288,768]{1,0:T(8,128)(2,1)S(1)}, u32[]{:S(2)}, u32[]{:S(2)}) collective-permute-start(bf16[288,768]{1,0:T(8,128)(2,1)S(1)} %constant_dynamic-update-slice_fusion.r0), channel_id=1, source_target_pairs={{0,96},{32,0},{64,32},{96,64},{1,97},{33,1},{65,33},{97,65},{2,98}... | collective-permute-start | bytes 1327112 | tf_op jit(solution)/shard_map/ppermute | solution.py:28
  24.6 19.2 %collective-permute-start.3 = (bf16[192,768]{1,0:T(8,128)(2,1)S(1)}, bf16[192,768]{1,0:T(8,128)(2,1)S(1)}, u32[]{:S(2)}, u32[]{:S(2)}) collective-permute-start(bf16[192,768]{1,0:T(8,128)(2,1)S(1)} %pad_maximum_fusion.n0), channel_id=1, source_target_pairs={{0,32},{32,64},{64,96},{96,0},{1,33},{33,65},{65,97},{97,1},{2,34}... | collective-permute-start | bytes 884744 | tf_op jit(solution)/shard_map/ppermute | solution.py:28
  26.1 19.5 %collective-permute-start.2 = (bf16[192,768]{1,0:T(8,128)(2,1)S(1)}, bf16[192,768]{1,0:T(8,128)(2,1)S(1)}, u32[]{:S(2)}, u32[]{:S(2)}) collective-permute-start(bf16[192,768]{1,0:T(8,128)(2,1)S(1)} %pad_maximum_fusion.n0), channel_id=1, source_target_pairs={{0,64},{32,96},{64,0},{96,32},{1,65},{33,97},{65,1},{97,33},{2,66}... | collective-permute-start | bytes 884744 | tf_op jit(solution)/shard_map/ppermute | solution.py:28
  34.6 12.7 %collective-permute-start.1 = (bf16[192,768]{1,0:T(8,128)(2,1)S(1)}, bf16[192,768]{1,0:T(8,128)(2,1)S(1)}, u32[]{:S(2)}, u32[]{:S(2)}) collective-permute-start(bf16[192,768]{1,0:T(8,128)(2,1)S(1)} %pad_maximum_fusion.n0), channel_id=1, source_target_pairs={{0,96},{32,0},{64,32},{96,64},{1,97},{33,1},{65,33},{97,65},{2,98}... | collective-permute-start | bytes 884744 | tf_op jit(solution)/shard_map/ppermute | solution.py:28
  52.5 26.4 %collective-permute-start.11 = (f32[256,768]{1,0:T(8,128)S(1)}, f32[256,768]{1,0:T(8,128)S(1)}, u32[]{:S(2)}, u32[]{:S(2)}) collective-permute-start(f32[256,768]{1,0:T(8,128)S(1)} %get-tuple-element.45), channel_id=1, source_target_pairs={{0,128},{128,0},{1,129},{129,1},{2,130},{130,2},{3,131},{131,3},{4... | collective-permute-start | bytes 2359304 | tf_op jit(solution)/shard_map/ppermute | solution.py:28
  52.6 15.2 %collective-permute-start.13 = (bf16[96,768]{1,0:T(8,128)(2,1)S(1)}, bf16[96,768]{1,0:T(8,128)(2,1)S(1)}, u32[]{:S(2)}, u32[]{:S(2)}) collective-permute-start(bf16[96,768]{1,0:T(8,128)(2,1)S(1)} %bitcast.16), channel_id=1, source_target_pairs={{0,24},{8,0},{16,8},{24,16},{1,25},{9,1},{17,9},{25,17},{2,26},{10... | collective-permute-start | bytes 442376 | tf_op jit(solution)/shard_map/ppermute | solution.py:28
  59.0 14.8 %collective-permute-start.14 = (bf16[96,768]{1,0:T(8,128)(2,1)S(1)}, bf16[96,768]{1,0:T(8,128)(2,1)S(1)}, u32[]{:S(2)}, u32[]{:S(2)}) collective-permute-start(bf16[96,768]{1,0:T(8,128)(2,1)S(1)} %bitcast.17), channel_id=1, source_target_pairs={{0,16},{8,24},{16,0},{24,8},{1,17},{9,25},{17,1},{25,9},{2,18},{10... | collective-permute-start | bytes 442376 | tf_op jit(solution)/shard_map/ppermute | solution.py:28
  63.0 13.4 %collective-permute-start.15 = (bf16[96,768]{1,0:T(8,128)(2,1)S(1)}, bf16[96,768]{1,0:T(8,128)(2,1)S(1)}, u32[]{:S(2)}, u32[]{:S(2)}) collective-permute-start(bf16[96,768]{1,0:T(8,128)(2,1)S(1)} %bitcast.18), channel_id=1, source_target_pairs={{0,8},{8,16},{16,24},{24,0},{1,9},{9,17},{17,25},{25,1},{2,10},{10... | collective-permute-start | bytes 442376 | tf_op jit(solution)/shard_map/ppermute | solution.py:28
  76.4 12.1 %collective-permute-start.18 = (bf16[288,768]{1,0:T(8,128)(2,1)S(1)}, bf16[288,768]{1,0:T(8,128)(2,1)S(1)}, u32[]{:S(2)}, u32[]{:S(2)}) collective-permute-start(bf16[288,768]{1,0:T(8,128)(2,1)S(1)} %constant_dynamic-update-slice_fusion.3.r0), channel_id=1, source_target_pairs={{0,96},{32,0},{64,32},{96,64},{1,97},{33,1},{65,33},{97,65},{2,98}... | collective-permute-start | bytes 1327112 | tf_op jit(solution)/shard_map/ppermute | solution.py:28
  77.2 11.8 %collective-permute-start.16 = (bf16[288,768]{1,0:T(8,128)(2,1)S(1)}, bf16[288,768]{1,0:T(8,128)(2,1)S(1)}, u32[]{:S(2)}, u32[]{:S(2)}) collective-permute-start(bf16[288,768]{1,0:T(8,128)(2,1)S(1)} %constant_dynamic-update-slice_fusion.3.r0), channel_id=1, source_target_pairs={{0,32},{32,64},{64,96},{96,0},{1,33},{33,65},{65,97},{97,1},{2,34}... | collective-permute-start | bytes 1327112 | tf_op jit(solution)/shard_map/ppermute | solution.py:28
  78.8 67.2 %collective-permute-start.22 = (bf16[3,3072,384]{2,1,0:T(8,128)(2,1)}, bf16[3,3072,384]{2,1,0:T(8,128)(2,1)}, u32[]{:S(2)}, u32[]{:S(2)}) collective-permute-start(bf16[3,3072,384]{2,1,0:T(8,128)(2,1)} %bitcast.7.own_hbm), channel_id=1, source_target_pairs={{0,128},{128,0},{1,129},{129,1},{2,130},{130,2},{3,131},{131,3},{4... | collective-permute-start | bytes 21233672 | tf_op jit(solution)/shard_map/ppermute | solution.py:28
  80.1 10.7 %collective-permute-start.12 = (bf16[256,768]{1,0:T(8,128)(2,1)S(1)}, bf16[256,768]{1,0:T(8,128)(2,1)S(1)}, u32[]{:S(2)}, u32[]{:S(2)}) collective-permute-start(bf16[256,768]{1,0:T(8,128)(2,1)S(1)} %get-tuple-element.46.hidden_ref), channel_id=1, source_target_pairs={{0,128},{128,0},{1,129},{129,1},{2,130},{130,2},{3,131},{131,3},{4... | collective-permute-start | bytes 1179656 | tf_op jit(solution)/shard_map/ppermute | solution.py:28
  108.2 26.4 %all-to-all-start = ((bf16[8,256,384]{2,1,0:T(8,128)(2,1)}), bf16[8,256,384]{2,1,0:T(8,128)(2,1)S(1)}, u32[]{:S(2)}, u32[]{:S(2)}) async-start(bf16[8,256,384]{2,1,0:T(8,128)(2,1)} %bitcast_dynamic-update-slice_fusion), calls=%async_computation | async-start | bytes 3145728 | tf_op jit(solution)/shard_map/all_to_all | solution.py:71
  137.5 24.3 %all-to-all-start.1 = ((bf16[8,256,384]{2,1,0:T(8,128)(2,1)}), bf16[8,256,384]{2,1,0:T(8,128)(2,1)S(1)}, u32[]{:S(2)}, u32[]{:S(2)}) async-start(bf16[8,256,384]{2,1,0:T(8,128)(2,1)} %copy-done.3), calls=%async_computation.1 | async-start | bytes 3145728 | tf_op jit(solution)/shard_map/all_to_all | solution.py:71
  209.7 24.0 %all-to-all-start.3 = ((bf16[8,256,384]{2,1,0:T(8,128)(2,1)}), bf16[8,256,384]{2,1,0:T(8,128)(2,1)S(1)}, u32[]{:S(2)}, u32[]{:S(2)}) async-start(bf16[8,256,384]{2,1,0:T(8,128)(2,1)} %copy-done.4), calls=%async_computation.3 | async-start | bytes 3145728 | tf_op jit(solution)/shard_map/all_to_all | solution.py:71
  244.8 10.6 %collective-permute-start.34 = (bf16[192,768]{1,0:T(8,128)(2,1)S(1)}, bf16[192,768]{1,0:T(8,128)(2,1)S(1)}, u32[]{:S(2)}, u32[]{:S(2)}) collective-permute-start(bf16[192,768]{1,0:T(8,128)(2,1)S(1)} %get-tuple-element.72), channel_id=1, source_target_pairs={{0,32},{32,64},{64,96},{96,0},{1,33},{33,65},{65,97},{97,1},{2,34}... | collective-permute-start | bytes 884744 | tf_op jit(solution)/shard_map/ppermute | solution.py:28
  250.0 11.8 %collective-permute-start.27 = (bf16[192,768]{1,0:T(8,128)(2,1)S(1)}, bf16[192,768]{1,0:T(8,128)(2,1)S(1)}, u32[]{:S(2)}, u32[]{:S(2)}) collective-permute-start(bf16[192,768]{1,0:T(8,128)(2,1)S(1)} %get-tuple-element.63), channel_id=1, source_target_pairs={{0,32},{32,64},{64,96},{96,0},{1,33},{33,65},{65,97},{97,1},{2,34}... | collective-permute-start | bytes 884744 | tf_op jit(solution)/shard_map/ppermute | solution.py:28
  250.0 11.7 %collective-permute-start.28 = (bf16[192,768]{1,0:T(8,128)(2,1)S(1)}, bf16[192,768]{1,0:T(8,128)(2,1)S(1)}, u32[]{:S(2)}, u32[]{:S(2)}) collective-permute-start(bf16[192,768]{1,0:T(8,128)(2,1)S(1)} %get-tuple-element.64), channel_id=1, source_target_pairs={{0,96},{32,0},{64,32},{96,64},{1,97},{33,1},{65,33},{97,65},{2,98}... | collective-permute-start | bytes 884744 | tf_op jit(solution)/shard_map/ppermute | solution.py:28
  255.6 18.8 %collective-permute-start.36 = (bf16[384,768]{1,0:T(8,128)(2,1)S(1)}, bf16[384,768]{1,0:T(8,128)(2,1)S(1)}, u32[]{:S(2)}, u32[]{:S(2)}) collective-permute-start(bf16[384,768]{1,0:T(8,128)(2,1)S(1)} %get-tuple-element.74), channel_id=1, source_target_pairs={{0,32},{32,64},{64,96},{96,0},{1,33},{33,65},{65,97},{97,1},{2,34}... | collective-permute-start | bytes 1769480 | tf_op jit(solution)/shard_map/ppermute | solution.py:28
  258.3 17.4 %collective-permute-start.37 = (bf16[384,768]{1,0:T(8,128)(2,1)S(1)}, bf16[384,768]{1,0:T(8,128)(2,1)S(1)}, u32[]{:S(2)}, u32[]{:S(2)}) collective-permute-start(bf16[384,768]{1,0:T(8,128)(2,1)S(1)} %get-tuple-element.75), channel_id=1, source_target_pairs={{0,96},{32,0},{64,32},{96,64},{1,97},{33,1},{65,33},{97,65},{2,98}... | collective-permute-start | bytes 1769480 | tf_op jit(solution)/shard_map/ppermute | solution.py:28
  261.9 24.8 %collective-permute-start.29 = (bf16[384,768]{1,0:T(8,128)(2,1)S(1)}, bf16[384,768]{1,0:T(8,128)(2,1)S(1)}, u32[]{:S(2)}, u32[]{:S(2)}) collective-permute-start(bf16[384,768]{1,0:T(8,128)(2,1)S(1)} %get-tuple-element.65), channel_id=1, source_target_pairs={{0,32},{32,64},{64,96},{96,0},{1,33},{33,65},{65,97},{97,1},{2,34}... | collective-permute-start | bytes 1769480 | tf_op jit(solution)/shard_map/ppermute | solution.py:28
  264.6 22.1 %collective-permute-start.30 = (bf16[384,768]{1,0:T(8,128)(2,1)S(1)}, bf16[384,768]{1,0:T(8,128)(2,1)S(1)}, u32[]{:S(2)}, u32[]{:S(2)}) collective-permute-start(bf16[384,768]{1,0:T(8,128)(2,1)S(1)} %get-tuple-element.66), channel_id=1, source_target_pairs={{0,96},{32,0},{64,32},{96,64},{1,97},{33,1},{65,33},{97,65},{2,98}... | collective-permute-start | bytes 1769480 | tf_op jit(solution)/shard_map/ppermute | solution.py:28
  276.1 15.2 %collective-permute-start.38 = (bf16[96,768]{1,0:T(8,128)(2,1)S(1)}, bf16[96,768]{1,0:T(8,128)(2,1)S(1)}, u32[]{:S(2)}, u32[]{:S(2)}) collective-permute-start(bf16[96,768]{1,0:T(8,128)(2,1)S(1)} %get-tuple-element.77), channel_id=1, source_target_pairs={{0,8},{8,16},{16,24},{24,0},{1,9},{9,17},{17,25},{25,1},{2,10},{10... | collective-permute-start | bytes 442376 | tf_op jit(solution)/shard_map/ppermute | solution.py:28
  278.5 17.7 %collective-permute-start.39 = (bf16[96,768]{1,0:T(8,128)(2,1)S(1)}, bf16[96,768]{1,0:T(8,128)(2,1)S(1)}, u32[]{:S(2)}, u32[]{:S(2)}) collective-permute-start(bf16[96,768]{1,0:T(8,128)(2,1)S(1)} %get-tuple-element.78), channel_id=1, source_target_pairs={{0,24},{8,0},{16,8},{24,16},{1,25},{9,1},{17,9},{25,17},{2,26},{10... | collective-permute-start | bytes 442376 | tf_op jit(solution)/shard_map/ppermute | solution.py:28
  280.3 15.9 %collective-permute-start.40 = (bf16[96,768]{1,0:T(8,128)(2,1)S(1)}, bf16[96,768]{1,0:T(8,128)(2,1)S(1)}, u32[]{:S(2)}, u32[]{:S(2)}) collective-permute-start(bf16[96,768]{1,0:T(8,128)(2,1)S(1)} %get-tuple-element.79), channel_id=1, source_target_pairs={{0,16},{8,24},{16,0},{24,8},{1,17},{9,25},{17,1},{25,9},{2,18},{10... | collective-permute-start | bytes 442376 | tf_op jit(solution)/shard_map/ppermute | solution.py:28
  289.5 17.6 %collective-permute-start.32 = (bf16[96,768]{1,0:T(8,128)(2,1)S(1)}, bf16[96,768]{1,0:T(8,128)(2,1)S(1)}, u32[]{:S(2)}, u32[]{:S(2)}) collective-permute-start(bf16[96,768]{1,0:T(8,128)(2,1)S(1)} %get-tuple-element.69), channel_id=1, source_target_pairs={{0,24},{8,0},{16,8},{24,16},{1,25},{9,1},{17,9},{25,17},{2,26},{10... | collective-permute-start | bytes 442376 | tf_op jit(solution)/shard_map/ppermute | solution.py:28
  291.3 15.8 %collective-permute-start.33 = (bf16[96,768]{1,0:T(8,128)(2,1)S(1)}, bf16[96,768]{1,0:T(8,128)(2,1)S(1)}, u32[]{:S(2)}, u32[]{:S(2)}) collective-permute-start(bf16[96,768]{1,0:T(8,128)(2,1)S(1)} %get-tuple-element.70), channel_id=1, source_target_pairs={{0,16},{8,24},{16,0},{24,8},{1,17},{9,25},{17,1},{25,9},{2,18},{10... | collective-permute-start | bytes 442376 | tf_op jit(solution)/shard_map/ppermute | solution.py:28
  (30 other events, 194.5 us)

commit v2 on v1

--- a/solution.py
+++ b/solution.py
@@ -36,16 +36,19 @@
     return value.astype(jnp.bfloat16)
 
 
-def direct_gather(block, axis):
-    return [block] + [hop(block, axis, -k) for k in (1, 2, 3)]
-
-
-def ring_gather(block, axis):
+def direct_gather(block, axis, offsets=(1, 2, 3)):
+    return [hop(block, axis, -k) for k in offsets]
+
+
+def ring_gather(block, axis, ahead=None):
     half = block.shape[0] // 2
     left = hop(block, axis, 1)
     right = hop(block, axis, -1)
-    far_top = hop(left[:half], axis, 1)
-    far_bottom = hop(right[half:], axis, -1)
+    top, bottom = left[:half], right[half:]
+    if ahead is not None:
+        top, bottom = jnp.concatenate([ahead[0], top]), jnp.concatenate([ahead[1], bottom])
+    far_top = hop(top, axis, 1)
+    far_bottom = hop(bottom, axis, -1)
     return [block, right, far_top, far_bottom, left]
 
 
@@ -131,13 +134,15 @@
     lax.fori_loop(0, SEQ // 16, tile, 0)
 
 
-def up_kernel(own_ref, crossed_ref, n0, n1, n2, n3, r0, r1, far_top, far_bottom, r3, here, away):
-    blocks = ((n0, (r0,)), (n1, (r1,)), (n2, (far_top, far_bottom)), (n3, (r3,)))
+def up_kernel(own_ref, crossed_ref, n0, n1, n3, r0, r1, far_top, far_bottom, r3, here, away):
+    blocks = ((n0, r0), (n1, r1), (None, None), (n3, r3))
 
     def columns(c, _):
         lanes = lane_chunk(c)
         weights = [
-            jnp.concatenate([near[:SHARD, lanes]] + [piece[:, lanes] for piece in rest])
+            jnp.concatenate([near[:SHARD, lanes], rest[:, lanes]])
+            if near is not None
+            else jnp.concatenate([far_top[:, lanes], far_bottom[SHARD:, lanes]])
             for near, rest in blocks
         ]
         for normed, total in ((own_ref, here), (crossed_ref, away)):
@@ -213,14 +218,14 @@
 
 
 def down_far_kernel(
-    at_ref, hidden_ref, crossed_ref, n2, far_top, far_bottom, here_ref, arrived_ref,
+    at_ref, hidden_ref, crossed_ref, own_far, far_top, far_bottom, here_ref, arrived_ref,
     down_ref, parts_ref, away_ref,
 ):
     group, x, zh = at_ref[0], at_ref[1], at_ref[2]
     half = SHARD // 2
     for dz, pieces in enumerate(
         (
-            (n2[SHARD : SHARD + half, :], n2[SHARD + half :, :]),
+            (own_far[:half, :], own_far[half:SHARD, :]),
             (far_top[:half, :], far_top[half:SHARD, :]),
             (far_top[SHARD:, :], far_bottom[:half, :]),
             (far_bottom[half:SHARD, :], far_bottom[SHARD:, :]),
@@ -236,22 +241,24 @@
         parts_ref[(1 - group) * 4 + ((x + dx) & 3)] = arrived_ref[i]
 
 
-def fetch_kernel(own_hbm, other_hbm, out_own_hbm, out_other_hbm, qkv_w, out_w, sems):
-    loads = [
-        pltpu.make_async_copy(own_hbm, qkv_w.at[:3], sems.at[0]),
-        pltpu.make_async_copy(other_hbm, qkv_w.at[3:], sems.at[1]),
-        pltpu.make_async_copy(out_own_hbm, out_w.at[0], sems.at[2]),
-        pltpu.make_async_copy(out_other_hbm, out_w.at[1], sems.at[3]),
-    ]
-    for load in loads:
-        load.start()
-    for load in loads:
-        load.wait()
-
-
 def score_kernel(
-    sign_ref, noisy_ref, qkv_w, out_w, gap_ref, normed_ref, qkv_ref, mix_ref
+    sign_ref, noisy_ref, own_hbm, other_hbm, out_own_hbm, out_other_hbm, gap_ref,
+    qkv_w, out_w, normed_ref, qkv_ref, mix_ref, qkv_sem, out_sem,
 ):
+    loads = []
+    for net, (source, out_source) in enumerate(
+        ((own_hbm, out_own_hbm), (other_hbm, out_other_hbm))
+    ):
+        for k in range(3):
+            loads.append(
+                pltpu.make_async_copy(
+                    source.at[k], qkv_w.at[net * 3 + k], qkv_sem.at[net * 3 + k]
+                )
+            )
+        loads.append(pltpu.make_async_copy(out_source, out_w.at[net], out_sem.at[net]))
+    for k in (0, 1, 2, 4, 5, 6, 3, 7):
+        loads[k].start()
+
     def norm(i, _):
         rows = row_tile(i)
         blocks = [wide(noisy_ref[j, rows, :]) for j in range(8)]
@@ -265,7 +272,9 @@
 
     def network(net, _):
         def project(k, _):
-            qkv_ref[k] = narrow(dot(normed_ref[...], qkv_w[net * 3 + k]))
+            slot = net * 3 + k
+            pltpu.make_async_copy(own_hbm.at[0], qkv_w.at[slot], qkv_sem.at[slot]).wait()
+            qkv_ref[k] = narrow(dot(normed_ref[...], qkv_w[slot]))
             return 0
 
         lax.fori_loop(0, 3, project, 0)
@@ -284,6 +293,8 @@
         return 0
 
     lax.fori_loop(0, 2, network, 0)
+    loads[3].wait()
+    loads[7].wait()
 
     def emit(j, _):
         columns = pl.ds(pl.multiple_of(j * 2 * BLOCK, 2 * BLOCK), 2 * BLOCK)
@@ -410,11 +421,12 @@
 
     down_shard = gen_down.T
     up_z = direct_gather(gen_up, "zh")
-    near = direct_gather(jnp.concatenate([gen_up, down_shard]), "x")
-    up_cat = jnp.concatenate(up_z[1:])
-    up_rest = ring_gather(up_cat, "x")
+    both = jnp.concatenate([gen_up, down_shard])
+    near_right, near_left = direct_gather(both, "x", (1, 3))
+    near = [both, near_right, near_left]
+    up_rest = ring_gather(jnp.concatenate(up_z), "x", (near_left[:SHARD], near_right[SHARD:]))
     down_z = direct_gather(down_shard, "zh")
-    down_rest = ring_gather(jnp.concatenate(down_z[1:]), "x")
+    down_rest = ring_gather(jnp.concatenate(down_z), "x")
     qkv_own, out_own = score_qkv[0], score_out[0]
     qkv_other, out_other = swap(qkv_own), swap(out_own)
 
@@ -428,7 +440,7 @@
     )(noise_seeds, (feature * 668265263)[None])
     normed_crossed = swap(normed_away)
     here, away = local_call(
-        up_kernel, [VMEM] * 11, (before_kind, before_kind), matmul, 5_000_000
+        up_kernel, [VMEM] * 10, (before_kind, before_kind), matmul, 5_000_000
     )(normed, normed_crossed, *near, *up_rest)
     before, hidden = local_call(
         hidden_kernel, [VMEM] * 2, (before_kind, hidden_kind), 3_000_000, 2_800_000
@@ -445,7 +457,7 @@
         at,
         hidden,
         hidden_crossed,
-        *(near[k] for k in EARLY),
+        *near,
         *(down_rest[k] for k in (0, 1, 4)),
     )
     eight_kind = array(8, SEQ, BLOCK)
@@ -455,7 +467,7 @@
         (array(BLOCK, FF_LOCAL), eight_kind, array(SEQ, BLOCK)),
         300_000_000,
         4_000_000,
-    )(at, hidden, hidden_crossed, near[2], down_rest[2], down_rest[3], parts_here, swap(parts_away))
+    )(at, hidden, hidden_crossed, up_rest[3], down_rest[2], down_rest[3], parts_here, swap(parts_away))
     parts = lax.dynamic_update_index_in_dim(
         parts, swap(part_away), (1 - group) * 4 + ((x + 2) & 3), 0
     )
@@ -471,29 +483,24 @@
         limit=16,
     )(noise_seeds, shift[None], (local * 668265263)[None], exchange(parts))
     noisy_all = exchange(noisy)
-    qkv_both, out_both = local_call(
-        fetch_kernel,
-        [HBM] * 4,
-        (array(6, D, BLOCK), array(2, BLOCK, D)),
-        1_000_000,
-        38_000_000,
-        scratch=[pltpu.SemaphoreType.DMA((4,))],
-        limit=44,
-    )(qkv_own, qkv_other, out_own, out_other)
     sign = wide(2 * group - 1)[None]
     gap_parts = local_call(
         score_kernel,
-        [SMEM] + [VMEM] * 3,
+        [SMEM, VMEM] + [HBM] * 4,
         array(8, SEQ, BLOCK),
         5_000_000_000,
         20_000_000,
         scratch=[
+            pltpu.VMEM((6, D, BLOCK), jnp.bfloat16),
+            pltpu.VMEM((2, BLOCK, D), jnp.bfloat16),
             pltpu.VMEM((SEQ, D), jnp.bfloat16),
             pltpu.VMEM((3, SEQ, BLOCK), jnp.bfloat16),
             pltpu.VMEM((2, SEQ, BLOCK), jnp.bfloat16),
+            pltpu.SemaphoreType.DMA((6,)),
+            pltpu.SemaphoreType.DMA((2,)),
         ],
-        limit=42,
-    )(sign, noisy_all, qkv_both, out_both)
+        limit=44,
+    )(sign, noisy_all, qkv_own, qkv_other, out_own, out_other)
     gap, gap_copies = local_call(
         gap_kernel, [VMEM], (array(SEQ, BLOCK), eight_kind), 1_000_000, 4_000_000
     )(exchange(gap_parts))

time: 312 us -> 297 us (0.952)
  Pallas kernels: 51.1 us -> 35.7 us
  waiting for transfers between devices: 135 us -> 145 us
  local copies, waits for them, and re-layouts: 11.1 us -> 6.71 us
    pallas_call x3 -> x2, Pallas kernels: 30.5 us -> 15 us  [the longest x1 12.8 us: step(): local_call(score_kernel, [SMEM, VMEM] + [HBM] * 4, array(8, SEQ, BLOCK),...]
    all_to_all x3, waiting for transfers between devices: 42.6 us -> 57.1 us  [exchange(): return lax.all_to_all(parts, MODEL, 0, 0, tiled=True)]
    ppermute x41 -> x40, waiting for transfers between devices: 92.8 us -> 87.7 us  [hop(): return lax.ppermute(value, axis, [(i, (i + step) % n) for i in range(n)])]
    unnamed x40 -> x36, local copies, waits for them, and re-layouts: 10.3 us -> 5.82 us
    ppermute x41 -> x40, starting transfers between devices: 67.6 us -> 64.2 us  [hop(): return lax.ppermute(value, axis, [(i, (i + step) % n) for i in range(n)])]
  transfers between devices with their start and end apart: 44 -> 43, of which waited for: 30 -> 27; matrix products, arithmetic and copies ran while one was open for 1% -> 1% of each run, Pallas kernels for 9% -> 6%
where the time goes in v2:
time: 297 us; the launch traced here: 294 us
  waiting for transfers between devices  145 us (49%)
  starting transfers between devices  78 us (26%)
  Pallas kernels  35.7 us (12%)
  blocking collectives  24.2 us (8%)
  local copies, waits for them, and re-layouts  6.71 us (2%)
    ppermute x40, waiting for transfers between devices, hop(): return lax.ppermute(value, axis, [(i, (i + step) % n) for i in range(n)])  87.7 us
    ppermute x40, starting transfers between devices, hop(): return lax.ppermute(value, axis, [(i, (i + step) % n) for i in range(n)])  64.2 us
    all_to_all x3, waiting for transfers between devices, exchange(): return lax.all_to_all(parts, MODEL, 0, 0, tiled=True)  57.1 us
    all_to_all x1, blocking collectives, exchange(): return lax.all_to_all(parts, MODEL, 0, 0, tiled=True)  24.2 us
    all_to_all x3, starting transfers between devices, exchange(): return lax.all_to_all(parts, MODEL, 0, 0, tiled=True)  13.8 us
    pallas_call x1, Pallas kernels, step(): local_call(score_kernel, [SMEM, VMEM] + [HBM] * 4, array(8, SEQ, BLOCK),...  12.8 us
  transfers between devices with their start and end apart: 43, of which 27 were waited for; matrix products, arithmetic and copies ran while one was open for 1% of the time, Pallas kernels for 6%

profile of v2, /device:TPU:2, one launch (start us, length us, event | category | flops | bytes accessed | tf_op | source)
XLA Modules:
  0.0 294.5 jit_solution(1828962666514615415)
XLA Ops:
  0.6 6.4 %collective-permute-start.3 = (bf16[96,768]{1,0:T(8,128)(2,1)}, bf16[96,768]{1,0:T(8,128)(2,1)S(1)}, u32[]{:S(2)}, u32[]{:S(2)}) collective-permute-start(bf16[96,768]{1,0:T(8,128)(2,1)} %param.8), channel_id=1, source_target_pairs={{0,24},{8,0},{16,8},{24,16},{1,25},{9,1},{17,9},{25,17},{2,26},{10... | collective-permute-start | bytes 442376 | tf_op jit(solution)/shard_map/ppermute | solution.py:28
  7.0 3.8 %collective-permute-start.4 = (bf16[96,768]{1,0:T(8,128)(2,1)}, bf16[96,768]{1,0:T(8,128)(2,1)S(1)}, u32[]{:S(2)}, u32[]{:S(2)}) collective-permute-start(bf16[96,768]{1,0:T(8,128)(2,1)} %param.8), channel_id=1, source_target_pairs={{0,16},{8,24},{16,0},{24,8},{1,17},{9,25},{17,1},{25,9},{2,18},{10... | collective-permute-start | bytes 442376 | tf_op jit(solution)/shard_map/ppermute | solution.py:28
  13.9 4.9 %collective-permute-done.3 = bf16[96,768]{1,0:T(8,128)(2,1)S(1)} collective-permute-done((bf16[96,768]{1,0:T(8,128)(2,1)}, bf16[96,768]{1,0:T(8,128)(2,1)S(1)}, u32[]{:S(2)}, u32[]{:S(2)}) %collective-permute-start.3) | collective-permute-done | bytes 147488 | tf_op jit(solution)/shard_map/ppermute | solution.py:28
  24.3 3.5 %shard_map.93 = (bf16[256,1536]{1,0:T(8,128)(2,1)S(1)}, bf16[256,1536]{1,0:T(8,128)(2,1)S(1)}) custom-call(s32[1]{0:T(128)S(6)} %copy.15.seed_ref.ids_ref, s32[1,3072]{1,0:T(1,128)S(1)} %fusion.2.feature_ref), custom_call_target="tpu_custom_call" | custom-call | flops 30000000 | bytes 1600000 | tf_op jit(solution)/shard_map/pallas_call | solution.py:438
  28.0 3.1 %collective-permute-done.7.r3 = bf16[288,768]{1,0:T(8,128)(2,1)S(1)} collective-permute-done((bf16[288,768]{1,0:T(8,128)(2,1)S(1)}, bf16[288,768]{1,0:T(8,128)(2,1)S(1)}, u32[]{:S(2)}, u32[]{:S(2)}) %collective-permute-start.7) | collective-permute-done | bytes 442400 | tf_op jit(solution)/shard_map/ppermute | solution.py:28
  33.3 5.8 %collective-permute-done.8.far_top = bf16[240,768]{1,0:T(8,128)(2,1)S(1)} collective-permute-done((bf16[240,768]{1,0:T(8,128)(2,1)S(1)}, bf16[240,768]{1,0:T(8,128)(2,1)S(1)}, u32[]{:S(2)}, u32[]{:S(2)}) %collective-permute-start.8) | collective-permute-done | bytes 368672 | tf_op jit(solution)/shard_map/ppermute | solution.py:28
  42.7 8.1 %collective-permute-start.12 = (bf16[96,768]{1,0:T(8,128)(2,1)S(1)}, bf16[96,768]{1,0:T(8,128)(2,1)S(1)}, u32[]{:S(2)}, u32[]{:S(2)}) collective-permute-start(bf16[96,768]{1,0:T(8,128)(2,1)S(1)} %bitcast.16), channel_id=1, source_target_pairs={{0,24},{8,0},{16,8},{24,16},{1,25},{9,1},{17,9},{25,17},{2,26},{10... | collective-permute-start | bytes 442376 | tf_op jit(solution)/shard_map/ppermute | solution.py:28
  53.3 3.3 %collective-permute-done.12 = bf16[96,768]{1,0:T(8,128)(2,1)S(1)} collective-permute-done((bf16[96,768]{1,0:T(8,128)(2,1)S(1)}, bf16[96,768]{1,0:T(8,128)(2,1)S(1)}, u32[]{:S(2)}, u32[]{:S(2)}) %collective-permute-start.12) | collective-permute-done | bytes 147488 | tf_op jit(solution)/shard_map/ppermute | solution.py:28
  56.6 8.0 %collective-permute-done.13 = bf16[96,768]{1,0:T(8,128)(2,1)S(1)} collective-permute-done((bf16[96,768]{1,0:T(8,128)(2,1)S(1)}, bf16[96,768]{1,0:T(8,128)(2,1)S(1)}, u32[]{:S(2)}, u32[]{:S(2)}) %collective-permute-start.13) | collective-permute-done | bytes 147488 | tf_op jit(solution)/shard_map/ppermute | solution.py:28
  69.7 7.7 %collective-permute-done.17.r1 = bf16[288,768]{1,0:T(8,128)(2,1)S(1)} collective-permute-done((bf16[288,768]{1,0:T(8,128)(2,1)S(1)}, bf16[288,768]{1,0:T(8,128)(2,1)S(1)}, u32[]{:S(2)}, u32[]{:S(2)}) %collective-permute-start.17) | collective-permute-done | bytes 442400 | tf_op jit(solution)/shard_map/ppermute | solution.py:28
  82.6 3.0 %collective-permute-start.18 = (bf16[144,768]{1,0:T(8,128)(2,1)S(1)}, bf16[144,768]{1,0:T(8,128)(2,1)S(1)}, u32[]{:S(2)}, u32[]{:S(2)}) collective-permute-start(bf16[144,768]{1,0:T(8,128)(2,1)S(1)} %slice.29), channel_id=1, source_target_pairs={{0,96},{32,0},{64,32},{96,64},{1,97},{33,1},{65,33},{97,65},{2,98}... | collective-permute-start | bytes 663560 | tf_op jit(solution)/shard_map/ppermute | solution.py:28
  85.7 5.2 %collective-permute-done.18.far_bottom = bf16[144,768]{1,0:T(8,128)(2,1)S(1)} collective-permute-done((bf16[144,768]{1,0:T(8,128)(2,1)S(1)}, bf16[144,768]{1,0:T(8,128)(2,1)S(1)}, u32[]{:S(2)}, u32[]{:S(2)}) %collective-permute-start.18) | collective-permute-done | bytes 221216 | tf_op jit(solution)/shard_map/ppermute | solution.py:28
  91.0 3.3 %collective-permute-done.16.far_top = bf16[144,768]{1,0:T(8,128)(2,1)S(1)} collective-permute-done((bf16[144,768]{1,0:T(8,128)(2,1)S(1)}, bf16[144,768]{1,0:T(8,128)(2,1)S(1)}, u32[]{:S(2)}, u32[]{:S(2)}) %collective-permute-start.16) | collective-permute-done | bytes 221216 | tf_op jit(solution)/shard_map/ppermute | solution.py:28
  99.9 6.6 %all-to-all-start = ((bf16[8,256,384]{2,1,0:T(8,128)(2,1)}), bf16[8,256,384]{2,1,0:T(8,128)(2,1)S(1)}, u32[]{:S(2)}, u32[]{:S(2)}) async-start(bf16[8,256,384]{2,1,0:T(8,128)(2,1)} %bitcast_dynamic-update-slice_fusion), calls=%async_computation | async-start | bytes 3145728 | tf_op jit(solution)/shard_map/all_to_all | solution.py:74
  107.2 21.0 %all-to-all-done.parts_ref = bf16[8,256,384]{2,1,0:T(8,128)(2,1)S(1)} async-done(((bf16[8,256,384]{2,1,0:T(8,128)(2,1)}), bf16[8,256,384]{2,1,0:T(8,128)(2,1)S(1)}, u32[]{:S(2)}, u32[]{:S(2)}) %all-to-all-start) | async-done | bytes 1572896 | tf_op jit(solution)/shard_map/all_to_all | solution.py:74
  131.0 3.6 %all-to-all-start.1 = ((bf16[8,256,384]{2,1,0:T(8,128)(2,1)}), bf16[8,256,384]{2,1,0:T(8,128)(2,1)S(1)}, u32[]{:S(2)}, u32[]{:S(2)}) async-start(bf16[8,256,384]{2,1,0:T(8,128)(2,1)} %copy-done.1), calls=%async_computation.1 | async-start | bytes 3145728 | tf_op jit(solution)/shard_map/all_to_all | solution.py:74
  134.7 4.9 %collective-permute-done.22.out_other_hbm = bf16[384,3072]{1,0:T(8,128)(2,1)} collective-permute-done((bf16[384,3072]{1,0:T(8,128)(2,1)}, bf16[384,3072]{1,0:T(8,128)(2,1)}, u32[]{:S(2)}, u32[]{:S(2)}) %collective-permute-start.22) | collective-permute-done | bytes 2359328 | tf_op jit(solution)/shard_map/ppermute | solution.py:28
  139.5 15.8 %all-to-all-done.1.noisy_ref = bf16[8,256,384]{2,1,0:T(8,128)(2,1)S(1)} async-done(((bf16[8,256,384]{2,1,0:T(8,128)(2,1)}), bf16[8,256,384]{2,1,0:T(8,128)(2,1)S(1)}, u32[]{:S(2)}, u32[]{:S(2)}) %all-to-all-start.1) | async-done | bytes 1572896 | tf_op jit(solution)/shard_map/all_to_all | solution.py:74
  157.0 12.8 %shard_map.99 = bf16[8,256,384]{2,1,0:T(8,128)(2,1)S(1)} custom-call(f32[1]{0:T(128)} %bitcast.6.sign_ref, bf16[8,256,384]{2,1,0:T(8,128)(2,1)S(1)} %all-to-all-done.1.noisy_ref, bf16[3,3072,384]{2,1,0:T(8,128)(2,1)} %bitcast.7.own_hbm, bf16[3,3072,384]{2,1,0:T(8,128)(2,1)} %collective-permute-done.21.other_hbm, bf16[384,3072]{1,0:T(8,128)(2,1)S(1)} %bitcast.14, ...), custom_call_target="tpu_custom_call" | custom-call | flops 5000000000 | bytes 20000000 | tf_op jit(solution)/shard_map/pallas_call | solution.py:487
  169.8 24.2 %all_to_all.20.parts_ref = bf16[8,256,384]{2,1,0:T(8,128)(2,1)S(1)} all-to-all(bf16[8,256,384]{2,1,0:T(8,128)(2,1)S(1)} %shard_map.99), channel_id=1, replica_groups=mesh['group'=2,'x'=4,'zh'=4,'y'=4,'zl'=2] {'y','zl'}, dimensions={0} | all-to-all | bytes 3145728 | tf_op jit(solution)/shard_map/all_to_all | solution.py:74
  196.2 3.6 %all-to-all-start.3 = ((bf16[8,256,384]{2,1,0:T(8,128)(2,1)}), bf16[8,256,384]{2,1,0:T(8,128)(2,1)S(1)}, u32[]{:S(2)}, u32[]{:S(2)}) async-start(bf16[8,256,384]{2,1,0:T(8,128)(2,1)} %copy-done.2), calls=%async_computation.3 | async-start | bytes 3145728 | tf_op jit(solution)/shard_map/all_to_all | solution.py:74
  199.8 20.3 %all-to-all-done.3.gap_ref = bf16[8,256,384]{2,1,0:T(8,128)(2,1)S(1)} async-done(((bf16[8,256,384]{2,1,0:T(8,128)(2,1)}), bf16[8,256,384]{2,1,0:T(8,128)(2,1)S(1)}, u32[]{:S(2)}, u32[]{:S(2)}) %all-to-all-start.3) | async-done | bytes 1572896 | tf_op jit(solution)/shard_map/all_to_all | solution.py:74
  231.3 3.2 %collective-permute-start.34 = (bf16[192,768]{1,0:T(8,128)(2,1)S(1)}, bf16[192,768]{1,0:T(8,128)(2,1)S(1)}, u32[]{:S(2)}, u32[]{:S(2)}) collective-permute-start(bf16[192,768]{1,0:T(8,128)(2,1)S(1)} %get-tuple-element.69), channel_id=1, source_target_pairs={{0,96},{32,0},{64,32},{96,64},{1,97},{33,1},{65,33},{97,65},{2,98}... | collective-permute-start | bytes 884744 | tf_op jit(solution)/shard_map/ppermute | solution.py:28
  236.7 3.0 %collective-permute-start.27 = (bf16[192,768]{1,0:T(8,128)(2,1)S(1)}, bf16[192,768]{1,0:T(8,128)(2,1)S(1)}, u32[]{:S(2)}, u32[]{:S(2)}) collective-permute-start(bf16[192,768]{1,0:T(8,128)(2,1)S(1)} %get-tuple-element.60), channel_id=1, source_target_pairs={{0,96},{32,0},{64,32},{96,64},{1,97},{33,1},{65,33},{97,65},{2,98}... | collective-permute-start | bytes 884744 | tf_op jit(solution)/shard_map/ppermute | solution.py:28
  242.3 2.7 collective-permute-start.35
  245.7 2.7 collective-permute-done.26.for_right
  252.0 9.0 %collective-permute-done.35.from_left = bf16[384,768]{1,0:T(8,128)(2,1)S(1)} collective-permute-done((bf16[384,768]{1,0:T(8,128)(2,1)S(1)}, bf16[384,768]{1,0:T(8,128)(2,1)S(1)}, u32[]{:S(2)}, u32[]{:S(2)}) %collective-permute-start.35) | collective-permute-done | bytes 589856 | tf_op jit(solution)/shard_map/ppermute | solution.py:28
  264.2 2.8 collective-permute-start.38
  267.0 4.4 %collective-permute-start.39 = (bf16[96,768]{1,0:T(8,128)(2,1)S(1)}, bf16[96,768]{1,0:T(8,128)(2,1)S(1)}, u32[]{:S(2)}, u32[]{:S(2)}) collective-permute-start(bf16[96,768]{1,0:T(8,128)(2,1)S(1)} %get-tuple-element.75), channel_id=1, source_target_pairs={{0,16},{8,24},{16,0},{24,8},{1,17},{9,25},{17,1},{25,9},{2,18},{10... | collective-permute-start | bytes 442376 | tf_op jit(solution)/shard_map/ppermute | solution.py:28
  275.2 2.8 collective-permute-start.31
  278.0 4.4 %collective-permute-start.32 = (bf16[96,768]{1,0:T(8,128)(2,1)S(1)}, bf16[96,768]{1,0:T(8,128)(2,1)S(1)}, u32[]{:S(2)}, u32[]{:S(2)}) collective-permute-start(bf16[96,768]{1,0:T(8,128)(2,1)S(1)} %get-tuple-element.66), channel_id=1, source_target_pairs={{0,16},{8,24},{16,0},{24,8},{1,17},{9,25},{17,1},{25,9},{2,18},{10... | collective-permute-start | bytes 442376 | tf_op jit(solution)/shard_map/ppermute | solution.py:28
  283.1 9.2 %collective-permute-done.31 = bf16[96,768]{1,0:T(8,128)(2,1)S(1)} collective-permute-done((bf16[96,768]{1,0:T(8,128)(2,1)S(1)}, bf16[96,768]{1,0:T(8,128)(2,1)S(1)}, u32[]{:S(2)}, u32[]{:S(2)}) %collective-permute-start.31) | collective-permute-done | bytes 147488 | tf_op jit(solution)/shard_map/ppermute | solution.py:28
  (125 shorter events, 69.0 us)
Async XLA Ops:
  0.6 18.2 %collective-permute-start.3 = (bf16[96,768]{1,0:T(8,128)(2,1)}, bf16[96,768]{1,0:T(8,128)(2,1)S(1)}, u32[]{:S(2)}, u32[]{:S(2)}) collective-permute-start(bf16[96,768]{1,0:T(8,128)(2,1)} %param.8), channel_id=1, source_target_pairs={{0,24},{8,0},{16,8},{24,16},{1,25},{9,1},{17,9},{25,17},{2,26},{10... | collective-permute-start | bytes 442376 | tf_op jit(solution)/shard_map/ppermute | solution.py:28
  7.0 14.4 %collective-permute-start.5 = (bf16[96,768]{1,0:T(8,128)(2,1)}, bf16[96,768]{1,0:T(8,128)(2,1)S(1)}, u32[]{:S(2)}, u32[]{:S(2)}) collective-permute-start(bf16[96,768]{1,0:T(8,128)(2,1)} %param.8), channel_id=1, source_target_pairs={{0,8},{8,16},{16,24},{24,0},{1,9},{9,17},{17,25},{25,1},{2,10},{10... | collective-permute-start | bytes 442376 | tf_op jit(solution)/shard_map/ppermute | solution.py:28
  7.0 12.9 %collective-permute-start.4 = (bf16[96,768]{1,0:T(8,128)(2,1)}, bf16[96,768]{1,0:T(8,128)(2,1)S(1)}, u32[]{:S(2)}, u32[]{:S(2)}) collective-permute-start(bf16[96,768]{1,0:T(8,128)(2,1)} %param.8), channel_id=1, source_target_pairs={{0,16},{8,24},{16,0},{24,8},{1,17},{9,25},{17,1},{25,9},{2,18},{10... | collective-permute-start | bytes 442376 | tf_op jit(solution)/shard_map/ppermute | solution.py:28
  11.8 16.1 %collective-permute-start.2 = (bf16[192,768]{1,0:T(8,128)(2,1)S(1)}, bf16[192,768]{1,0:T(8,128)(2,1)S(1)}, u32[]{:S(2)}, u32[]{:S(2)}) collective-permute-start(bf16[192,768]{1,0:T(8,128)(2,1)S(1)} %pad_maximum_fusion.2.n0), channel_id=1, source_target_pairs={{0,32},{32,64},{64,96},{96,0},{1,33},{33,65},{65,97},{97,1},{2,34}... | collective-permute-start | bytes 884744 | tf_op jit(solution)/shard_map/ppermute | solution.py:28
  13.4 14.5 %collective-permute-start.1 = (bf16[192,768]{1,0:T(8,128)(2,1)S(1)}, bf16[192,768]{1,0:T(8,128)(2,1)S(1)}, u32[]{:S(2)}, u32[]{:S(2)}) collective-permute-start(bf16[192,768]{1,0:T(8,128)(2,1)S(1)} %pad_maximum_fusion.2.n0), channel_id=1, source_target_pairs={{0,96},{32,0},{64,32},{96,64},{1,97},{33,1},{65,33},{97,65},{2,98}... | collective-permute-start | bytes 884744 | tf_op jit(solution)/shard_map/ppermute | solution.py:28
  21.5 9.6 %collective-permute-start.7 = (bf16[288,768]{1,0:T(8,128)(2,1)S(1)}, bf16[288,768]{1,0:T(8,128)(2,1)S(1)}, u32[]{:S(2)}, u32[]{:S(2)}) collective-permute-start(bf16[288,768]{1,0:T(8,128)(2,1)S(1)} %constant_dynamic-update-slice_fusion.r0), channel_id=1, source_target_pairs={{0,32},{32,64},{64,96},{96,0},{1,33},{33,65},{65,97},{97,1},{2,34}... | collective-permute-start | bytes 1327112 | tf_op jit(solution)/shard_map/ppermute | solution.py:28
  23.0 9.6 %collective-permute-start.6 = (bf16[288,768]{1,0:T(8,128)(2,1)S(1)}, bf16[288,768]{1,0:T(8,128)(2,1)S(1)}, u32[]{:S(2)}, u32[]{:S(2)}) collective-permute-start(bf16[288,768]{1,0:T(8,128)(2,1)S(1)} %constant_dynamic-update-slice_fusion.r0), channel_id=1, source_target_pairs={{0,96},{32,0},{64,32},{96,64},{1,97},{33,1},{65,33},{97,65},{2,98}... | collective-permute-start | bytes 1327112 | tf_op jit(solution)/shard_map/ppermute | solution.py:28
  42.6 25.2 %collective-permute-start.10 = (f32[256,768]{1,0:T(8,128)S(1)}, f32[256,768]{1,0:T(8,128)S(1)}, u32[]{:S(2)}, u32[]{:S(2)}) collective-permute-start(f32[256,768]{1,0:T(8,128)S(1)} %get-tuple-element.43), channel_id=1, source_target_pairs={{0,128},{128,0},{1,129},{129,1},{2,130},{130,2},{3,131},{131,3},{4... | collective-permute-start | bytes 2359304 | tf_op jit(solution)/shard_map/ppermute | solution.py:28
  42.7 13.9 %collective-permute-start.12 = (bf16[96,768]{1,0:T(8,128)(2,1)S(1)}, bf16[96,768]{1,0:T(8,128)(2,1)S(1)}, u32[]{:S(2)}, u32[]{:S(2)}) collective-permute-start(bf16[96,768]{1,0:T(8,128)(2,1)S(1)} %bitcast.16), channel_id=1, source_target_pairs={{0,24},{8,0},{16,8},{24,16},{1,25},{9,1},{17,9},{25,17},{2,26},{10... | collective-permute-start | bytes 442376 | tf_op jit(solution)/shard_map/ppermute | solution.py:28
  50.8 13.8 %collective-permute-start.13 = (bf16[96,768]{1,0:T(8,128)(2,1)S(1)}, bf16[96,768]{1,0:T(8,128)(2,1)S(1)}, u32[]{:S(2)}, u32[]{:S(2)}) collective-permute-start(bf16[96,768]{1,0:T(8,128)(2,1)S(1)} %bitcast.17), channel_id=1, source_target_pairs={{0,16},{8,24},{16,0},{24,8},{1,17},{9,25},{17,1},{25,9},{2,18},{10... | collective-permute-start | bytes 442376 | tf_op jit(solution)/shard_map/ppermute | solution.py:28
  53.3 12.4 %collective-permute-start.14 = (bf16[96,768]{1,0:T(8,128)(2,1)S(1)}, bf16[96,768]{1,0:T(8,128)(2,1)S(1)}, u32[]{:S(2)}, u32[]{:S(2)}) collective-permute-start(bf16[96,768]{1,0:T(8,128)(2,1)S(1)} %bitcast.18), channel_id=1, source_target_pairs={{0,8},{8,16},{16,24},{24,0},{1,9},{9,17},{17,25},{25,1},{2,10},{10... | collective-permute-start | bytes 442376 | tf_op jit(solution)/shard_map/ppermute | solution.py:28
  65.7 11.7 %collective-permute-start.17 = (bf16[288,768]{1,0:T(8,128)(2,1)S(1)}, bf16[288,768]{1,0:T(8,128)(2,1)S(1)}, u32[]{:S(2)}, u32[]{:S(2)}) collective-permute-start(bf16[288,768]{1,0:T(8,128)(2,1)S(1)} %constant_dynamic-update-slice_fusion.3.r0), channel_id=1, source_target_pairs={{0,96},{32,0},{64,32},{96,64},{1,97},{33,1},{65,33},{97,65},{2,98}... | collective-permute-start | bytes 1327112 | tf_op jit(solution)/shard_map/ppermute | solution.py:28
  67.3 12.7 %collective-permute-start.15 = (bf16[288,768]{1,0:T(8,128)(2,1)S(1)}, bf16[288,768]{1,0:T(8,128)(2,1)S(1)}, u32[]{:S(2)}, u32[]{:S(2)}) collective-permute-start(bf16[288,768]{1,0:T(8,128)(2,1)S(1)} %constant_dynamic-update-slice_fusion.3.r0), channel_id=1, source_target_pairs={{0,32},{32,64},{64,96},{96,0},{1,33},{33,65},{65,97},{97,1},{2,34}... | collective-permute-start | bytes 1327112 | tf_op jit(solution)/shard_map/ppermute | solution.py:28
  67.8 71.8 %collective-permute-start.21 = (bf16[3,3072,384]{2,1,0:T(8,128)(2,1)}, bf16[3,3072,384]{2,1,0:T(8,128)(2,1)}, u32[]{:S(2)}, u32[]{:S(2)}) collective-permute-start(bf16[3,3072,384]{2,1,0:T(8,128)(2,1)} %bitcast.7.own_hbm), channel_id=1, source_target_pairs={{0,128},{128,0},{1,129},{129,1},{2,130},{130,2},{3,131},{131,3},{4... | collective-permute-start | bytes 21233672 | tf_op jit(solution)/shard_map/ppermute | solution.py:28
  69.1 10.9 %collective-permute-start.11 = (bf16[256,768]{1,0:T(8,128)(2,1)S(1)}, bf16[256,768]{1,0:T(8,128)(2,1)S(1)}, u32[]{:S(2)}, u32[]{:S(2)}) collective-permute-start(bf16[256,768]{1,0:T(8,128)(2,1)S(1)} %get-tuple-element.44.hidden_ref), channel_id=1, source_target_pairs={{0,128},{128,0},{1,129},{129,1},{2,130},{130,2},{3,131},{131,3},{4... | collective-permute-start | bytes 1179656 | tf_op jit(solution)/shard_map/ppermute | solution.py:28
  82.5 11.8 %collective-permute-start.19 = (bf16[3,256,384]{2,1,0:T(8,128)(2,1)S(1)}, bf16[3,256,384]{2,1,0:T(8,128)(2,1)S(1)}, u32[]{:S(2)}, u32[]{:S(2)}) collective-permute-start(bf16[3,256,384]{2,1,0:T(8,128)(2,1)S(1)} %get-tuple-element.46), channel_id=1, source_target_pairs={{0,128},{128,0},{1,129},{129,1},{2,130},{130,2},{3,131},{131,3},{4... | collective-permute-start | bytes 1769480 | tf_op jit(solution)/shard_map/ppermute | solution.py:28
  99.9 28.3 %all-to-all-start = ((bf16[8,256,384]{2,1,0:T(8,128)(2,1)}), bf16[8,256,384]{2,1,0:T(8,128)(2,1)S(1)}, u32[]{:S(2)}, u32[]{:S(2)}) async-start(bf16[8,256,384]{2,1,0:T(8,128)(2,1)} %bitcast_dynamic-update-slice_fusion), calls=%async_computation | async-start | bytes 3145728 | tf_op jit(solution)/shard_map/all_to_all | solution.py:74
  131.0 24.3 %all-to-all-start.1 = ((bf16[8,256,384]{2,1,0:T(8,128)(2,1)}), bf16[8,256,384]{2,1,0:T(8,128)(2,1)S(1)}, u32[]{:S(2)}, u32[]{:S(2)}) async-start(bf16[8,256,384]{2,1,0:T(8,128)(2,1)} %copy-done.1), calls=%async_computation.1 | async-start | bytes 3145728 | tf_op jit(solution)/shard_map/all_to_all | solution.py:74
  196.2 23.9 %all-to-all-start.3 = ((bf16[8,256,384]{2,1,0:T(8,128)(2,1)}), bf16[8,256,384]{2,1,0:T(8,128)(2,1)S(1)}, u32[]{:S(2)}, u32[]{:S(2)}) async-start(bf16[8,256,384]{2,1,0:T(8,128)(2,1)} %copy-done.2), calls=%async_computation.3 | async-start | bytes 3145728 | tf_op jit(solution)/shard_map/all_to_all | solution.py:74
  231.2 10.9 %collective-permute-start.33 = (bf16[192,768]{1,0:T(8,128)(2,1)S(1)}, bf16[192,768]{1,0:T(8,128)(2,1)S(1)}, u32[]{:S(2)}, u32[]{:S(2)}) collective-permute-start(bf16[192,768]{1,0:T(8,128)(2,1)S(1)} %get-tuple-element.68), channel_id=1, source_target_pairs={{0,32},{32,64},{64,96},{96,0},{1,33},{33,65},{65,97},{97,1},{2,34}... | collective-permute-start | bytes 884744 | tf_op jit(solution)/shard_map/ppermute | solution.py:28
  231.3 10.8 %collective-permute-start.34 = (bf16[192,768]{1,0:T(8,128)(2,1)S(1)}, bf16[192,768]{1,0:T(8,128)(2,1)S(1)}, u32[]{:S(2)}, u32[]{:S(2)}) collective-permute-start(bf16[192,768]{1,0:T(8,128)(2,1)S(1)} %get-tuple-element.69), channel_id=1, source_target_pairs={{0,96},{32,0},{64,32},{96,64},{1,97},{33,1},{65,33},{97,65},{2,98}... | collective-permute-start | bytes 884744 | tf_op jit(solution)/shard_map/ppermute | solution.py:28
  236.6 11.8 %collective-permute-start.26 = (bf16[192,768]{1,0:T(8,128)(2,1)S(1)}, bf16[192,768]{1,0:T(8,128)(2,1)S(1)}, u32[]{:S(2)}, u32[]{:S(2)}) collective-permute-start(bf16[192,768]{1,0:T(8,128)(2,1)S(1)} %get-tuple-element.59), channel_id=1, source_target_pairs={{0,32},{32,64},{64,96},{96,0},{1,33},{33,65},{65,97},{97,1},{2,34}... | collective-permute-start | bytes 884744 | tf_op jit(solution)/shard_map/ppermute | solution.py:28
  236.7 11.7 %collective-permute-start.27 = (bf16[192,768]{1,0:T(8,128)(2,1)S(1)}, bf16[192,768]{1,0:T(8,128)(2,1)S(1)}, u32[]{:S(2)}, u32[]{:S(2)}) collective-permute-start(bf16[192,768]{1,0:T(8,128)(2,1)S(1)} %get-tuple-element.60), channel_id=1, source_target_pairs={{0,96},{32,0},{64,32},{96,64},{1,97},{33,1},{65,33},{97,65},{2,98}... | collective-permute-start | bytes 884744 | tf_op jit(solution)/shard_map/ppermute | solution.py:28
  242.3 18.8 %collective-permute-start.35 = (bf16[384,768]{1,0:T(8,128)(2,1)S(1)}, bf16[384,768]{1,0:T(8,128)(2,1)S(1)}, u32[]{:S(2)}, u32[]{:S(2)}) collective-permute-start(bf16[384,768]{1,0:T(8,128)(2,1)S(1)} %get-tuple-element.70), channel_id=1, source_target_pairs={{0,32},{32,64},{64,96},{96,0},{1,33},{33,65},{65,97},{97,1},{2,34}... | collective-permute-start | bytes 1769480 | tf_op jit(solution)/shard_map/ppermute | solution.py:28
  245.0 17.4 %collective-permute-start.36 = (bf16[384,768]{1,0:T(8,128)(2,1)S(1)}, bf16[384,768]{1,0:T(8,128)(2,1)S(1)}, u32[]{:S(2)}, u32[]{:S(2)}) collective-permute-start(bf16[384,768]{1,0:T(8,128)(2,1)S(1)} %get-tuple-element.71), channel_id=1, source_target_pairs={{0,96},{32,0},{64,32},{96,64},{1,97},{33,1},{65,33},{97,65},{2,98}... | collective-permute-start | bytes 1769480 | tf_op jit(solution)/shard_map/ppermute | solution.py:28
  248.6 24.8 %collective-permute-start.28 = (bf16[384,768]{1,0:T(8,128)(2,1)S(1)}, bf16[384,768]{1,0:T(8,128)(2,1)S(1)}, u32[]{:S(2)}, u32[]{:S(2)}) collective-permute-start(bf16[384,768]{1,0:T(8,128)(2,1)S(1)} %get-tuple-element.61), channel_id=1, source_target_pairs={{0,32},{32,64},{64,96},{96,0},{1,33},{33,65},{65,97},{97,1},{2,34}... | collective-permute-start | bytes 1769480 | tf_op jit(solution)/shard_map/ppermute | solution.py:28
  251.3 22.1 %collective-permute-start.29 = (bf16[384,768]{1,0:T(8,128)(2,1)S(1)}, bf16[384,768]{1,0:T(8,128)(2,1)S(1)}, u32[]{:S(2)}, u32[]{:S(2)}) collective-permute-start(bf16[384,768]{1,0:T(8,128)(2,1)S(1)} %get-tuple-element.62), channel_id=1, source_target_pairs={{0,96},{32,0},{64,32},{96,64},{1,97},{33,1},{65,33},{97,65},{2,98}... | collective-permute-start | bytes 1769480 | tf_op jit(solution)/shard_map/ppermute | solution.py:28
  262.8 15.2 %collective-permute-start.37 = (bf16[96,768]{1,0:T(8,128)(2,1)S(1)}, bf16[96,768]{1,0:T(8,128)(2,1)S(1)}, u32[]{:S(2)}, u32[]{:S(2)}) collective-permute-start(bf16[96,768]{1,0:T(8,128)(2,1)S(1)} %get-tuple-element.73), channel_id=1, source_target_pairs={{0,8},{8,16},{16,24},{24,0},{1,9},{9,17},{17,25},{25,1},{2,10},{10... | collective-permute-start | bytes 442376 | tf_op jit(solution)/shard_map/ppermute | solution.py:28
  264.2 18.2 %collective-permute-start.38 = (bf16[96,768]{1,0:T(8,128)(2,1)S(1)}, bf16[96,768]{1,0:T(8,128)(2,1)S(1)}, u32[]{:S(2)}, u32[]{:S(2)}) collective-permute-start(bf16[96,768]{1,0:T(8,128)(2,1)S(1)} %get-tuple-element.74), channel_id=1, source_target_pairs={{0,24},{8,0},{16,8},{24,16},{1,25},{9,1},{17,9},{25,17},{2,26},{10... | collective-permute-start | bytes 442376 | tf_op jit(solution)/shard_map/ppermute | solution.py:28
  267.0 15.4 %collective-permute-start.39 = (bf16[96,768]{1,0:T(8,128)(2,1)S(1)}, bf16[96,768]{1,0:T(8,128)(2,1)S(1)}, u32[]{:S(2)}, u32[]{:S(2)}) collective-permute-start(bf16[96,768]{1,0:T(8,128)(2,1)S(1)} %get-tuple-element.75), channel_id=1, source_target_pairs={{0,16},{8,24},{16,0},{24,8},{1,17},{9,25},{17,1},{25,9},{2,18},{10... | collective-permute-start | bytes 442376 | tf_op jit(solution)/shard_map/ppermute | solution.py:28
  275.2 17.2 %collective-permute-start.31 = (bf16[96,768]{1,0:T(8,128)(2,1)S(1)}, bf16[96,768]{1,0:T(8,128)(2,1)S(1)}, u32[]{:S(2)}, u32[]{:S(2)}) collective-permute-start(bf16[96,768]{1,0:T(8,128)(2,1)S(1)} %get-tuple-element.65), channel_id=1, source_target_pairs={{0,24},{8,0},{16,8},{24,16},{1,25},{9,1},{17,9},{25,17},{2,26},{10... | collective-permute-start | bytes 442376 | tf_op jit(solution)/shard_map/ppermute | solution.py:28
  278.0 15.8 %collective-permute-start.32 = (bf16[96,768]{1,0:T(8,128)(2,1)S(1)}, bf16[96,768]{1,0:T(8,128)(2,1)S(1)}, u32[]{:S(2)}, u32[]{:S(2)}) collective-permute-start(bf16[96,768]{1,0:T(8,128)(2,1)S(1)} %get-tuple-element.66), channel_id=1, source_target_pairs={{0,16},{8,24},{16,0},{24,8},{1,17},{9,25},{17,1},{25,9},{2,18},{10... | collective-permute-start | bytes 442376 | tf_op jit(solution)/shard_map/ppermute | solution.py:28
  (27 other events, 162.9 us)

commit v3 on v2

--- a/solution.py
+++ b/solution.py
@@ -1,3 +1,5 @@
+import functools
+
 import jax
 import jax.numpy as jnp
 from jax import lax
@@ -56,7 +58,7 @@
     return wide(parts[0]) + sum(wide(hop(parts[k], axis, k)) for k in (1, 3, 2))
 
 
-def ring_scatter(grads, far_top, far_bottom, shift, axis):
+def ring_scatter(grads, far_top, far_bottom, at, axis, turned):
     for_right = hop(far_top, axis, 1)
     for_left = hop(far_bottom, axis, -1)
     part = array(BLOCK, FF_LOCAL)
@@ -66,8 +68,12 @@
     from_left = hop(right, axis, 1)
     from_right = hop(left, axis, -1)
     return local_call(
-        sum_kernel, [SMEM] + [VMEM] * 3, (array(SHARD, FF_LOCAL),) * 4, 500_000, 3_000_000
-    )(shift[None], grads, from_left, from_right)
+        functools.partial(sum_kernel, turned=turned),
+        [SMEM] + [VMEM] * 3,
+        (array(SHARD, FF_LOCAL),) * 4,
+        500_000,
+        3_000_000,
+    )(at, grads, from_left, from_right)
 
 
 def exchange(parts):
@@ -182,9 +188,10 @@
     lax.fori_loop(0, half // 16, tile, 0)
 
 
-def sum_kernel(shift_ref, grads_ref, from_left, from_right, *shards):
+def sum_kernel(at_ref, grads_ref, from_left, from_right, *shards, turned):
+    first = at_ref[2] if turned else 0
     for dz, shard in enumerate(shards):
-        base = ((shift_ref[0] + dz) & 3) * SHARD
+        base = ((first + dz) & 3) * SHARD
 
         def tile(i, _):
             rows = pl.ds(pl.multiple_of(base + i * 16, 16), 16)
@@ -217,11 +224,8 @@
     lax.fori_loop(0, 3, block, 0)
 
 
-def down_far_kernel(
-    at_ref, hidden_ref, crossed_ref, own_far, far_top, far_bottom, here_ref, arrived_ref,
-    down_ref, parts_ref, away_ref,
-):
-    group, x, zh = at_ref[0], at_ref[1], at_ref[2]
+def down_far_kernel(at_ref, crossed_ref, own_far, far_top, far_bottom, down_ref, away_ref):
+    zh = at_ref[2]
     half = SHARD // 2
     for dz, pieces in enumerate(
         (
@@ -235,6 +239,10 @@
         for k, piece in enumerate(pieces):
             down_ref[pl.ds(pl.multiple_of(base + k * half, 16), half), :] = piece
     away_ref[...] = narrow(dot(crossed_ref[...], down_ref[...], 1, 1))
+
+
+def parts_kernel(at_ref, hidden_ref, down_ref, here_ref, arrived_ref, parts_ref):
+    group, x = at_ref[0], at_ref[1]
     parts_ref[group * 4 + ((x + 2) & 3)] = narrow(dot(hidden_ref[...], down_ref[...], 1, 1))
     for i, dx in enumerate(EARLY):
         parts_ref[group * 4 + ((x + dx) & 3)] = here_ref[i]
@@ -461,15 +469,19 @@
         *(down_rest[k] for k in (0, 1, 4)),
     )
     eight_kind = array(8, SEQ, BLOCK)
-    down_far, parts, part_away = local_call(
+    down_far, part_away = local_call(
         down_far_kernel,
-        [SMEM] + [VMEM] * 7,
-        (array(BLOCK, FF_LOCAL), eight_kind, array(SEQ, BLOCK)),
-        300_000_000,
-        4_000_000,
-    )(at, hidden, hidden_crossed, up_rest[3], down_rest[2], down_rest[3], parts_here, swap(parts_away))
+        [SMEM] + [VMEM] * 4,
+        (array(BLOCK, FF_LOCAL), array(SEQ, BLOCK)),
+        150_000_000,
+        2_000_000,
+    )(at, hidden_crossed, up_rest[3], down_rest[2], down_rest[3])
+    part_arrived = swap(part_away)
+    parts = local_call(
+        parts_kernel, [SMEM] + [VMEM] * 4, eight_kind, 150_000_000, 4_000_000
+    )(at, hidden, down_far, parts_here, swap(parts_away))
     parts = lax.dynamic_update_index_in_dim(
-        parts, swap(part_away), (1 - group) * 4 + ((x + 2) & 3), 0
+        parts, part_arrived, (1 - group) * 4 + ((x + 2) & 3), 0
     )
 
     local = lax.iota(jnp.int32, BLOCK) + (y * 2 + zl) * BLOCK
@@ -510,7 +522,7 @@
     down_grads = local_call(down_grad_kernel, [SMEM] + [VMEM] * 4, grad_kinds, matmul, 5_000_000)(
         at, gap_all, gap_crossed, hidden, hidden_crossed
     )
-    down_shards = ring_scatter(*down_grads, zh, "x")
+    down_shards = ring_scatter(*down_grads, at, "x", True)
     grad_down = narrow(direct_scatter(down_shards, "zh")).T
 
     here, away = local_call(
@@ -522,7 +534,7 @@
     up_grads = local_call(up_grad_kernel, [VMEM] * 4, grad_kinds, matmul, 5_000_000)(
         normed, normed_crossed, change, swap(change)
     )
-    up_shards = ring_scatter(*up_grads, jnp.int32(0), "x")
+    up_shards = ring_scatter(*up_grads, at, "x", False)
     grad_up = narrow(direct_scatter(up_shards, "zh"))
     return (latent[None], gap[None], grad_up, grad_down)
 

time: 297 us -> 300 us (1.010)
  starting transfers between devices: 78 us -> 74.9 us
    ppermute x40, starting transfers between devices: 64.2 us -> 60.6 us  [hop(): return lax.ppermute(value, axis, [(i, (i + step) % n) for i in range(n)])]
    unnamed x36 -> x30, local copies, waits for them, and re-layouts: 5.82 us -> 7.81 us
  transfers between devices with their start and end apart: 43 -> 43, of which waited for: 27 -> 30; matrix products, arithmetic and copies ran while one was open for 1% -> 1% of each run, Pallas kernels for 6% -> 6%
where the time goes in v3:
time: 300 us; the launch traced here: 296 us
  waiting for transfers between devices  145 us (48%)
  starting transfers between devices  74.9 us (25%)
  Pallas kernels  38.4 us (13%)
  blocking collectives  24.2 us (8%)
  local copies, waits for them, and re-layouts  8.69 us (3%)
    ppermute x40, waiting for transfers between devices, hop(): return lax.ppermute(value, axis, [(i, (i + step) % n) for i in range(n)])  87.2 us
    ppermute x40, starting transfers between devices, hop(): return lax.ppermute(value, axis, [(i, (i + step) % n) for i in range(n)])  60.6 us
    all_to_all x3, waiting for transfers between devices, exchange(): return lax.all_to_all(parts, MODEL, 0, 0, tiled=True)  57.8 us
    all_to_all x1, blocking collectives, exchange(): return lax.all_to_all(parts, MODEL, 0, 0, tiled=True)  24.2 us
    all_to_all x3, starting transfers between devices, exchange(): return lax.all_to_all(parts, MODEL, 0, 0, tiled=True)  14.2 us
    pallas_call x1, Pallas kernels, step(): local_call(score_kernel, [SMEM, VMEM] + [HBM] * 4, array(8, SEQ, BLOCK),...  12.8 us
    unnamed x30, local copies, waits for them, and re-layouts  7.81 us
  transfers between devices with their start and end apart: 43, of which 30 were waited for; matrix products, arithmetic and copies ran while one was open for 1% of the time, Pallas kernels for 6%

profile of v3, /device:TPU:2, one launch (start us, length us, event | category | flops | bytes accessed | tf_op | source)
XLA Modules:
  0.0 296.2 jit_solution(1243337096974767148)
XLA Ops:
  0.6 6.4 %collective-permute-start.3 = (bf16[96,768]{1,0:T(8,128)(2,1)}, bf16[96,768]{1,0:T(8,128)(2,1)S(1)}, u32[]{:S(2)}, u32[]{:S(2)}) collective-permute-start(bf16[96,768]{1,0:T(8,128)(2,1)} %param.8), channel_id=1, source_target_pairs={{0,24},{8,0},{16,8},{24,16},{1,25},{9,1},{17,9},{25,17},{2,26},{10... | collective-permute-start | bytes 442376 | tf_op jit(solution)/shard_map/ppermute | solution.py:30
  7.0 3.8 %collective-permute-start.4 = (bf16[96,768]{1,0:T(8,128)(2,1)}, bf16[96,768]{1,0:T(8,128)(2,1)S(1)}, u32[]{:S(2)}, u32[]{:S(2)}) collective-permute-start(bf16[96,768]{1,0:T(8,128)(2,1)} %param.8), channel_id=1, source_target_pairs={{0,16},{8,24},{16,0},{24,8},{1,17},{9,25},{17,1},{25,9},{2,18},{10... | collective-permute-start | bytes 442376 | tf_op jit(solution)/shard_map/ppermute | solution.py:30
  13.9 4.9 %collective-permute-done.3 = bf16[96,768]{1,0:T(8,128)(2,1)S(1)} collective-permute-done((bf16[96,768]{1,0:T(8,128)(2,1)}, bf16[96,768]{1,0:T(8,128)(2,1)S(1)}, u32[]{:S(2)}, u32[]{:S(2)}) %collective-permute-start.3) | collective-permute-done | bytes 147488 | tf_op jit(solution)/shard_map/ppermute | solution.py:30
  24.3 3.5 %shard_map.93 = (bf16[256,1536]{1,0:T(8,128)(2,1)S(1)}, bf16[256,1536]{1,0:T(8,128)(2,1)S(1)}) custom-call(s32[1]{0:T(128)S(6)} %copy.15.seed_ref.ids_ref, s32[1,3072]{1,0:T(1,128)S(1)} %fusion.2.feature_ref), custom_call_target="tpu_custom_call" | custom-call | flops 30000000 | bytes 1600000 | tf_op jit(solution)/shard_map/pallas_call | solution.py:446
  28.0 3.1 %collective-permute-done.7.r3 = bf16[288,768]{1,0:T(8,128)(2,1)S(1)} collective-permute-done((bf16[288,768]{1,0:T(8,128)(2,1)S(1)}, bf16[288,768]{1,0:T(8,128)(2,1)S(1)}, u32[]{:S(2)}, u32[]{:S(2)}) %collective-permute-start.7) | collective-permute-done | bytes 442400 | tf_op jit(solution)/shard_map/ppermute | solution.py:30
  33.3 5.8 %collective-permute-done.8.far_top = bf16[240,768]{1,0:T(8,128)(2,1)S(1)} collective-permute-done((bf16[240,768]{1,0:T(8,128)(2,1)S(1)}, bf16[240,768]{1,0:T(8,128)(2,1)S(1)}, u32[]{:S(2)}, u32[]{:S(2)}) %collective-permute-start.8) | collective-permute-done | bytes 368672 | tf_op jit(solution)/shard_map/ppermute | solution.py:30
  42.7 8.1 %collective-permute-start.12 = (bf16[96,768]{1,0:T(8,128)(2,1)S(1)}, bf16[96,768]{1,0:T(8,128)(2,1)S(1)}, u32[]{:S(2)}, u32[]{:S(2)}) collective-permute-start(bf16[96,768]{1,0:T(8,128)(2,1)S(1)} %bitcast.16), channel_id=1, source_target_pairs={{0,24},{8,0},{16,8},{24,16},{1,25},{9,1},{17,9},{25,17},{2,26},{10... | collective-permute-start | bytes 442376 | tf_op jit(solution)/shard_map/ppermute | solution.py:30
  53.3 3.3 %collective-permute-done.12 = bf16[96,768]{1,0:T(8,128)(2,1)S(1)} collective-permute-done((bf16[96,768]{1,0:T(8,128)(2,1)S(1)}, bf16[96,768]{1,0:T(8,128)(2,1)S(1)}, u32[]{:S(2)}, u32[]{:S(2)}) %collective-permute-start.12) | collective-permute-done | bytes 147488 | tf_op jit(solution)/shard_map/ppermute | solution.py:30
  56.6 8.0 %collective-permute-done.13 = bf16[96,768]{1,0:T(8,128)(2,1)S(1)} collective-permute-done((bf16[96,768]{1,0:T(8,128)(2,1)S(1)}, bf16[96,768]{1,0:T(8,128)(2,1)S(1)}, u32[]{:S(2)}, u32[]{:S(2)}) %collective-permute-start.13) | collective-permute-done | bytes 147488 | tf_op jit(solution)/shard_map/ppermute | solution.py:30
  68.4 9.0 %collective-permute-done.17.r1 = bf16[288,768]{1,0:T(8,128)(2,1)S(1)} collective-permute-done((bf16[288,768]{1,0:T(8,128)(2,1)S(1)}, bf16[288,768]{1,0:T(8,128)(2,1)S(1)}, u32[]{:S(2)}, u32[]{:S(2)}) %collective-permute-start.17) | collective-permute-done | bytes 442400 | tf_op jit(solution)/shard_map/ppermute | solution.py:30
  77.4 2.7 collective-permute-done.15.r3
  80.1 3.2 %shard_map.97 = (bf16[3,384,768]{2,1,0:T(8,128)(2,1)S(1)}, bf16[3,256,384]{2,1,0:T(8,128)(2,1)S(1)}, bf16[3,256,384]{2,1,0:T(8,128)(2,1)}) custom-call(s32[3]{0:T(128)S(1)} %pad_add_fusion.at_ref, bf16[256,768]{1,0:T(8,128)(2,1)S(1)} %get-tuple-element.43.hidden_ref, bf16[256,768]{1,0:T(8,128)(2,1)S(1)} %collective-permute-done.11.crossed_ref.hidden_crossed_ref, ...), custom_call_target="tpu_custom_call" | custom-call | flops 900000000 | bytes 6000000 | tf_op jit(solution)/shard_map/pallas_call | solution.py:458
  84.5 3.0 %collective-permute-start.18 = (bf16[144,768]{1,0:T(8,128)(2,1)S(1)}, bf16[144,768]{1,0:T(8,128)(2,1)S(1)}, u32[]{:S(2)}, u32[]{:S(2)}) collective-permute-start(bf16[144,768]{1,0:T(8,128)(2,1)S(1)} %slice.29), channel_id=1, source_target_pairs={{0,96},{32,0},{64,32},{96,64},{1,97},{33,1},{65,33},{97,65},{2,98}... | collective-permute-start | bytes 663560 | tf_op jit(solution)/shard_map/ppermute | solution.py:30
  87.7 5.2 %collective-permute-done.18.far_bottom = bf16[144,768]{1,0:T(8,128)(2,1)S(1)} collective-permute-done((bf16[144,768]{1,0:T(8,128)(2,1)S(1)}, bf16[144,768]{1,0:T(8,128)(2,1)S(1)}, u32[]{:S(2)}, u32[]{:S(2)}) %collective-permute-start.18) | collective-permute-done | bytes 221216 | tf_op jit(solution)/shard_map/ppermute | solution.py:30
  100.3 7.1 %all-to-all-start = ((bf16[8,256,384]{2,1,0:T(8,128)(2,1)}), bf16[8,256,384]{2,1,0:T(8,128)(2,1)S(1)}, u32[]{:S(2)}, u32[]{:S(2)}) async-start(bf16[8,256,384]{2,1,0:T(8,128)(2,1)} %bitcast_dynamic-update-slice_fusion), calls=%async_computation | async-start | bytes 3145728 | tf_op jit(solution)/shard_map/all_to_all | solution.py:80
  108.1 21.4 %all-to-all-done.parts_ref = bf16[8,256,384]{2,1,0:T(8,128)(2,1)S(1)} async-done(((bf16[8,256,384]{2,1,0:T(8,128)(2,1)}), bf16[8,256,384]{2,1,0:T(8,128)(2,1)S(1)}, u32[]{:S(2)}, u32[]{:S(2)}) %all-to-all-start) | async-done | bytes 1572896 | tf_op jit(solution)/shard_map/all_to_all | solution.py:80
  132.3 3.6 %all-to-all-start.1 = ((bf16[8,256,384]{2,1,0:T(8,128)(2,1)}), bf16[8,256,384]{2,1,0:T(8,128)(2,1)S(1)}, u32[]{:S(2)}, u32[]{:S(2)}) async-start(bf16[8,256,384]{2,1,0:T(8,128)(2,1)} %copy-done.3), calls=%async_computation.1 | async-start | bytes 3145728 | tf_op jit(solution)/shard_map/all_to_all | solution.py:80
  136.0 4.9 %collective-permute-done.22.out_other_hbm = bf16[384,3072]{1,0:T(8,128)(2,1)} collective-permute-done((bf16[384,3072]{1,0:T(8,128)(2,1)}, bf16[384,3072]{1,0:T(8,128)(2,1)}, u32[]{:S(2)}, u32[]{:S(2)}) %collective-permute-start.22) | collective-permute-done | bytes 2359328 | tf_op jit(solution)/shard_map/ppermute | solution.py:30
  140.9 16.1 %all-to-all-done.1.noisy_ref = bf16[8,256,384]{2,1,0:T(8,128)(2,1)S(1)} async-done(((bf16[8,256,384]{2,1,0:T(8,128)(2,1)}), bf16[8,256,384]{2,1,0:T(8,128)(2,1)S(1)}, u32[]{:S(2)}, u32[]{:S(2)}) %all-to-all-start.1) | async-done | bytes 1572896 | tf_op jit(solution)/shard_map/all_to_all | solution.py:80
  158.7 12.8 %shard_map.100 = bf16[8,256,384]{2,1,0:T(8,128)(2,1)S(1)} custom-call(f32[1]{0:T(128)} %bitcast.6.sign_ref, bf16[8,256,384]{2,1,0:T(8,128)(2,1)S(1)} %all-to-all-done.1.noisy_ref, bf16[3,3072,384]{2,1,0:T(8,128)(2,1)} %bitcast.7.own_hbm, bf16[3,3072,384]{2,1,0:T(8,128)(2,1)} %collective-permute-done.21.other_hbm, bf16[384,3072]{1,0:T(8,128)(2,1)S(1)} %bitcast.14, ...), custom_call_target="tpu_custom_call" | custom-call | flops 5000000000 | bytes 20000000 | tf_op jit(solution)/shard_map/pallas_call | solution.py:499
  171.5 24.2 %all_to_all.20.parts_ref = bf16[8,256,384]{2,1,0:T(8,128)(2,1)S(1)} all-to-all(bf16[8,256,384]{2,1,0:T(8,128)(2,1)S(1)} %shard_map.100), channel_id=1, replica_groups=mesh['group'=2,'x'=4,'zh'=4,'y'=4,'zl'=2] {'y','zl'}, dimensions={0} | all-to-all | bytes 3145728 | tf_op jit(solution)/shard_map/all_to_all | solution.py:80
  197.9 3.6 %all-to-all-start.3 = ((bf16[8,256,384]{2,1,0:T(8,128)(2,1)}), bf16[8,256,384]{2,1,0:T(8,128)(2,1)S(1)}, u32[]{:S(2)}, u32[]{:S(2)}) async-start(bf16[8,256,384]{2,1,0:T(8,128)(2,1)} %copy-done.4), calls=%async_computation.3 | async-start | bytes 3145728 | tf_op jit(solution)/shard_map/all_to_all | solution.py:80
  201.5 20.3 %all-to-all-done.3.gap_ref = bf16[8,256,384]{2,1,0:T(8,128)(2,1)S(1)} async-done(((bf16[8,256,384]{2,1,0:T(8,128)(2,1)}), bf16[8,256,384]{2,1,0:T(8,128)(2,1)S(1)}, u32[]{:S(2)}, u32[]{:S(2)}) %all-to-all-start.3) | async-done | bytes 1572896 | tf_op jit(solution)/shard_map/all_to_all | solution.py:80
  225.7 2.7 shard_map.102
  241.4 2.9 collective-permute-done.33.for_right
  247.4 3.3 %collective-permute-done.26.for_right = bf16[192,768]{1,0:T(8,128)(2,1)S(1)} collective-permute-done((bf16[192,768]{1,0:T(8,128)(2,1)S(1)}, bf16[192,768]{1,0:T(8,128)(2,1)S(1)}, u32[]{:S(2)}, u32[]{:S(2)}) %collective-permute-start.26) | collective-permute-done | bytes 294944 | tf_op jit(solution)/shard_map/ppermute | solution.py:30
  253.7 9.6 %collective-permute-done.35.from_left = bf16[384,768]{1,0:T(8,128)(2,1)S(1)} collective-permute-done((bf16[384,768]{1,0:T(8,128)(2,1)S(1)}, bf16[384,768]{1,0:T(8,128)(2,1)S(1)}, u32[]{:S(2)}, u32[]{:S(2)}) %collective-permute-start.35) | collective-permute-done | bytes 589856 | tf_op jit(solution)/shard_map/ppermute | solution.py:30
  265.4 3.9 %collective-permute-start.38 = (bf16[96,768]{1,0:T(8,128)(2,1)S(1)}, bf16[96,768]{1,0:T(8,128)(2,1)S(1)}, u32[]{:S(2)}, u32[]{:S(2)}) collective-permute-start(bf16[96,768]{1,0:T(8,128)(2,1)S(1)} %get-tuple-element.72), channel_id=1, source_target_pairs={{0,24},{8,0},{16,8},{24,16},{1,25},{9,1},{17,9},{25,17},{2,26},{10... | collective-permute-start | bytes 442376 | tf_op jit(solution)/shard_map/ppermute | solution.py:30
  269.2 4.4 %collective-permute-start.39 = (bf16[96,768]{1,0:T(8,128)(2,1)S(1)}, bf16[96,768]{1,0:T(8,128)(2,1)S(1)}, u32[]{:S(2)}, u32[]{:S(2)}) collective-permute-start(bf16[96,768]{1,0:T(8,128)(2,1)S(1)} %get-tuple-element.73), channel_id=1, source_target_pairs={{0,16},{8,24},{16,0},{24,8},{1,17},{9,25},{17,1},{25,9},{2,18},{10... | collective-permute-start | bytes 442376 | tf_op jit(solution)/shard_map/ppermute | solution.py:30
  276.9 3.9 %collective-permute-start.31 = (bf16[96,768]{1,0:T(8,128)(2,1)S(1)}, bf16[96,768]{1,0:T(8,128)(2,1)S(1)}, u32[]{:S(2)}, u32[]{:S(2)}) collective-permute-start(bf16[96,768]{1,0:T(8,128)(2,1)S(1)} %get-tuple-element.63), channel_id=1, source_target_pairs={{0,24},{8,0},{16,8},{24,16},{1,25},{9,1},{17,9},{25,17},{2,26},{10... | collective-permute-start | bytes 442376 | tf_op jit(solution)/shard_map/ppermute | solution.py:30
  280.8 4.4 %collective-permute-start.32 = (bf16[96,768]{1,0:T(8,128)(2,1)S(1)}, bf16[96,768]{1,0:T(8,128)(2,1)S(1)}, u32[]{:S(2)}, u32[]{:S(2)}) collective-permute-start(bf16[96,768]{1,0:T(8,128)(2,1)S(1)} %get-tuple-element.64), channel_id=1, source_target_pairs={{0,16},{8,24},{16,0},{24,8},{1,17},{9,25},{17,1},{25,9},{2,18},{10... | collective-permute-start | bytes 442376 | tf_op jit(solution)/shard_map/ppermute | solution.py:30
  286.6 6.9 %collective-permute-done.31 = bf16[96,768]{1,0:T(8,128)(2,1)S(1)} collective-permute-done((bf16[96,768]{1,0:T(8,128)(2,1)S(1)}, bf16[96,768]{1,0:T(8,128)(2,1)S(1)}, u32[]{:S(2)}, u32[]{:S(2)}) %collective-permute-start.31) | collective-permute-done | bytes 147488 | tf_op jit(solution)/shard_map/ppermute | solution.py:30
  (120 shorter events, 68.1 us)
Async XLA Ops:
  0.6 18.2 %collective-permute-start.3 = (bf16[96,768]{1,0:T(8,128)(2,1)}, bf16[96,768]{1,0:T(8,128)(2,1)S(1)}, u32[]{:S(2)}, u32[]{:S(2)}) collective-permute-start(bf16[96,768]{1,0:T(8,128)(2,1)} %param.8), channel_id=1, source_target_pairs={{0,24},{8,0},{16,8},{24,16},{1,25},{9,1},{17,9},{25,17},{2,26},{10... | collective-permute-start | bytes 442376 | tf_op jit(solution)/shard_map/ppermute | solution.py:30
  7.0 14.4 %collective-permute-start.5 = (bf16[96,768]{1,0:T(8,128)(2,1)}, bf16[96,768]{1,0:T(8,128)(2,1)S(1)}, u32[]{:S(2)}, u32[]{:S(2)}) collective-permute-start(bf16[96,768]{1,0:T(8,128)(2,1)} %param.8), channel_id=1, source_target_pairs={{0,8},{8,16},{16,24},{24,0},{1,9},{9,17},{17,25},{25,1},{2,10},{10... | collective-permute-start | bytes 442376 | tf_op jit(solution)/shard_map/ppermute | solution.py:30
  7.0 12.9 %collective-permute-start.4 = (bf16[96,768]{1,0:T(8,128)(2,1)}, bf16[96,768]{1,0:T(8,128)(2,1)S(1)}, u32[]{:S(2)}, u32[]{:S(2)}) collective-permute-start(bf16[96,768]{1,0:T(8,128)(2,1)} %param.8), channel_id=1, source_target_pairs={{0,16},{8,24},{16,0},{24,8},{1,17},{9,25},{17,1},{25,9},{2,18},{10... | collective-permute-start | bytes 442376 | tf_op jit(solution)/shard_map/ppermute | solution.py:30
  11.8 16.1 %collective-permute-start.2 = (bf16[192,768]{1,0:T(8,128)(2,1)S(1)}, bf16[192,768]{1,0:T(8,128)(2,1)S(1)}, u32[]{:S(2)}, u32[]{:S(2)}) collective-permute-start(bf16[192,768]{1,0:T(8,128)(2,1)S(1)} %pad_maximum_fusion.2.n0), channel_id=1, source_target_pairs={{0,32},{32,64},{64,96},{96,0},{1,33},{33,65},{65,97},{97,1},{2,34}... | collective-permute-start | bytes 884744 | tf_op jit(solution)/shard_map/ppermute | solution.py:30
  13.4 14.5 %collective-permute-start.1 = (bf16[192,768]{1,0:T(8,128)(2,1)S(1)}, bf16[192,768]{1,0:T(8,128)(2,1)S(1)}, u32[]{:S(2)}, u32[]{:S(2)}) collective-permute-start(bf16[192,768]{1,0:T(8,128)(2,1)S(1)} %pad_maximum_fusion.2.n0), channel_id=1, source_target_pairs={{0,96},{32,0},{64,32},{96,64},{1,97},{33,1},{65,33},{97,65},{2,98}... | collective-permute-start | bytes 884744 | tf_op jit(solution)/shard_map/ppermute | solution.py:30
  23.0 9.6 %collective-permute-start.6 = (bf16[288,768]{1,0:T(8,128)(2,1)S(1)}, bf16[288,768]{1,0:T(8,128)(2,1)S(1)}, u32[]{:S(2)}, u32[]{:S(2)}) collective-permute-start(bf16[288,768]{1,0:T(8,128)(2,1)S(1)} %constant_dynamic-update-slice_fusion.r0), channel_id=1, source_target_pairs={{0,96},{32,0},{64,32},{96,64},{1,97},{33,1},{65,33},{97,65},{2,98}... | collective-permute-start | bytes 1327112 | tf_op jit(solution)/shard_map/ppermute | solution.py:30
  42.6 25.2 %collective-permute-start.10 = (f32[256,768]{1,0:T(8,128)S(1)}, f32[256,768]{1,0:T(8,128)S(1)}, u32[]{:S(2)}, u32[]{:S(2)}) collective-permute-start(f32[256,768]{1,0:T(8,128)S(1)} %get-tuple-element.42), channel_id=1, source_target_pairs={{0,128},{128,0},{1,129},{129,1},{2,130},{130,2},{3,131},{131,3},{4... | collective-permute-start | bytes 2359304 | tf_op jit(solution)/shard_map/ppermute | solution.py:30
  42.7 13.9 %collective-permute-start.12 = (bf16[96,768]{1,0:T(8,128)(2,1)S(1)}, bf16[96,768]{1,0:T(8,128)(2,1)S(1)}, u32[]{:S(2)}, u32[]{:S(2)}) collective-permute-start(bf16[96,768]{1,0:T(8,128)(2,1)S(1)} %bitcast.16), channel_id=1, source_target_pairs={{0,24},{8,0},{16,8},{24,16},{1,25},{9,1},{17,9},{25,17},{2,26},{10... | collective-permute-start | bytes 442376 | tf_op jit(solution)/shard_map/ppermute | solution.py:30
  50.8 13.8 %collective-permute-start.13 = (bf16[96,768]{1,0:T(8,128)(2,1)S(1)}, bf16[96,768]{1,0:T(8,128)(2,1)S(1)}, u32[]{:S(2)}, u32[]{:S(2)}) collective-permute-start(bf16[96,768]{1,0:T(8,128)(2,1)S(1)} %bitcast.17), channel_id=1, source_target_pairs={{0,16},{8,24},{16,0},{24,8},{1,17},{9,25},{17,1},{25,9},{2,18},{10... | collective-permute-start | bytes 442376 | tf_op jit(solution)/shard_map/ppermute | solution.py:30
  53.3 12.4 %collective-permute-start.14 = (bf16[96,768]{1,0:T(8,128)(2,1)S(1)}, bf16[96,768]{1,0:T(8,128)(2,1)S(1)}, u32[]{:S(2)}, u32[]{:S(2)}) collective-permute-start(bf16[96,768]{1,0:T(8,128)(2,1)S(1)} %bitcast.18), channel_id=1, source_target_pairs={{0,8},{8,16},{16,24},{24,0},{1,9},{9,17},{17,25},{25,1},{2,10},{10... | collective-permute-start | bytes 442376 | tf_op jit(solution)/shard_map/ppermute | solution.py:30
  53.3 87.6 %collective-permute-start.21 = (bf16[3,3072,384]{2,1,0:T(8,128)(2,1)}, bf16[3,3072,384]{2,1,0:T(8,128)(2,1)}, u32[]{:S(2)}, u32[]{:S(2)}) collective-permute-start(bf16[3,3072,384]{2,1,0:T(8,128)(2,1)} %bitcast.7.own_hbm), channel_id=1, source_target_pairs={{0,128},{128,0},{1,129},{129,1},{2,130},{130,2},{3,131},{131,3},{4... | collective-permute-start | bytes 21233672 | tf_op jit(solution)/shard_map/ppermute | solution.py:30
  65.7 11.7 %collective-permute-start.17 = (bf16[288,768]{1,0:T(8,128)(2,1)S(1)}, bf16[288,768]{1,0:T(8,128)(2,1)S(1)}, u32[]{:S(2)}, u32[]{:S(2)}) collective-permute-start(bf16[288,768]{1,0:T(8,128)(2,1)S(1)} %constant_dynamic-update-slice_fusion.3.r0), channel_id=1, source_target_pairs={{0,96},{32,0},{64,32},{96,64},{1,97},{33,1},{65,33},{97,65},{2,98}... | collective-permute-start | bytes 1327112 | tf_op jit(solution)/shard_map/ppermute | solution.py:30
  67.3 12.7 %collective-permute-start.15 = (bf16[288,768]{1,0:T(8,128)(2,1)S(1)}, bf16[288,768]{1,0:T(8,128)(2,1)S(1)}, u32[]{:S(2)}, u32[]{:S(2)}) collective-permute-start(bf16[288,768]{1,0:T(8,128)(2,1)S(1)} %constant_dynamic-update-slice_fusion.3.r0), channel_id=1, source_target_pairs={{0,32},{32,64},{64,96},{96,0},{1,33},{33,65},{65,97},{97,1},{2,34}... | collective-permute-start | bytes 1327112 | tf_op jit(solution)/shard_map/ppermute | solution.py:30
  68.2 11.8 %collective-permute-start.11 = (bf16[256,768]{1,0:T(8,128)(2,1)S(1)}, bf16[256,768]{1,0:T(8,128)(2,1)S(1)}, u32[]{:S(2)}, u32[]{:S(2)}) collective-permute-start(bf16[256,768]{1,0:T(8,128)(2,1)S(1)} %get-tuple-element.43.hidden_ref), channel_id=1, source_target_pairs={{0,128},{128,0},{1,129},{129,1},{2,130},{130,2},{3,131},{131,3},{4... | collective-permute-start | bytes 1179656 | tf_op jit(solution)/shard_map/ppermute | solution.py:30
  84.5 11.8 %collective-permute-start.19 = (bf16[3,256,384]{2,1,0:T(8,128)(2,1)}, bf16[3,256,384]{2,1,0:T(8,128)(2,1)S(1)}, u32[]{:S(2)}, u32[]{:S(2)}) collective-permute-start(bf16[3,256,384]{2,1,0:T(8,128)(2,1)} %get-tuple-element.46), channel_id=1, source_target_pairs={{0,128},{128,0},{1,129},{129,1},{2,130},{130,2},{3,131},{131,3},{4... | collective-permute-start | bytes 1769480 | tf_op jit(solution)/shard_map/ppermute | solution.py:30
  100.3 29.1 %all-to-all-start = ((bf16[8,256,384]{2,1,0:T(8,128)(2,1)}), bf16[8,256,384]{2,1,0:T(8,128)(2,1)S(1)}, u32[]{:S(2)}, u32[]{:S(2)}) async-start(bf16[8,256,384]{2,1,0:T(8,128)(2,1)} %bitcast_dynamic-update-slice_fusion), calls=%async_computation | async-start | bytes 3145728 | tf_op jit(solution)/shard_map/all_to_all | solution.py:80
  132.3 24.7 %all-to-all-start.1 = ((bf16[8,256,384]{2,1,0:T(8,128)(2,1)}), bf16[8,256,384]{2,1,0:T(8,128)(2,1)S(1)}, u32[]{:S(2)}, u32[]{:S(2)}) async-start(bf16[8,256,384]{2,1,0:T(8,128)(2,1)} %copy-done.3), calls=%async_computation.1 | async-start | bytes 3145728 | tf_op jit(solution)/shard_map/all_to_all | solution.py:80
  197.9 23.9 %all-to-all-start.3 = ((bf16[8,256,384]{2,1,0:T(8,128)(2,1)}), bf16[8,256,384]{2,1,0:T(8,128)(2,1)S(1)}, u32[]{:S(2)}, u32[]{:S(2)}) async-start(bf16[8,256,384]{2,1,0:T(8,128)(2,1)} %copy-done.4), calls=%async_computation.3 | async-start | bytes 3145728 | tf_op jit(solution)/shard_map/all_to_all | solution.py:80
  234.3 10.0 %collective-permute-start.33 = (bf16[192,768]{1,0:T(8,128)(2,1)S(1)}, bf16[192,768]{1,0:T(8,128)(2,1)S(1)}, u32[]{:S(2)}, u32[]{:S(2)}) collective-permute-start(bf16[192,768]{1,0:T(8,128)(2,1)S(1)} %get-tuple-element.66), channel_id=1, source_target_pairs={{0,32},{32,64},{64,96},{96,0},{1,33},{33,65},{65,97},{97,1},{2,34}... | collective-permute-start | bytes 884744 | tf_op jit(solution)/shard_map/ppermute | solution.py:30
  234.8 9.9 %collective-permute-start.34 = (bf16[192,768]{1,0:T(8,128)(2,1)S(1)}, bf16[192,768]{1,0:T(8,128)(2,1)S(1)}, u32[]{:S(2)}, u32[]{:S(2)}) collective-permute-start(bf16[192,768]{1,0:T(8,128)(2,1)S(1)} %get-tuple-element.67), channel_id=1, source_target_pairs={{0,96},{32,0},{64,32},{96,64},{1,97},{33,1},{65,33},{97,65},{2,98}... | collective-permute-start | bytes 884744 | tf_op jit(solution)/shard_map/ppermute | solution.py:30
  238.6 12.1 %collective-permute-start.26 = (bf16[192,768]{1,0:T(8,128)(2,1)S(1)}, bf16[192,768]{1,0:T(8,128)(2,1)S(1)}, u32[]{:S(2)}, u32[]{:S(2)}) collective-permute-start(bf16[192,768]{1,0:T(8,128)(2,1)S(1)} %get-tuple-element.57), channel_id=1, source_target_pairs={{0,32},{32,64},{64,96},{96,0},{1,33},{33,65},{65,97},{97,1},{2,34}... | collective-permute-start | bytes 884744 | tf_op jit(solution)/shard_map/ppermute | solution.py:30
  239.0 12.0 %collective-permute-start.27 = (bf16[192,768]{1,0:T(8,128)(2,1)S(1)}, bf16[192,768]{1,0:T(8,128)(2,1)S(1)}, u32[]{:S(2)}, u32[]{:S(2)}) collective-permute-start(bf16[192,768]{1,0:T(8,128)(2,1)S(1)} %get-tuple-element.58), channel_id=1, source_target_pairs={{0,96},{32,0},{64,32},{96,64},{1,97},{33,1},{65,33},{97,65},{2,98}... | collective-permute-start | bytes 884744 | tf_op jit(solution)/shard_map/ppermute | solution.py:30
  244.9 18.4 %collective-permute-start.35 = (bf16[384,768]{1,0:T(8,128)(2,1)S(1)}, bf16[384,768]{1,0:T(8,128)(2,1)S(1)}, u32[]{:S(2)}, u32[]{:S(2)}) collective-permute-start(bf16[384,768]{1,0:T(8,128)(2,1)S(1)} %get-tuple-element.68), channel_id=1, source_target_pairs={{0,32},{32,64},{64,96},{96,0},{1,33},{33,65},{65,97},{97,1},{2,34}... | collective-permute-start | bytes 1769480 | tf_op jit(solution)/shard_map/ppermute | solution.py:30
  246.7 17.4 %collective-permute-start.36 = (bf16[384,768]{1,0:T(8,128)(2,1)S(1)}, bf16[384,768]{1,0:T(8,128)(2,1)S(1)}, u32[]{:S(2)}, u32[]{:S(2)}) collective-permute-start(bf16[384,768]{1,0:T(8,128)(2,1)S(1)} %get-tuple-element.69), channel_id=1, source_target_pairs={{0,96},{32,0},{64,32},{96,64},{1,97},{33,1},{65,33},{97,65},{2,98}... | collective-permute-start | bytes 1769480 | tf_op jit(solution)/shard_map/ppermute | solution.py:30
  251.2 24.1 %collective-permute-start.28 = (bf16[384,768]{1,0:T(8,128)(2,1)S(1)}, bf16[384,768]{1,0:T(8,128)(2,1)S(1)}, u32[]{:S(2)}, u32[]{:S(2)}) collective-permute-start(bf16[384,768]{1,0:T(8,128)(2,1)S(1)} %get-tuple-element.59), channel_id=1, source_target_pairs={{0,32},{32,64},{64,96},{96,0},{1,33},{33,65},{65,97},{97,1},{2,34}... | collective-permute-start | bytes 1769480 | tf_op jit(solution)/shard_map/ppermute | solution.py:30
  253.0 22.6 %collective-permute-start.29 = (bf16[384,768]{1,0:T(8,128)(2,1)S(1)}, bf16[384,768]{1,0:T(8,128)(2,1)S(1)}, u32[]{:S(2)}, u32[]{:S(2)}) collective-permute-start(bf16[384,768]{1,0:T(8,128)(2,1)S(1)} %get-tuple-element.60), channel_id=1, source_target_pairs={{0,96},{32,0},{64,32},{96,64},{1,97},{33,1},{65,33},{97,65},{2,98}... | collective-permute-start | bytes 1769480 | tf_op jit(solution)/shard_map/ppermute | solution.py:30
  265.0 15.7 %collective-permute-start.37 = (bf16[96,768]{1,0:T(8,128)(2,1)S(1)}, bf16[96,768]{1,0:T(8,128)(2,1)S(1)}, u32[]{:S(2)}, u32[]{:S(2)}) collective-permute-start(bf16[96,768]{1,0:T(8,128)(2,1)S(1)} %get-tuple-element.71), channel_id=1, source_target_pairs={{0,8},{8,16},{16,24},{24,0},{1,9},{9,17},{17,25},{25,1},{2,10},{10... | collective-permute-start | bytes 442376 | tf_op jit(solution)/shard_map/ppermute | solution.py:30
  265.4 19.8 %collective-permute-start.38 = (bf16[96,768]{1,0:T(8,128)(2,1)S(1)}, bf16[96,768]{1,0:T(8,128)(2,1)S(1)}, u32[]{:S(2)}, u32[]{:S(2)}) collective-permute-start(bf16[96,768]{1,0:T(8,128)(2,1)S(1)} %get-tuple-element.72), channel_id=1, source_target_pairs={{0,24},{8,0},{16,8},{24,16},{1,25},{9,1},{17,9},{25,17},{2,26},{10... | collective-permute-start | bytes 442376 | tf_op jit(solution)/shard_map/ppermute | solution.py:30
  269.2 16.0 %collective-permute-start.39 = (bf16[96,768]{1,0:T(8,128)(2,1)S(1)}, bf16[96,768]{1,0:T(8,128)(2,1)S(1)}, u32[]{:S(2)}, u32[]{:S(2)}) collective-permute-start(bf16[96,768]{1,0:T(8,128)(2,1)S(1)} %get-tuple-element.73), channel_id=1, source_target_pairs={{0,16},{8,24},{16,0},{24,8},{1,17},{9,25},{17,1},{25,9},{2,18},{10... | collective-permute-start | bytes 442376 | tf_op jit(solution)/shard_map/ppermute | solution.py:30
  276.5 10.1 %collective-permute-start.30 = (bf16[96,768]{1,0:T(8,128)(2,1)S(1)}, bf16[96,768]{1,0:T(8,128)(2,1)S(1)}, u32[]{:S(2)}, u32[]{:S(2)}) collective-permute-start(bf16[96,768]{1,0:T(8,128)(2,1)S(1)} %get-tuple-element.62), channel_id=1, source_target_pairs={{0,8},{8,16},{16,24},{24,0},{1,9},{9,17},{17,25},{25,1},{2,10},{10... | collective-permute-start | bytes 442376 | tf_op jit(solution)/shard_map/ppermute | solution.py:30
  276.9 16.6 %collective-permute-start.31 = (bf16[96,768]{1,0:T(8,128)(2,1)S(1)}, bf16[96,768]{1,0:T(8,128)(2,1)S(1)}, u32[]{:S(2)}, u32[]{:S(2)}) collective-permute-start(bf16[96,768]{1,0:T(8,128)(2,1)S(1)} %get-tuple-element.63), channel_id=1, source_target_pairs={{0,24},{8,0},{16,8},{24,16},{1,25},{9,1},{17,9},{25,17},{2,26},{10... | collective-permute-start | bytes 442376 | tf_op jit(solution)/shard_map/ppermute | solution.py:30
  280.8 14.7 %collective-permute-start.32 = (bf16[96,768]{1,0:T(8,128)(2,1)S(1)}, bf16[96,768]{1,0:T(8,128)(2,1)S(1)}, u32[]{:S(2)}, u32[]{:S(2)}) collective-permute-start(bf16[96,768]{1,0:T(8,128)(2,1)S(1)} %get-tuple-element.64), channel_id=1, source_target_pairs={{0,16},{8,24},{16,0},{24,8},{1,17},{9,25},{17,1},{25,9},{2,18},{10... | collective-permute-start | bytes 442376 | tf_op jit(solution)/shard_map/ppermute | solution.py:30
  (24 other events, 127.3 us)

commit v4 on v3

--- a/solution.py
+++ b/solution.py
@@ -241,12 +241,17 @@
     away_ref[...] = narrow(dot(crossed_ref[...], down_ref[...], 1, 1))
 
 
-def parts_kernel(at_ref, hidden_ref, down_ref, here_ref, arrived_ref, parts_ref):
+def parts_kernel(
+    at_ref, hidden_hbm, down_ref, here_ref, arrived_ref, parts_ref, hidden_ref, sem
+):
+    load = pltpu.make_async_copy(hidden_hbm, hidden_ref, sem)
+    load.start()
     group, x = at_ref[0], at_ref[1]
-    parts_ref[group * 4 + ((x + 2) & 3)] = narrow(dot(hidden_ref[...], down_ref[...], 1, 1))
     for i, dx in enumerate(EARLY):
         parts_ref[group * 4 + ((x + dx) & 3)] = here_ref[i]
         parts_ref[(1 - group) * 4 + ((x + dx) & 3)] = arrived_ref[i]
+    load.wait()
+    parts_ref[group * 4 + ((x + 2) & 3)] = narrow(dot(hidden_ref[...], down_ref[...], 1, 1))
 
 
 def score_kernel(
@@ -381,7 +386,7 @@
     low[...] = grad_ref[2, BLOCK // 2 :]
 
 
-def latent_kernel(ids_ref, shift_ref, feature_ref, parts_ref, latent_ref, noisy_ref):
+def latent_kernel(ids_ref, shift_ref, feature_ref, parts_ref, latent_ref, noisy_hbm, noisy_ref, sems):
     start = ids_ref[0] * 747796405
     shift = shift_ref[0]
 
@@ -392,24 +397,34 @@
         mixed = sum(wide(parts_ref[j, rows, :]) for j in range(8))
         latent = narrow(finish(mixing) + mixed)
         latent_ref[rows, :] = latent
-        noisy = narrow((1.0 - shift) * wide(latent) + shift * finish(mixing + 374761393))
-        for j in range(8):
-            noisy_ref[j, rows, :] = noisy
+        noisy_ref[rows, :] = narrow(
+            (1.0 - shift) * wide(latent) + shift * finish(mixing + 374761393)
+        )
         return 0
 
     lax.fori_loop(0, SEQ // 16, tile, 0)
-
-
-def gap_kernel(parts_ref, gap_ref, copies_ref):
+    spread(noisy_ref, noisy_hbm, sems)
+
+
+def spread(block_ref, copies_hbm, sems):
+    stores = [
+        pltpu.make_async_copy(block_ref, copies_hbm.at[j], sems.at[j]) for j in range(8)
+    ]
+    for store in stores:
+        store.start()
+    for store in stores:
+        store.wait()
+
+
+def gap_kernel(parts_ref, gap_ref, copies_hbm, sems):
     def tile(i, _):
         rows = row_tile(i)
         gap = narrow(sum(wide(parts_ref[j, rows, :]) for j in range(8)))
         gap_ref[rows, :] = gap
-        for j in range(8):
-            copies_ref[j, rows, :] = gap
         return 0
 
     lax.fori_loop(0, SEQ // 16, tile, 0)
+    spread(gap_ref, copies_hbm, sems)
 
 
 def swap(value):
@@ -478,8 +493,19 @@
     )(at, hidden_crossed, up_rest[3], down_rest[2], down_rest[3])
     part_arrived = swap(part_away)
     parts = local_call(
-        parts_kernel, [SMEM] + [VMEM] * 4, eight_kind, 150_000_000, 4_000_000
-    )(at, hidden, down_far, parts_here, swap(parts_away))
+        parts_kernel,
+        [SMEM, HBM] + [VMEM] * 3,
+        eight_kind,
+        150_000_000,
+        4_000_000,
+        scratch=[pltpu.VMEM((SEQ, FF_LOCAL), jnp.bfloat16), pltpu.SemaphoreType.DMA],
+    )(
+        at,
+        pltpu.with_memory_space_constraint(hidden, pltpu.HBM),
+        down_far,
+        parts_here,
+        swap(parts_away),
+    )
     parts = lax.dynamic_update_index_in_dim(
         parts, part_arrived, (1 - group) * 4 + ((x + 2) & 3), 0
     )
@@ -489,9 +515,11 @@
     latent, noisy = local_call(
         latent_kernel,
         [SMEM, SMEM, VMEM, VMEM],
-        (array(SEQ, BLOCK), eight_kind),
+        (array(SEQ, BLOCK), pltpu.HBM((8, SEQ, BLOCK), jnp.bfloat16)),
         9_000_000,
         4_000_000,
+        scratch=[pltpu.VMEM((SEQ, BLOCK), jnp.bfloat16), pltpu.SemaphoreType.DMA((8,))],
+        to=(VMEM, HBM),
         limit=16,
     )(noise_seeds, shift[None], (local * 668265263)[None], exchange(parts))
     noisy_all = exchange(noisy)
@@ -512,9 +540,22 @@
             pltpu.SemaphoreType.DMA((2,)),
         ],
         limit=44,
-    )(sign, noisy_all, qkv_own, qkv_other, out_own, out_other)
+    )(
+        sign,
+        noisy_all,
+        qkv_own,
+        qkv_other,
+        pltpu.with_memory_space_constraint(out_own, pltpu.HBM),
+        out_other,
+    )
     gap, gap_copies = local_call(
-        gap_kernel, [VMEM], (array(SEQ, BLOCK), eight_kind), 1_000_000, 4_000_000
+        gap_kernel,
+        [VMEM],
+        (array(SEQ, BLOCK), pltpu.HBM((8, SEQ, BLOCK), jnp.bfloat16)),
+        1_000_000,
+        4_000_000,
+        scratch=[pltpu.SemaphoreType.DMA((8,))],
+        to=(VMEM, HBM),
     )(exchange(gap_parts))
     gap_all = exchange(gap_copies)
     gap_crossed = swap(lax.dynamic_slice_in_dim(gap_all, (1 - group) * 4, 4, 0))

time: 300 us -> 298 us (level)
  local copies, waits for them, and re-layouts: 8.69 us -> 3.63 us
  Pallas kernels: 38.4 us -> 41.6 us
    unnamed x30 -> x22, local copies, waits for them, and re-layouts: 7.81 us -> 2.75 us
    pallas_call x3, Pallas kernels: 5.01 us -> 8.34 us  [the longest x1 3.2 us: step(): local_call(parts_kernel, [SMEM, HBM] + [VMEM] * 3, eight_kind, 150000000,...]
  transfers between devices with their start and end apart: 43 -> 43, of which waited for: 30 -> 30; matrix products, arithmetic and copies ran while one was open for 1% -> 1% of each run, Pallas kernels for 6% -> 7%
where the time goes in v4:
time: 298 us; the launch traced here: 294 us
  waiting for transfers between devices  145 us (49%)
  starting transfers between devices  75 us (25%)
  Pallas kernels  41.6 us (14%)
  blocking collectives  24.2 us (8%)
  local copies, waits for them, and re-layouts  3.63 us (1%)
    ppermute x40, waiting for transfers between devices, hop(): return lax.ppermute(value, axis, [(i, (i + step) % n) for i in range(n)])  87.2 us
    ppermute x40, starting transfers between devices, hop(): return lax.ppermute(value, axis, [(i, (i + step) % n) for i in range(n)])  60.7 us
    all_to_all x3, waiting for transfers between devices, exchange(): return lax.all_to_all(parts, MODEL, 0, 0, tiled=True)  57.7 us
    all_to_all x1, blocking collectives, exchange(): return lax.all_to_all(parts, MODEL, 0, 0, tiled=True)  24.2 us
    all_to_all x3, starting transfers between devices, exchange(): return lax.all_to_all(parts, MODEL, 0, 0, tiled=True)  14.3 us
    pallas_call x1, Pallas kernels, step(): local_call(score_kernel, [SMEM, VMEM] + [HBM] * 4, array(8, SEQ, BLOCK),...  12.8 us
  transfers between devices with their start and end apart: 43, of which 30 were waited for; matrix products, arithmetic and copies ran while one was open for 1% of the time, Pallas kernels for 7%

profile of v4, /device:TPU:2, one launch (start us, length us, event | category | flops | bytes accessed | tf_op | source)
XLA Modules:
  0.0 294.4 jit_solution(9079086597958369864)
XLA Ops:
  0.6 6.4 %collective-permute-start.3 = (bf16[96,768]{1,0:T(8,128)(2,1)}, bf16[96,768]{1,0:T(8,128)(2,1)S(1)}, u32[]{:S(2)}, u32[]{:S(2)}) collective-permute-start(bf16[96,768]{1,0:T(8,128)(2,1)} %param.8), channel_id=1, source_target_pairs={{0,24},{8,0},{16,8},{24,16},{1,25},{9,1},{17,9},{25,17},{2,26},{10... | collective-permute-start | bytes 442376 | tf_op jit(solution)/shard_map/ppermute | solution.py:30
  7.0 3.8 %collective-permute-start.4 = (bf16[96,768]{1,0:T(8,128)(2,1)}, bf16[96,768]{1,0:T(8,128)(2,1)S(1)}, u32[]{:S(2)}, u32[]{:S(2)}) collective-permute-start(bf16[96,768]{1,0:T(8,128)(2,1)} %param.8), channel_id=1, source_target_pairs={{0,16},{8,24},{16,0},{24,8},{1,17},{9,25},{17,1},{25,9},{2,18},{10... | collective-permute-start | bytes 442376 | tf_op jit(solution)/shard_map/ppermute | solution.py:30
  13.9 4.9 %collective-permute-done.3 = bf16[96,768]{1,0:T(8,128)(2,1)S(1)} collective-permute-done((bf16[96,768]{1,0:T(8,128)(2,1)}, bf16[96,768]{1,0:T(8,128)(2,1)S(1)}, u32[]{:S(2)}, u32[]{:S(2)}) %collective-permute-start.3) | collective-permute-done | bytes 147488 | tf_op jit(solution)/shard_map/ppermute | solution.py:30
  24.3 3.5 %shard_map.93 = (bf16[256,1536]{1,0:T(8,128)(2,1)S(1)}, bf16[256,1536]{1,0:T(8,128)(2,1)S(1)}) custom-call(s32[1]{0:T(128)S(6)} %copy.15.seed_ref.ids_ref, s32[1,3072]{1,0:T(1,128)S(1)} %fusion.2.feature_ref), custom_call_target="tpu_custom_call" | custom-call | flops 30000000 | bytes 1600000 | tf_op jit(solution)/shard_map/pallas_call | solution.py:461
  28.0 3.1 %collective-permute-done.7.r3 = bf16[288,768]{1,0:T(8,128)(2,1)S(1)} collective-permute-done((bf16[288,768]{1,0:T(8,128)(2,1)S(1)}, bf16[288,768]{1,0:T(8,128)(2,1)S(1)}, u32[]{:S(2)}, u32[]{:S(2)}) %collective-permute-start.7) | collective-permute-done | bytes 442400 | tf_op jit(solution)/shard_map/ppermute | solution.py:30
  33.3 5.8 %collective-permute-done.8.far_top = bf16[240,768]{1,0:T(8,128)(2,1)S(1)} collective-permute-done((bf16[240,768]{1,0:T(8,128)(2,1)S(1)}, bf16[240,768]{1,0:T(8,128)(2,1)S(1)}, u32[]{:S(2)}, u32[]{:S(2)}) %collective-permute-start.8) | collective-permute-done | bytes 368672 | tf_op jit(solution)/shard_map/ppermute | solution.py:30
  42.7 8.1 %collective-permute-start.12 = (bf16[96,768]{1,0:T(8,128)(2,1)S(1)}, bf16[96,768]{1,0:T(8,128)(2,1)S(1)}, u32[]{:S(2)}, u32[]{:S(2)}) collective-permute-start(bf16[96,768]{1,0:T(8,128)(2,1)S(1)} %bitcast.16), channel_id=1, source_target_pairs={{0,24},{8,0},{16,8},{24,16},{1,25},{9,1},{17,9},{25,17},{2,26},{10... | collective-permute-start | bytes 442376 | tf_op jit(solution)/shard_map/ppermute | solution.py:30
  53.3 3.3 %collective-permute-done.12 = bf16[96,768]{1,0:T(8,128)(2,1)S(1)} collective-permute-done((bf16[96,768]{1,0:T(8,128)(2,1)S(1)}, bf16[96,768]{1,0:T(8,128)(2,1)S(1)}, u32[]{:S(2)}, u32[]{:S(2)}) %collective-permute-start.12) | collective-permute-done | bytes 147488 | tf_op jit(solution)/shard_map/ppermute | solution.py:30
  56.6 8.0 %collective-permute-done.13 = bf16[96,768]{1,0:T(8,128)(2,1)S(1)} collective-permute-done((bf16[96,768]{1,0:T(8,128)(2,1)S(1)}, bf16[96,768]{1,0:T(8,128)(2,1)S(1)}, u32[]{:S(2)}, u32[]{:S(2)}) %collective-permute-start.13) | collective-permute-done | bytes 147488 | tf_op jit(solution)/shard_map/ppermute | solution.py:30
  68.4 9.0 %collective-permute-done.17.r1 = bf16[288,768]{1,0:T(8,128)(2,1)S(1)} collective-permute-done((bf16[288,768]{1,0:T(8,128)(2,1)S(1)}, bf16[288,768]{1,0:T(8,128)(2,1)S(1)}, u32[]{:S(2)}, u32[]{:S(2)}) %collective-permute-start.17) | collective-permute-done | bytes 442400 | tf_op jit(solution)/shard_map/ppermute | solution.py:30
  80.1 3.2 %shard_map.97 = (bf16[3,384,768]{2,1,0:T(8,128)(2,1)S(1)}, bf16[3,256,384]{2,1,0:T(8,128)(2,1)S(1)}, bf16[3,256,384]{2,1,0:T(8,128)(2,1)}) custom-call(s32[3]{0:T(128)S(1)} %pad_add_fusion.at_ref, bf16[256,768]{1,0:T(8,128)(2,1)S(1)} %get-tuple-element.43.hidden_ref.hidden_hbm, bf16[256,768]{1,0:T(8,128)(2,1)S(1)} %collective-permute-done.11.crossed_ref.hidden_crossed_ref, ...), custom_call_target="tpu_custom_call" | custom-call | flops 900000000 | bytes 6000000 | tf_op jit(solution)/shard_map/pallas_call | solution.py:473
  84.5 3.0 %collective-permute-start.18 = (bf16[144,768]{1,0:T(8,128)(2,1)S(1)}, bf16[144,768]{1,0:T(8,128)(2,1)S(1)}, u32[]{:S(2)}, u32[]{:S(2)}) collective-permute-start(bf16[144,768]{1,0:T(8,128)(2,1)S(1)} %slice.29), channel_id=1, source_target_pairs={{0,96},{32,0},{64,32},{96,64},{1,97},{33,1},{65,33},{97,65},{2,98}... | collective-permute-start | bytes 663560 | tf_op jit(solution)/shard_map/ppermute | solution.py:30
  87.7 5.2 %collective-permute-done.18.far_bottom = bf16[144,768]{1,0:T(8,128)(2,1)S(1)} collective-permute-done((bf16[144,768]{1,0:T(8,128)(2,1)S(1)}, bf16[144,768]{1,0:T(8,128)(2,1)S(1)}, u32[]{:S(2)}, u32[]{:S(2)}) %collective-permute-start.18) | collective-permute-done | bytes 221216 | tf_op jit(solution)/shard_map/ppermute | solution.py:30
  96.3 3.2 %shard_map.98 = bf16[8,256,384]{2,1,0:T(8,128)(2,1)} custom-call(s32[3]{0:T(128)S(1)} %pad_add_fusion.at_ref, bf16[256,768]{1,0:T(8,128)(2,1)} %copy-done.6, bf16[384,768]{1,0:T(8,128)(2,1)S(1)} %get-tuple-element.44.down_ref.far_ref, bf16[3,256,384]{2,1,0:T(8,128)(2,1)S(1)} %get-tuple-element.45.here_ref, ...), custom_call_target="tpu_custom_call" | custom-call | flops 150000000 | bytes 4000000 | tf_op jit(solution)/shard_map/pallas_call | solution.py:495
  100.2 7.1 %all-to-all-start = ((bf16[8,256,384]{2,1,0:T(8,128)(2,1)}), bf16[8,256,384]{2,1,0:T(8,128)(2,1)S(1)}, u32[]{:S(2)}, u32[]{:S(2)}) async-start(bf16[8,256,384]{2,1,0:T(8,128)(2,1)} %bitcast_dynamic-update-slice_fusion), calls=%async_computation | async-start | bytes 3145728 | tf_op jit(solution)/shard_map/all_to_all | solution.py:80
  108.0 21.3 %all-to-all-done.parts_ref = bf16[8,256,384]{2,1,0:T(8,128)(2,1)S(1)} async-done(((bf16[8,256,384]{2,1,0:T(8,128)(2,1)}), bf16[8,256,384]{2,1,0:T(8,128)(2,1)S(1)}, u32[]{:S(2)}, u32[]{:S(2)}) %all-to-all-start) | async-done | bytes 1572896 | tf_op jit(solution)/shard_map/all_to_all | solution.py:80
  129.3 2.9 shard_map.99
  132.3 3.6 %all-to-all-start.1 = ((bf16[8,256,384]{2,1,0:T(8,128)(2,1)}), bf16[8,256,384]{2,1,0:T(8,128)(2,1)S(1)}, u32[]{:S(2)}, u32[]{:S(2)}) async-start(bf16[8,256,384]{2,1,0:T(8,128)(2,1)} %get-tuple-element.49), calls=%async_computation.1 | async-start | bytes 3145728 | tf_op jit(solution)/shard_map/all_to_all | solution.py:80
  136.0 4.9 %collective-permute-done.22.out_other_hbm = bf16[384,3072]{1,0:T(8,128)(2,1)} collective-permute-done((bf16[384,3072]{1,0:T(8,128)(2,1)}, bf16[384,3072]{1,0:T(8,128)(2,1)}, u32[]{:S(2)}, u32[]{:S(2)}) %collective-permute-start.22) | collective-permute-done | bytes 2359328 | tf_op jit(solution)/shard_map/ppermute | solution.py:30
  140.8 16.1 %all-to-all-done.1.noisy_ref = bf16[8,256,384]{2,1,0:T(8,128)(2,1)S(1)} async-done(((bf16[8,256,384]{2,1,0:T(8,128)(2,1)}), bf16[8,256,384]{2,1,0:T(8,128)(2,1)S(1)}, u32[]{:S(2)}, u32[]{:S(2)}) %all-to-all-start.1) | async-done | bytes 1572896 | tf_op jit(solution)/shard_map/all_to_all | solution.py:80
  156.9 12.8 %shard_map.100 = bf16[8,256,384]{2,1,0:T(8,128)(2,1)S(1)} custom-call(f32[1]{0:T(128)} %bitcast.6.sign_ref, bf16[8,256,384]{2,1,0:T(8,128)(2,1)S(1)} %all-to-all-done.1.noisy_ref, bf16[3,3072,384]{2,1,0:T(8,128)(2,1)} %bitcast.7.own_hbm, bf16[3,3072,384]{2,1,0:T(8,128)(2,1)} %collective-permute-done.21.other_hbm, bf16[384,3072]{1,0:T(8,128)(2,1)} %bitcast.14, ...), custom_call_target="tpu_custom_call" | custom-call | flops 5000000000 | bytes 20000000 | tf_op jit(solution)/shard_map/pallas_call | solution.py:527
  169.7 24.2 %all_to_all.20.parts_ref = bf16[8,256,384]{2,1,0:T(8,128)(2,1)S(1)} all-to-all(bf16[8,256,384]{2,1,0:T(8,128)(2,1)S(1)} %shard_map.100), channel_id=1, replica_groups=mesh['group'=2,'x'=4,'zh'=4,'y'=4,'zl'=2] {'y','zl'}, dimensions={0} | all-to-all | bytes 3145728 | tf_op jit(solution)/shard_map/all_to_all | solution.py:80
  196.1 3.6 %all-to-all-start.3 = ((bf16[8,256,384]{2,1,0:T(8,128)(2,1)}), bf16[8,256,384]{2,1,0:T(8,128)(2,1)S(1)}, u32[]{:S(2)}, u32[]{:S(2)}) async-start(bf16[8,256,384]{2,1,0:T(8,128)(2,1)} %get-tuple-element.51), calls=%async_computation.3 | async-start | bytes 3145728 | tf_op jit(solution)/shard_map/all_to_all | solution.py:80
  199.7 20.3 %all-to-all-done.3.gap_ref = bf16[8,256,384]{2,1,0:T(8,128)(2,1)S(1)} async-done(((bf16[8,256,384]{2,1,0:T(8,128)(2,1)}), bf16[8,256,384]{2,1,0:T(8,128)(2,1)S(1)}, u32[]{:S(2)}, u32[]{:S(2)}) %all-to-all-start.3) | async-done | bytes 1572896 | tf_op jit(solution)/shard_map/all_to_all | solution.py:80
  239.7 2.9 collective-permute-done.33.for_right
  245.6 3.2 %collective-permute-done.26.for_right = bf16[192,768]{1,0:T(8,128)(2,1)S(1)} collective-permute-done((bf16[192,768]{1,0:T(8,128)(2,1)S(1)}, bf16[192,768]{1,0:T(8,128)(2,1)S(1)}, u32[]{:S(2)}, u32[]{:S(2)}) %collective-permute-start.26) | collective-permute-done | bytes 294944 | tf_op jit(solution)/shard_map/ppermute | solution.py:30
  251.9 9.5 %collective-permute-done.35.from_left = bf16[384,768]{1,0:T(8,128)(2,1)S(1)} collective-permute-done((bf16[384,768]{1,0:T(8,128)(2,1)S(1)}, bf16[384,768]{1,0:T(8,128)(2,1)S(1)}, u32[]{:S(2)}, u32[]{:S(2)}) %collective-permute-start.35) | collective-permute-done | bytes 589856 | tf_op jit(solution)/shard_map/ppermute | solution.py:30
  263.6 3.9 %collective-permute-start.38 = (bf16[96,768]{1,0:T(8,128)(2,1)S(1)}, bf16[96,768]{1,0:T(8,128)(2,1)S(1)}, u32[]{:S(2)}, u32[]{:S(2)}) collective-permute-start(bf16[96,768]{1,0:T(8,128)(2,1)S(1)} %get-tuple-element.72), channel_id=1, source_target_pairs={{0,24},{8,0},{16,8},{24,16},{1,25},{9,1},{17,9},{25,17},{2,26},{10... | collective-permute-start | bytes 442376 | tf_op jit(solution)/shard_map/ppermute | solution.py:30
  267.5 4.4 %collective-permute-start.39 = (bf16[96,768]{1,0:T(8,128)(2,1)S(1)}, bf16[96,768]{1,0:T(8,128)(2,1)S(1)}, u32[]{:S(2)}, u32[]{:S(2)}) collective-permute-start(bf16[96,768]{1,0:T(8,128)(2,1)S(1)} %get-tuple-element.73), channel_id=1, source_target_pairs={{0,16},{8,24},{16,0},{24,8},{1,17},{9,25},{17,1},{25,9},{2,18},{10... | collective-permute-start | bytes 442376 | tf_op jit(solution)/shard_map/ppermute | solution.py:30
  275.1 3.9 %collective-permute-start.31 = (bf16[96,768]{1,0:T(8,128)(2,1)S(1)}, bf16[96,768]{1,0:T(8,128)(2,1)S(1)}, u32[]{:S(2)}, u32[]{:S(2)}) collective-permute-start(bf16[96,768]{1,0:T(8,128)(2,1)S(1)} %get-tuple-element.63), channel_id=1, source_target_pairs={{0,24},{8,0},{16,8},{24,16},{1,25},{9,1},{17,9},{25,17},{2,26},{10... | collective-permute-start | bytes 442376 | tf_op jit(solution)/shard_map/ppermute | solution.py:30
  279.0 4.4 %collective-permute-start.32 = (bf16[96,768]{1,0:T(8,128)(2,1)S(1)}, bf16[96,768]{1,0:T(8,128)(2,1)S(1)}, u32[]{:S(2)}, u32[]{:S(2)}) collective-permute-start(bf16[96,768]{1,0:T(8,128)(2,1)S(1)} %get-tuple-element.64), channel_id=1, source_target_pairs={{0,16},{8,24},{16,0},{24,8},{1,17},{9,25},{17,1},{25,9},{2,18},{10... | collective-permute-start | bytes 442376 | tf_op jit(solution)/shard_map/ppermute | solution.py:30
  285.0 6.8 %collective-permute-done.31 = bf16[96,768]{1,0:T(8,128)(2,1)S(1)} collective-permute-done((bf16[96,768]{1,0:T(8,128)(2,1)S(1)}, bf16[96,768]{1,0:T(8,128)(2,1)S(1)}, u32[]{:S(2)}, u32[]{:S(2)}) %collective-permute-start.31) | collective-permute-done | bytes 147488 | tf_op jit(solution)/shard_map/ppermute | solution.py:30
  (112 shorter events, 65.8 us)
Async XLA Ops:
  0.6 18.2 %collective-permute-start.3 = (bf16[96,768]{1,0:T(8,128)(2,1)}, bf16[96,768]{1,0:T(8,128)(2,1)S(1)}, u32[]{:S(2)}, u32[]{:S(2)}) collective-permute-start(bf16[96,768]{1,0:T(8,128)(2,1)} %param.8), channel_id=1, source_target_pairs={{0,24},{8,0},{16,8},{24,16},{1,25},{9,1},{17,9},{25,17},{2,26},{10... | collective-permute-start | bytes 442376 | tf_op jit(solution)/shard_map/ppermute | solution.py:30
  7.0 14.4 %collective-permute-start.5 = (bf16[96,768]{1,0:T(8,128)(2,1)}, bf16[96,768]{1,0:T(8,128)(2,1)S(1)}, u32[]{:S(2)}, u32[]{:S(2)}) collective-permute-start(bf16[96,768]{1,0:T(8,128)(2,1)} %param.8), channel_id=1, source_target_pairs={{0,8},{8,16},{16,24},{24,0},{1,9},{9,17},{17,25},{25,1},{2,10},{10... | collective-permute-start | bytes 442376 | tf_op jit(solution)/shard_map/ppermute | solution.py:30
  7.0 12.9 %collective-permute-start.4 = (bf16[96,768]{1,0:T(8,128)(2,1)}, bf16[96,768]{1,0:T(8,128)(2,1)S(1)}, u32[]{:S(2)}, u32[]{:S(2)}) collective-permute-start(bf16[96,768]{1,0:T(8,128)(2,1)} %param.8), channel_id=1, source_target_pairs={{0,16},{8,24},{16,0},{24,8},{1,17},{9,25},{17,1},{25,9},{2,18},{10... | collective-permute-start | bytes 442376 | tf_op jit(solution)/shard_map/ppermute | solution.py:30
  11.8 16.1 %collective-permute-start.2 = (bf16[192,768]{1,0:T(8,128)(2,1)S(1)}, bf16[192,768]{1,0:T(8,128)(2,1)S(1)}, u32[]{:S(2)}, u32[]{:S(2)}) collective-permute-start(bf16[192,768]{1,0:T(8,128)(2,1)S(1)} %pad_maximum_fusion.2.n0), channel_id=1, source_target_pairs={{0,32},{32,64},{64,96},{96,0},{1,33},{33,65},{65,97},{97,1},{2,34}... | collective-permute-start | bytes 884744 | tf_op jit(solution)/shard_map/ppermute | solution.py:30
  13.4 14.5 %collective-permute-start.1 = (bf16[192,768]{1,0:T(8,128)(2,1)S(1)}, bf16[192,768]{1,0:T(8,128)(2,1)S(1)}, u32[]{:S(2)}, u32[]{:S(2)}) collective-permute-start(bf16[192,768]{1,0:T(8,128)(2,1)S(1)} %pad_maximum_fusion.2.n0), channel_id=1, source_target_pairs={{0,96},{32,0},{64,32},{96,64},{1,97},{33,1},{65,33},{97,65},{2,98}... | collective-permute-start | bytes 884744 | tf_op jit(solution)/shard_map/ppermute | solution.py:30
  23.0 9.6 %collective-permute-start.6 = (bf16[288,768]{1,0:T(8,128)(2,1)S(1)}, bf16[288,768]{1,0:T(8,128)(2,1)S(1)}, u32[]{:S(2)}, u32[]{:S(2)}) collective-permute-start(bf16[288,768]{1,0:T(8,128)(2,1)S(1)} %constant_dynamic-update-slice_fusion.r0), channel_id=1, source_target_pairs={{0,96},{32,0},{64,32},{96,64},{1,97},{33,1},{65,33},{97,65},{2,98}... | collective-permute-start | bytes 1327112 | tf_op jit(solution)/shard_map/ppermute | solution.py:30
  42.6 25.2 %collective-permute-start.10 = (f32[256,768]{1,0:T(8,128)S(1)}, f32[256,768]{1,0:T(8,128)S(1)}, u32[]{:S(2)}, u32[]{:S(2)}) collective-permute-start(f32[256,768]{1,0:T(8,128)S(1)} %get-tuple-element.42), channel_id=1, source_target_pairs={{0,128},{128,0},{1,129},{129,1},{2,130},{130,2},{3,131},{131,3},{4... | collective-permute-start | bytes 2359304 | tf_op jit(solution)/shard_map/ppermute | solution.py:30
  42.7 13.9 %collective-permute-start.12 = (bf16[96,768]{1,0:T(8,128)(2,1)S(1)}, bf16[96,768]{1,0:T(8,128)(2,1)S(1)}, u32[]{:S(2)}, u32[]{:S(2)}) collective-permute-start(bf16[96,768]{1,0:T(8,128)(2,1)S(1)} %bitcast.16), channel_id=1, source_target_pairs={{0,24},{8,0},{16,8},{24,16},{1,25},{9,1},{17,9},{25,17},{2,26},{10... | collective-permute-start | bytes 442376 | tf_op jit(solution)/shard_map/ppermute | solution.py:30
  50.8 13.8 %collective-permute-start.13 = (bf16[96,768]{1,0:T(8,128)(2,1)S(1)}, bf16[96,768]{1,0:T(8,128)(2,1)S(1)}, u32[]{:S(2)}, u32[]{:S(2)}) collective-permute-start(bf16[96,768]{1,0:T(8,128)(2,1)S(1)} %bitcast.17), channel_id=1, source_target_pairs={{0,16},{8,24},{16,0},{24,8},{1,17},{9,25},{17,1},{25,9},{2,18},{10... | collective-permute-start | bytes 442376 | tf_op jit(solution)/shard_map/ppermute | solution.py:30
  53.3 12.4 %collective-permute-start.14 = (bf16[96,768]{1,0:T(8,128)(2,1)S(1)}, bf16[96,768]{1,0:T(8,128)(2,1)S(1)}, u32[]{:S(2)}, u32[]{:S(2)}) collective-permute-start(bf16[96,768]{1,0:T(8,128)(2,1)S(1)} %bitcast.18), channel_id=1, source_target_pairs={{0,8},{8,16},{16,24},{24,0},{1,9},{9,17},{17,25},{25,1},{2,10},{10... | collective-permute-start | bytes 442376 | tf_op jit(solution)/shard_map/ppermute | solution.py:30
  53.3 87.6 %collective-permute-start.21 = (bf16[3,3072,384]{2,1,0:T(8,128)(2,1)}, bf16[3,3072,384]{2,1,0:T(8,128)(2,1)}, u32[]{:S(2)}, u32[]{:S(2)}) collective-permute-start(bf16[3,3072,384]{2,1,0:T(8,128)(2,1)} %bitcast.7.own_hbm), channel_id=1, source_target_pairs={{0,128},{128,0},{1,129},{129,1},{2,130},{130,2},{3,131},{131,3},{4... | collective-permute-start | bytes 21233672 | tf_op jit(solution)/shard_map/ppermute | solution.py:30
  65.7 11.7 %collective-permute-start.17 = (bf16[288,768]{1,0:T(8,128)(2,1)S(1)}, bf16[288,768]{1,0:T(8,128)(2,1)S(1)}, u32[]{:S(2)}, u32[]{:S(2)}) collective-permute-start(bf16[288,768]{1,0:T(8,128)(2,1)S(1)} %constant_dynamic-update-slice_fusion.3.r0), channel_id=1, source_target_pairs={{0,96},{32,0},{64,32},{96,64},{1,97},{33,1},{65,33},{97,65},{2,98}... | collective-permute-start | bytes 1327112 | tf_op jit(solution)/shard_map/ppermute | solution.py:30
  67.3 12.7 %collective-permute-start.15 = (bf16[288,768]{1,0:T(8,128)(2,1)S(1)}, bf16[288,768]{1,0:T(8,128)(2,1)S(1)}, u32[]{:S(2)}, u32[]{:S(2)}) collective-permute-start(bf16[288,768]{1,0:T(8,128)(2,1)S(1)} %constant_dynamic-update-slice_fusion.3.r0), channel_id=1, source_target_pairs={{0,32},{32,64},{64,96},{96,0},{1,33},{33,65},{65,97},{97,1},{2,34}... | collective-permute-start | bytes 1327112 | tf_op jit(solution)/shard_map/ppermute | solution.py:30
  68.2 11.8 %collective-permute-start.11 = (bf16[256,768]{1,0:T(8,128)(2,1)S(1)}, bf16[256,768]{1,0:T(8,128)(2,1)S(1)}, u32[]{:S(2)}, u32[]{:S(2)}) collective-permute-start(bf16[256,768]{1,0:T(8,128)(2,1)S(1)} %get-tuple-element.43.hidden_ref.hidden_hbm), channel_id=1, source_target_pairs={{0,128},{128,0},{1,129},{129,1},{2,130},{130,2},{3,131},{131,3},{4... | collective-permute-start | bytes 1179656 | tf_op jit(solution)/shard_map/ppermute | solution.py:30
  84.5 11.8 %collective-permute-start.19 = (bf16[3,256,384]{2,1,0:T(8,128)(2,1)}, bf16[3,256,384]{2,1,0:T(8,128)(2,1)S(1)}, u32[]{:S(2)}, u32[]{:S(2)}) collective-permute-start(bf16[3,256,384]{2,1,0:T(8,128)(2,1)} %get-tuple-element.46), channel_id=1, source_target_pairs={{0,128},{128,0},{1,129},{129,1},{2,130},{130,2},{3,131},{131,3},{4... | collective-permute-start | bytes 1769480 | tf_op jit(solution)/shard_map/ppermute | solution.py:30
  100.2 29.1 %all-to-all-start = ((bf16[8,256,384]{2,1,0:T(8,128)(2,1)}), bf16[8,256,384]{2,1,0:T(8,128)(2,1)S(1)}, u32[]{:S(2)}, u32[]{:S(2)}) async-start(bf16[8,256,384]{2,1,0:T(8,128)(2,1)} %bitcast_dynamic-update-slice_fusion), calls=%async_computation | async-start | bytes 3145728 | tf_op jit(solution)/shard_map/all_to_all | solution.py:80
  132.3 24.7 %all-to-all-start.1 = ((bf16[8,256,384]{2,1,0:T(8,128)(2,1)}), bf16[8,256,384]{2,1,0:T(8,128)(2,1)S(1)}, u32[]{:S(2)}, u32[]{:S(2)}) async-start(bf16[8,256,384]{2,1,0:T(8,128)(2,1)} %get-tuple-element.49), calls=%async_computation.1 | async-start | bytes 3145728 | tf_op jit(solution)/shard_map/all_to_all | solution.py:80
  196.1 23.9 %all-to-all-start.3 = ((bf16[8,256,384]{2,1,0:T(8,128)(2,1)}), bf16[8,256,384]{2,1,0:T(8,128)(2,1)S(1)}, u32[]{:S(2)}, u32[]{:S(2)}) async-start(bf16[8,256,384]{2,1,0:T(8,128)(2,1)} %get-tuple-element.51), calls=%async_computation.3 | async-start | bytes 3145728 | tf_op jit(solution)/shard_map/all_to_all | solution.py:80
  232.6 10.0 %collective-permute-start.33 = (bf16[192,768]{1,0:T(8,128)(2,1)S(1)}, bf16[192,768]{1,0:T(8,128)(2,1)S(1)}, u32[]{:S(2)}, u32[]{:S(2)}) collective-permute-start(bf16[192,768]{1,0:T(8,128)(2,1)S(1)} %get-tuple-element.66), channel_id=1, source_target_pairs={{0,32},{32,64},{64,96},{96,0},{1,33},{33,65},{65,97},{97,1},{2,34}... | collective-permute-start | bytes 884744 | tf_op jit(solution)/shard_map/ppermute | solution.py:30
  233.0 9.9 %collective-permute-start.34 = (bf16[192,768]{1,0:T(8,128)(2,1)S(1)}, bf16[192,768]{1,0:T(8,128)(2,1)S(1)}, u32[]{:S(2)}, u32[]{:S(2)}) collective-permute-start(bf16[192,768]{1,0:T(8,128)(2,1)S(1)} %get-tuple-element.67), channel_id=1, source_target_pairs={{0,96},{32,0},{64,32},{96,64},{1,97},{33,1},{65,33},{97,65},{2,98}... | collective-permute-start | bytes 884744 | tf_op jit(solution)/shard_map/ppermute | solution.py:30
  236.8 12.1 %collective-permute-start.26 = (bf16[192,768]{1,0:T(8,128)(2,1)S(1)}, bf16[192,768]{1,0:T(8,128)(2,1)S(1)}, u32[]{:S(2)}, u32[]{:S(2)}) collective-permute-start(bf16[192,768]{1,0:T(8,128)(2,1)S(1)} %get-tuple-element.57), channel_id=1, source_target_pairs={{0,32},{32,64},{64,96},{96,0},{1,33},{33,65},{65,97},{97,1},{2,34}... | collective-permute-start | bytes 884744 | tf_op jit(solution)/shard_map/ppermute | solution.py:30
  237.2 12.0 %collective-permute-start.27 = (bf16[192,768]{1,0:T(8,128)(2,1)S(1)}, bf16[192,768]{1,0:T(8,128)(2,1)S(1)}, u32[]{:S(2)}, u32[]{:S(2)}) collective-permute-start(bf16[192,768]{1,0:T(8,128)(2,1)S(1)} %get-tuple-element.58), channel_id=1, source_target_pairs={{0,96},{32,0},{64,32},{96,64},{1,97},{33,1},{65,33},{97,65},{2,98}... | collective-permute-start | bytes 884744 | tf_op jit(solution)/shard_map/ppermute | solution.py:30
  243.1 18.4 %collective-permute-start.35 = (bf16[384,768]{1,0:T(8,128)(2,1)S(1)}, bf16[384,768]{1,0:T(8,128)(2,1)S(1)}, u32[]{:S(2)}, u32[]{:S(2)}) collective-permute-start(bf16[384,768]{1,0:T(8,128)(2,1)S(1)} %get-tuple-element.68), channel_id=1, source_target_pairs={{0,32},{32,64},{64,96},{96,0},{1,33},{33,65},{65,97},{97,1},{2,34}... | collective-permute-start | bytes 1769480 | tf_op jit(solution)/shard_map/ppermute | solution.py:30
  244.9 17.4 %collective-permute-start.36 = (bf16[384,768]{1,0:T(8,128)(2,1)S(1)}, bf16[384,768]{1,0:T(8,128)(2,1)S(1)}, u32[]{:S(2)}, u32[]{:S(2)}) collective-permute-start(bf16[384,768]{1,0:T(8,128)(2,1)S(1)} %get-tuple-element.69), channel_id=1, source_target_pairs={{0,96},{32,0},{64,32},{96,64},{1,97},{33,1},{65,33},{97,65},{2,98}... | collective-permute-start | bytes 1769480 | tf_op jit(solution)/shard_map/ppermute | solution.py:30
  249.4 24.1 %collective-permute-start.28 = (bf16[384,768]{1,0:T(8,128)(2,1)S(1)}, bf16[384,768]{1,0:T(8,128)(2,1)S(1)}, u32[]{:S(2)}, u32[]{:S(2)}) collective-permute-start(bf16[384,768]{1,0:T(8,128)(2,1)S(1)} %get-tuple-element.59), channel_id=1, source_target_pairs={{0,32},{32,64},{64,96},{96,0},{1,33},{33,65},{65,97},{97,1},{2,34}... | collective-permute-start | bytes 1769480 | tf_op jit(solution)/shard_map/ppermute | solution.py:30
  251.2 22.6 %collective-permute-start.29 = (bf16[384,768]{1,0:T(8,128)(2,1)S(1)}, bf16[384,768]{1,0:T(8,128)(2,1)S(1)}, u32[]{:S(2)}, u32[]{:S(2)}) collective-permute-start(bf16[384,768]{1,0:T(8,128)(2,1)S(1)} %get-tuple-element.60), channel_id=1, source_target_pairs={{0,96},{32,0},{64,32},{96,64},{1,97},{33,1},{65,33},{97,65},{2,98}... | collective-permute-start | bytes 1769480 | tf_op jit(solution)/shard_map/ppermute | solution.py:30
  263.3 15.7 %collective-permute-start.37 = (bf16[96,768]{1,0:T(8,128)(2,1)S(1)}, bf16[96,768]{1,0:T(8,128)(2,1)S(1)}, u32[]{:S(2)}, u32[]{:S(2)}) collective-permute-start(bf16[96,768]{1,0:T(8,128)(2,1)S(1)} %get-tuple-element.71), channel_id=1, source_target_pairs={{0,8},{8,16},{16,24},{24,0},{1,9},{9,17},{17,25},{25,1},{2,10},{10... | collective-permute-start | bytes 442376 | tf_op jit(solution)/shard_map/ppermute | solution.py:30
  263.6 19.8 %collective-permute-start.38 = (bf16[96,768]{1,0:T(8,128)(2,1)S(1)}, bf16[96,768]{1,0:T(8,128)(2,1)S(1)}, u32[]{:S(2)}, u32[]{:S(2)}) collective-permute-start(bf16[96,768]{1,0:T(8,128)(2,1)S(1)} %get-tuple-element.72), channel_id=1, source_target_pairs={{0,24},{8,0},{16,8},{24,16},{1,25},{9,1},{17,9},{25,17},{2,26},{10... | collective-permute-start | bytes 442376 | tf_op jit(solution)/shard_map/ppermute | solution.py:30
  267.5 15.9 %collective-permute-start.39 = (bf16[96,768]{1,0:T(8,128)(2,1)S(1)}, bf16[96,768]{1,0:T(8,128)(2,1)S(1)}, u32[]{:S(2)}, u32[]{:S(2)}) collective-permute-start(bf16[96,768]{1,0:T(8,128)(2,1)S(1)} %get-tuple-element.73), channel_id=1, source_target_pairs={{0,16},{8,24},{16,0},{24,8},{1,17},{9,25},{17,1},{25,9},{2,18},{10... | collective-permute-start | bytes 442376 | tf_op jit(solution)/shard_map/ppermute | solution.py:30
  274.8 10.2 %collective-permute-start.30 = (bf16[96,768]{1,0:T(8,128)(2,1)S(1)}, bf16[96,768]{1,0:T(8,128)(2,1)S(1)}, u32[]{:S(2)}, u32[]{:S(2)}) collective-permute-start(bf16[96,768]{1,0:T(8,128)(2,1)S(1)} %get-tuple-element.62), channel_id=1, source_target_pairs={{0,8},{8,16},{16,24},{24,0},{1,9},{9,17},{17,25},{25,1},{2,10},{10... | collective-permute-start | bytes 442376 | tf_op jit(solution)/shard_map/ppermute | solution.py:30
  275.1 16.7 %collective-permute-start.31 = (bf16[96,768]{1,0:T(8,128)(2,1)S(1)}, bf16[96,768]{1,0:T(8,128)(2,1)S(1)}, u32[]{:S(2)}, u32[]{:S(2)}) collective-permute-start(bf16[96,768]{1,0:T(8,128)(2,1)S(1)} %get-tuple-element.63), channel_id=1, source_target_pairs={{0,24},{8,0},{16,8},{24,16},{1,25},{9,1},{17,9},{25,17},{2,26},{10... | collective-permute-start | bytes 442376 | tf_op jit(solution)/shard_map/ppermute | solution.py:30
  279.0 14.7 %collective-permute-start.32 = (bf16[96,768]{1,0:T(8,128)(2,1)S(1)}, bf16[96,768]{1,0:T(8,128)(2,1)S(1)}, u32[]{:S(2)}, u32[]{:S(2)}) collective-permute-start(bf16[96,768]{1,0:T(8,128)(2,1)S(1)} %get-tuple-element.64), channel_id=1, source_target_pairs={{0,16},{8,24},{16,0},{24,8},{1,17},{9,25},{17,1},{25,9},{2,18},{10... | collective-permute-start | bytes 442376 | tf_op jit(solution)/shard_map/ppermute | solution.py:30
  (20 other events, 122.1 us)

commit v5 on v4

--- a/solution.py
+++ b/solution.py
@@ -402,16 +402,21 @@
         )
         return 0
 
-    lax.fori_loop(0, SEQ // 16, tile, 0)
-    spread(noisy_ref, noisy_hbm, sems)
-
-
-def spread(block_ref, copies_hbm, sems):
-    stores = [
-        pltpu.make_async_copy(block_ref, copies_hbm.at[j], sems.at[j]) for j in range(8)
-    ]
-    for store in stores:
-        store.start()
+    spread(tile, noisy_ref, noisy_hbm, sems)
+
+
+def spread(tile, block_ref, copies_hbm, sems):
+    stores = []
+    for quarter in range(4):
+        lax.fori_loop(quarter * 4, quarter * 4 + 4, tile, 0)
+        rows = pl.ds(quarter * (SEQ // 4), SEQ // 4)
+        for j in range(8):
+            stores.append(
+                pltpu.make_async_copy(
+                    block_ref.at[rows, :], copies_hbm.at[j, rows, :], sems.at[quarter, j]
+                )
+            )
+            stores[-1].start()
     for store in stores:
         store.wait()
 
@@ -423,8 +428,7 @@
         gap_ref[rows, :] = gap
         return 0
 
-    lax.fori_loop(0, SEQ // 16, tile, 0)
-    spread(gap_ref, copies_hbm, sems)
+    spread(tile, gap_ref, copies_hbm, sems)
 
 
 def swap(value):
@@ -518,7 +522,7 @@
         (array(SEQ, BLOCK), pltpu.HBM((8, SEQ, BLOCK), jnp.bfloat16)),
         9_000_000,
         4_000_000,
-        scratch=[pltpu.VMEM((SEQ, BLOCK), jnp.bfloat16), pltpu.SemaphoreType.DMA((8,))],
+        scratch=[pltpu.VMEM((SEQ, BLOCK), jnp.bfloat16), pltpu.SemaphoreType.DMA((4, 8))],
         to=(VMEM, HBM),
         limit=16,
     )(noise_seeds, shift[None], (local * 668265263)[None], exchange(parts))
@@ -554,7 +558,7 @@
         (array(SEQ, BLOCK), pltpu.HBM((8, SEQ, BLOCK), jnp.bfloat16)),
         1_000_000,
         4_000_000,
-        scratch=[pltpu.SemaphoreType.DMA((8,))],
+        scratch=[pltpu.SemaphoreType.DMA((4, 8))],
         to=(VMEM, HBM),
     )(exchange(gap_parts))
     gap_all = exchange(gap_copies)

time: 298 us -> 298 us (level)
  no operation moved by 1% of the time
where the time goes in v5:
time: 298 us; the launch traced here: 294 us
  waiting for transfers between devices  145 us (49%)
  starting transfers between devices  75 us (25%)
  Pallas kernels  41.3 us (14%)
  blocking collectives  24.2 us (8%)
  local copies, waits for them, and re-layouts  3.63 us (1%)
    ppermute x40, waiting for transfers between devices, hop(): return lax.ppermute(value, axis, [(i, (i + step) % n) for i in range(n)])  87.2 us
    ppermute x40, starting transfers between devices, hop(): return lax.ppermute(value, axis, [(i, (i + step) % n) for i in range(n)])  60.7 us
    all_to_all x3, waiting for transfers between devices, exchange(): return lax.all_to_all(parts, MODEL, 0, 0, tiled=True)  57.8 us
    all_to_all x1, blocking collectives, exchange(): return lax.all_to_all(parts, MODEL, 0, 0, tiled=True)  24.2 us
    all_to_all x3, starting transfers between devices, exchange(): return lax.all_to_all(parts, MODEL, 0, 0, tiled=True)  14.3 us
    pallas_call x1, Pallas kernels, step(): local_call(score_kernel, [SMEM, VMEM] + [HBM] * 4, array(8, SEQ, BLOCK),...  12.8 us
  transfers between devices with their start and end apart: 43, of which 30 were waited for; matrix products, arithmetic and copies ran while one was open for 1% of the time, Pallas kernels for 7%

profile of v5, /device:TPU:2, one launch (start us, length us, event | category | flops | bytes accessed | tf_op | source)
XLA Modules:
  0.0 294.2 jit_solution(13362639709256449897)
XLA Ops:
  0.6 6.4 %collective-permute-start.3 = (bf16[96,768]{1,0:T(8,128)(2,1)}, bf16[96,768]{1,0:T(8,128)(2,1)S(1)}, u32[]{:S(2)}, u32[]{:S(2)}) collective-permute-start(bf16[96,768]{1,0:T(8,128)(2,1)} %param.8), channel_id=1, source_target_pairs={{0,24},{8,0},{16,8},{24,16},{1,25},{9,1},{17,9},{25,17},{2,26},{10... | collective-permute-start | bytes 442376 | tf_op jit(solution)/shard_map/ppermute | solution.py:30
  7.0 3.8 %collective-permute-start.4 = (bf16[96,768]{1,0:T(8,128)(2,1)}, bf16[96,768]{1,0:T(8,128)(2,1)S(1)}, u32[]{:S(2)}, u32[]{:S(2)}) collective-permute-start(bf16[96,768]{1,0:T(8,128)(2,1)} %param.8), channel_id=1, source_target_pairs={{0,16},{8,24},{16,0},{24,8},{1,17},{9,25},{17,1},{25,9},{2,18},{10... | collective-permute-start | bytes 442376 | tf_op jit(solution)/shard_map/ppermute | solution.py:30
  13.9 4.9 %collective-permute-done.3 = bf16[96,768]{1,0:T(8,128)(2,1)S(1)} collective-permute-done((bf16[96,768]{1,0:T(8,128)(2,1)}, bf16[96,768]{1,0:T(8,128)(2,1)S(1)}, u32[]{:S(2)}, u32[]{:S(2)}) %collective-permute-start.3) | collective-permute-done | bytes 147488 | tf_op jit(solution)/shard_map/ppermute | solution.py:30
  24.3 3.5 %shard_map.93 = (bf16[256,1536]{1,0:T(8,128)(2,1)S(1)}, bf16[256,1536]{1,0:T(8,128)(2,1)S(1)}) custom-call(s32[1]{0:T(128)S(6)} %copy.15.seed_ref.ids_ref, s32[1,3072]{1,0:T(1,128)S(1)} %fusion.2.feature_ref), custom_call_target="tpu_custom_call" | custom-call | flops 30000000 | bytes 1600000 | tf_op jit(solution)/shard_map/pallas_call | solution.py:465
  28.0 3.1 %collective-permute-done.7.r3 = bf16[288,768]{1,0:T(8,128)(2,1)S(1)} collective-permute-done((bf16[288,768]{1,0:T(8,128)(2,1)S(1)}, bf16[288,768]{1,0:T(8,128)(2,1)S(1)}, u32[]{:S(2)}, u32[]{:S(2)}) %collective-permute-start.7) | collective-permute-done | bytes 442400 | tf_op jit(solution)/shard_map/ppermute | solution.py:30
  33.3 5.8 %collective-permute-done.8.far_top = bf16[240,768]{1,0:T(8,128)(2,1)S(1)} collective-permute-done((bf16[240,768]{1,0:T(8,128)(2,1)S(1)}, bf16[240,768]{1,0:T(8,128)(2,1)S(1)}, u32[]{:S(2)}, u32[]{:S(2)}) %collective-permute-start.8) | collective-permute-done | bytes 368672 | tf_op jit(solution)/shard_map/ppermute | solution.py:30
  42.7 8.1 %collective-permute-start.12 = (bf16[96,768]{1,0:T(8,128)(2,1)S(1)}, bf16[96,768]{1,0:T(8,128)(2,1)S(1)}, u32[]{:S(2)}, u32[]{:S(2)}) collective-permute-start(bf16[96,768]{1,0:T(8,128)(2,1)S(1)} %bitcast.16), channel_id=1, source_target_pairs={{0,24},{8,0},{16,8},{24,16},{1,25},{9,1},{17,9},{25,17},{2,26},{10... | collective-permute-start | bytes 442376 | tf_op jit(solution)/shard_map/ppermute | solution.py:30
  53.3 3.3 %collective-permute-done.12 = bf16[96,768]{1,0:T(8,128)(2,1)S(1)} collective-permute-done((bf16[96,768]{1,0:T(8,128)(2,1)S(1)}, bf16[96,768]{1,0:T(8,128)(2,1)S(1)}, u32[]{:S(2)}, u32[]{:S(2)}) %collective-permute-start.12) | collective-permute-done | bytes 147488 | tf_op jit(solution)/shard_map/ppermute | solution.py:30
  56.6 8.0 %collective-permute-done.13 = bf16[96,768]{1,0:T(8,128)(2,1)S(1)} collective-permute-done((bf16[96,768]{1,0:T(8,128)(2,1)S(1)}, bf16[96,768]{1,0:T(8,128)(2,1)S(1)}, u32[]{:S(2)}, u32[]{:S(2)}) %collective-permute-start.13) | collective-permute-done | bytes 147488 | tf_op jit(solution)/shard_map/ppermute | solution.py:30
  68.4 9.0 %collective-permute-done.17.r1 = bf16[288,768]{1,0:T(8,128)(2,1)S(1)} collective-permute-done((bf16[288,768]{1,0:T(8,128)(2,1)S(1)}, bf16[288,768]{1,0:T(8,128)(2,1)S(1)}, u32[]{:S(2)}, u32[]{:S(2)}) %collective-permute-start.17) | collective-permute-done | bytes 442400 | tf_op jit(solution)/shard_map/ppermute | solution.py:30
  77.4 2.7 collective-permute-done.15.r3
  80.1 3.2 %shard_map.97 = (bf16[3,384,768]{2,1,0:T(8,128)(2,1)S(1)}, bf16[3,256,384]{2,1,0:T(8,128)(2,1)S(1)}, bf16[3,256,384]{2,1,0:T(8,128)(2,1)}) custom-call(s32[3]{0:T(128)S(1)} %pad_add_fusion.at_ref, bf16[256,768]{1,0:T(8,128)(2,1)S(1)} %get-tuple-element.43.hidden_ref.hidden_hbm, bf16[256,768]{1,0:T(8,128)(2,1)S(1)} %collective-permute-done.11.crossed_ref.hidden_crossed_ref, ...), custom_call_target="tpu_custom_call" | custom-call | flops 900000000 | bytes 6000000 | tf_op jit(solution)/shard_map/pallas_call | solution.py:477
  84.5 3.0 %collective-permute-start.18 = (bf16[144,768]{1,0:T(8,128)(2,1)S(1)}, bf16[144,768]{1,0:T(8,128)(2,1)S(1)}, u32[]{:S(2)}, u32[]{:S(2)}) collective-permute-start(bf16[144,768]{1,0:T(8,128)(2,1)S(1)} %slice.29), channel_id=1, source_target_pairs={{0,96},{32,0},{64,32},{96,64},{1,97},{33,1},{65,33},{97,65},{2,98}... | collective-permute-start | bytes 663560 | tf_op jit(solution)/shard_map/ppermute | solution.py:30
  87.7 5.2 %collective-permute-done.18.far_bottom = bf16[144,768]{1,0:T(8,128)(2,1)S(1)} collective-permute-done((bf16[144,768]{1,0:T(8,128)(2,1)S(1)}, bf16[144,768]{1,0:T(8,128)(2,1)S(1)}, u32[]{:S(2)}, u32[]{:S(2)}) %collective-permute-start.18) | collective-permute-done | bytes 221216 | tf_op jit(solution)/shard_map/ppermute | solution.py:30
  96.3 3.2 %shard_map.98 = bf16[8,256,384]{2,1,0:T(8,128)(2,1)} custom-call(s32[3]{0:T(128)S(1)} %pad_add_fusion.at_ref, bf16[256,768]{1,0:T(8,128)(2,1)} %copy-done.6, bf16[384,768]{1,0:T(8,128)(2,1)S(1)} %get-tuple-element.44.down_ref.far_ref, bf16[3,256,384]{2,1,0:T(8,128)(2,1)S(1)} %get-tuple-element.45.here_ref, ...), custom_call_target="tpu_custom_call" | custom-call | flops 150000000 | bytes 4000000 | tf_op jit(solution)/shard_map/pallas_call | solution.py:499
  100.2 7.1 %all-to-all-start = ((bf16[8,256,384]{2,1,0:T(8,128)(2,1)}), bf16[8,256,384]{2,1,0:T(8,128)(2,1)S(1)}, u32[]{:S(2)}, u32[]{:S(2)}) async-start(bf16[8,256,384]{2,1,0:T(8,128)(2,1)} %bitcast_dynamic-update-slice_fusion), calls=%async_computation | async-start | bytes 3145728 | tf_op jit(solution)/shard_map/all_to_all | solution.py:80
  108.0 21.3 %all-to-all-done.parts_ref = bf16[8,256,384]{2,1,0:T(8,128)(2,1)S(1)} async-done(((bf16[8,256,384]{2,1,0:T(8,128)(2,1)}), bf16[8,256,384]{2,1,0:T(8,128)(2,1)S(1)}, u32[]{:S(2)}, u32[]{:S(2)}) %all-to-all-start) | async-done | bytes 1572896 | tf_op jit(solution)/shard_map/all_to_all | solution.py:80
  132.0 3.6 %all-to-all-start.1 = ((bf16[8,256,384]{2,1,0:T(8,128)(2,1)}), bf16[8,256,384]{2,1,0:T(8,128)(2,1)S(1)}, u32[]{:S(2)}, u32[]{:S(2)}) async-start(bf16[8,256,384]{2,1,0:T(8,128)(2,1)} %get-tuple-element.49), calls=%async_computation.1 | async-start | bytes 3145728 | tf_op jit(solution)/shard_map/all_to_all | solution.py:80
  135.7 4.9 %collective-permute-done.22.out_other_hbm = bf16[384,3072]{1,0:T(8,128)(2,1)} collective-permute-done((bf16[384,3072]{1,0:T(8,128)(2,1)}, bf16[384,3072]{1,0:T(8,128)(2,1)}, u32[]{:S(2)}, u32[]{:S(2)}) %collective-permute-start.22) | collective-permute-done | bytes 2359328 | tf_op jit(solution)/shard_map/ppermute | solution.py:30
  140.6 16.1 %all-to-all-done.1.noisy_ref = bf16[8,256,384]{2,1,0:T(8,128)(2,1)S(1)} async-done(((bf16[8,256,384]{2,1,0:T(8,128)(2,1)}), bf16[8,256,384]{2,1,0:T(8,128)(2,1)S(1)}, u32[]{:S(2)}, u32[]{:S(2)}) %all-to-all-start.1) | async-done | bytes 1572896 | tf_op jit(solution)/shard_map/all_to_all | solution.py:80
  156.7 12.8 %shard_map.100 = bf16[8,256,384]{2,1,0:T(8,128)(2,1)S(1)} custom-call(f32[1]{0:T(128)} %bitcast.6.sign_ref, bf16[8,256,384]{2,1,0:T(8,128)(2,1)S(1)} %all-to-all-done.1.noisy_ref, bf16[3,3072,384]{2,1,0:T(8,128)(2,1)} %bitcast.7.own_hbm, bf16[3,3072,384]{2,1,0:T(8,128)(2,1)} %collective-permute-done.21.other_hbm, bf16[384,3072]{1,0:T(8,128)(2,1)} %bitcast.14, ...), custom_call_target="tpu_custom_call" | custom-call | flops 5000000000 | bytes 20000000 | tf_op jit(solution)/shard_map/pallas_call | solution.py:531
  169.5 24.2 %all_to_all.20.parts_ref = bf16[8,256,384]{2,1,0:T(8,128)(2,1)S(1)} all-to-all(bf16[8,256,384]{2,1,0:T(8,128)(2,1)S(1)} %shard_map.100), channel_id=1, replica_groups=mesh['group'=2,'x'=4,'zh'=4,'y'=4,'zl'=2] {'y','zl'}, dimensions={0} | all-to-all | bytes 3145728 | tf_op jit(solution)/shard_map/all_to_all | solution.py:80
  195.9 3.6 %all-to-all-start.3 = ((bf16[8,256,384]{2,1,0:T(8,128)(2,1)}), bf16[8,256,384]{2,1,0:T(8,128)(2,1)S(1)}, u32[]{:S(2)}, u32[]{:S(2)}) async-start(bf16[8,256,384]{2,1,0:T(8,128)(2,1)} %get-tuple-element.51), calls=%async_computation.3 | async-start | bytes 3145728 | tf_op jit(solution)/shard_map/all_to_all | solution.py:80
  199.5 20.3 %all-to-all-done.3.gap_ref = bf16[8,256,384]{2,1,0:T(8,128)(2,1)S(1)} async-done(((bf16[8,256,384]{2,1,0:T(8,128)(2,1)}), bf16[8,256,384]{2,1,0:T(8,128)(2,1)S(1)}, u32[]{:S(2)}, u32[]{:S(2)}) %all-to-all-start.3) | async-done | bytes 1572896 | tf_op jit(solution)/shard_map/all_to_all | solution.py:80
  239.4 2.9 collective-permute-done.33.for_right
  245.3 3.2 %collective-permute-done.26.for_right = bf16[192,768]{1,0:T(8,128)(2,1)S(1)} collective-permute-done((bf16[192,768]{1,0:T(8,128)(2,1)S(1)}, bf16[192,768]{1,0:T(8,128)(2,1)S(1)}, u32[]{:S(2)}, u32[]{:S(2)}) %collective-permute-start.26) | collective-permute-done | bytes 294944 | tf_op jit(solution)/shard_map/ppermute | solution.py:30
  251.7 9.6 %collective-permute-done.35.from_left = bf16[384,768]{1,0:T(8,128)(2,1)S(1)} collective-permute-done((bf16[384,768]{1,0:T(8,128)(2,1)S(1)}, bf16[384,768]{1,0:T(8,128)(2,1)S(1)}, u32[]{:S(2)}, u32[]{:S(2)}) %collective-permute-start.35) | collective-permute-done | bytes 589856 | tf_op jit(solution)/shard_map/ppermute | solution.py:30
  263.3 3.9 %collective-permute-start.38 = (bf16[96,768]{1,0:T(8,128)(2,1)S(1)}, bf16[96,768]{1,0:T(8,128)(2,1)S(1)}, u32[]{:S(2)}, u32[]{:S(2)}) collective-permute-start(bf16[96,768]{1,0:T(8,128)(2,1)S(1)} %get-tuple-element.72), channel_id=1, source_target_pairs={{0,24},{8,0},{16,8},{24,16},{1,25},{9,1},{17,9},{25,17},{2,26},{10... | collective-permute-start | bytes 442376 | tf_op jit(solution)/shard_map/ppermute | solution.py:30
  267.2 4.4 %collective-permute-start.39 = (bf16[96,768]{1,0:T(8,128)(2,1)S(1)}, bf16[96,768]{1,0:T(8,128)(2,1)S(1)}, u32[]{:S(2)}, u32[]{:S(2)}) collective-permute-start(bf16[96,768]{1,0:T(8,128)(2,1)S(1)} %get-tuple-element.73), channel_id=1, source_target_pairs={{0,16},{8,24},{16,0},{24,8},{1,17},{9,25},{17,1},{25,9},{2,18},{10... | collective-permute-start | bytes 442376 | tf_op jit(solution)/shard_map/ppermute | solution.py:30
  274.9 3.9 %collective-permute-start.31 = (bf16[96,768]{1,0:T(8,128)(2,1)S(1)}, bf16[96,768]{1,0:T(8,128)(2,1)S(1)}, u32[]{:S(2)}, u32[]{:S(2)}) collective-permute-start(bf16[96,768]{1,0:T(8,128)(2,1)S(1)} %get-tuple-element.63), channel_id=1, source_target_pairs={{0,24},{8,0},{16,8},{24,16},{1,25},{9,1},{17,9},{25,17},{2,26},{10... | collective-permute-start | bytes 442376 | tf_op jit(solution)/shard_map/ppermute | solution.py:30
  278.7 4.4 %collective-permute-start.32 = (bf16[96,768]{1,0:T(8,128)(2,1)S(1)}, bf16[96,768]{1,0:T(8,128)(2,1)S(1)}, u32[]{:S(2)}, u32[]{:S(2)}) collective-permute-start(bf16[96,768]{1,0:T(8,128)(2,1)S(1)} %get-tuple-element.64), channel_id=1, source_target_pairs={{0,16},{8,24},{16,0},{24,8},{1,17},{9,25},{17,1},{25,9},{2,18},{10... | collective-permute-start | bytes 442376 | tf_op jit(solution)/shard_map/ppermute | solution.py:30
  284.7 6.8 %collective-permute-done.31 = bf16[96,768]{1,0:T(8,128)(2,1)S(1)} collective-permute-done((bf16[96,768]{1,0:T(8,128)(2,1)S(1)}, bf16[96,768]{1,0:T(8,128)(2,1)S(1)}, u32[]{:S(2)}, u32[]{:S(2)}) %collective-permute-start.31) | collective-permute-done | bytes 147488 | tf_op jit(solution)/shard_map/ppermute | solution.py:30
  (112 shorter events, 65.7 us)
Async XLA Ops:
  0.6 18.2 %collective-permute-start.3 = (bf16[96,768]{1,0:T(8,128)(2,1)}, bf16[96,768]{1,0:T(8,128)(2,1)S(1)}, u32[]{:S(2)}, u32[]{:S(2)}) collective-permute-start(bf16[96,768]{1,0:T(8,128)(2,1)} %param.8), channel_id=1, source_target_pairs={{0,24},{8,0},{16,8},{24,16},{1,25},{9,1},{17,9},{25,17},{2,26},{10... | collective-permute-start | bytes 442376 | tf_op jit(solution)/shard_map/ppermute | solution.py:30
  7.0 14.4 %collective-permute-start.5 = (bf16[96,768]{1,0:T(8,128)(2,1)}, bf16[96,768]{1,0:T(8,128)(2,1)S(1)}, u32[]{:S(2)}, u32[]{:S(2)}) collective-permute-start(bf16[96,768]{1,0:T(8,128)(2,1)} %param.8), channel_id=1, source_target_pairs={{0,8},{8,16},{16,24},{24,0},{1,9},{9,17},{17,25},{25,1},{2,10},{10... | collective-permute-start | bytes 442376 | tf_op jit(solution)/shard_map/ppermute | solution.py:30
  7.0 12.9 %collective-permute-start.4 = (bf16[96,768]{1,0:T(8,128)(2,1)}, bf16[96,768]{1,0:T(8,128)(2,1)S(1)}, u32[]{:S(2)}, u32[]{:S(2)}) collective-permute-start(bf16[96,768]{1,0:T(8,128)(2,1)} %param.8), channel_id=1, source_target_pairs={{0,16},{8,24},{16,0},{24,8},{1,17},{9,25},{17,1},{25,9},{2,18},{10... | collective-permute-start | bytes 442376 | tf_op jit(solution)/shard_map/ppermute | solution.py:30
  11.8 16.1 %collective-permute-start.2 = (bf16[192,768]{1,0:T(8,128)(2,1)S(1)}, bf16[192,768]{1,0:T(8,128)(2,1)S(1)}, u32[]{:S(2)}, u32[]{:S(2)}) collective-permute-start(bf16[192,768]{1,0:T(8,128)(2,1)S(1)} %pad_maximum_fusion.2.n0), channel_id=1, source_target_pairs={{0,32},{32,64},{64,96},{96,0},{1,33},{33,65},{65,97},{97,1},{2,34}... | collective-permute-start | bytes 884744 | tf_op jit(solution)/shard_map/ppermute | solution.py:30
  13.4 14.5 %collective-permute-start.1 = (bf16[192,768]{1,0:T(8,128)(2,1)S(1)}, bf16[192,768]{1,0:T(8,128)(2,1)S(1)}, u32[]{:S(2)}, u32[]{:S(2)}) collective-permute-start(bf16[192,768]{1,0:T(8,128)(2,1)S(1)} %pad_maximum_fusion.2.n0), channel_id=1, source_target_pairs={{0,96},{32,0},{64,32},{96,64},{1,97},{33,1},{65,33},{97,65},{2,98}... | collective-permute-start | bytes 884744 | tf_op jit(solution)/shard_map/ppermute | solution.py:30
  23.0 9.6 %collective-permute-start.6 = (bf16[288,768]{1,0:T(8,128)(2,1)S(1)}, bf16[288,768]{1,0:T(8,128)(2,1)S(1)}, u32[]{:S(2)}, u32[]{:S(2)}) collective-permute-start(bf16[288,768]{1,0:T(8,128)(2,1)S(1)} %constant_dynamic-update-slice_fusion.r0), channel_id=1, source_target_pairs={{0,96},{32,0},{64,32},{96,64},{1,97},{33,1},{65,33},{97,65},{2,98}... | collective-permute-start | bytes 1327112 | tf_op jit(solution)/shard_map/ppermute | solution.py:30
  42.6 25.2 %collective-permute-start.10 = (f32[256,768]{1,0:T(8,128)S(1)}, f32[256,768]{1,0:T(8,128)S(1)}, u32[]{:S(2)}, u32[]{:S(2)}) collective-permute-start(f32[256,768]{1,0:T(8,128)S(1)} %get-tuple-element.42), channel_id=1, source_target_pairs={{0,128},{128,0},{1,129},{129,1},{2,130},{130,2},{3,131},{131,3},{4... | collective-permute-start | bytes 2359304 | tf_op jit(solution)/shard_map/ppermute | solution.py:30
  42.7 13.9 %collective-permute-start.12 = (bf16[96,768]{1,0:T(8,128)(2,1)S(1)}, bf16[96,768]{1,0:T(8,128)(2,1)S(1)}, u32[]{:S(2)}, u32[]{:S(2)}) collective-permute-start(bf16[96,768]{1,0:T(8,128)(2,1)S(1)} %bitcast.16), channel_id=1, source_target_pairs={{0,24},{8,0},{16,8},{24,16},{1,25},{9,1},{17,9},{25,17},{2,26},{10... | collective-permute-start | bytes 442376 | tf_op jit(solution)/shard_map/ppermute | solution.py:30
  50.8 13.8 %collective-permute-start.13 = (bf16[96,768]{1,0:T(8,128)(2,1)S(1)}, bf16[96,768]{1,0:T(8,128)(2,1)S(1)}, u32[]{:S(2)}, u32[]{:S(2)}) collective-permute-start(bf16[96,768]{1,0:T(8,128)(2,1)S(1)} %bitcast.17), channel_id=1, source_target_pairs={{0,16},{8,24},{16,0},{24,8},{1,17},{9,25},{17,1},{25,9},{2,18},{10... | collective-permute-start | bytes 442376 | tf_op jit(solution)/shard_map/ppermute | solution.py:30
  53.3 12.4 %collective-permute-start.14 = (bf16[96,768]{1,0:T(8,128)(2,1)S(1)}, bf16[96,768]{1,0:T(8,128)(2,1)S(1)}, u32[]{:S(2)}, u32[]{:S(2)}) collective-permute-start(bf16[96,768]{1,0:T(8,128)(2,1)S(1)} %bitcast.18), channel_id=1, source_target_pairs={{0,8},{8,16},{16,24},{24,0},{1,9},{9,17},{17,25},{25,1},{2,10},{10... | collective-permute-start | bytes 442376 | tf_op jit(solution)/shard_map/ppermute | solution.py:30
  53.3 87.3 %collective-permute-start.21 = (bf16[3,3072,384]{2,1,0:T(8,128)(2,1)}, bf16[3,3072,384]{2,1,0:T(8,128)(2,1)}, u32[]{:S(2)}, u32[]{:S(2)}) collective-permute-start(bf16[3,3072,384]{2,1,0:T(8,128)(2,1)} %bitcast.7.own_hbm), channel_id=1, source_target_pairs={{0,128},{128,0},{1,129},{129,1},{2,130},{130,2},{3,131},{131,3},{4... | collective-permute-start | bytes 21233672 | tf_op jit(solution)/shard_map/ppermute | solution.py:30
  65.7 11.7 %collective-permute-start.17 = (bf16[288,768]{1,0:T(8,128)(2,1)S(1)}, bf16[288,768]{1,0:T(8,128)(2,1)S(1)}, u32[]{:S(2)}, u32[]{:S(2)}) collective-permute-start(bf16[288,768]{1,0:T(8,128)(2,1)S(1)} %constant_dynamic-update-slice_fusion.3.r0), channel_id=1, source_target_pairs={{0,96},{32,0},{64,32},{96,64},{1,97},{33,1},{65,33},{97,65},{2,98}... | collective-permute-start | bytes 1327112 | tf_op jit(solution)/shard_map/ppermute | solution.py:30
  67.3 12.7 %collective-permute-start.15 = (bf16[288,768]{1,0:T(8,128)(2,1)S(1)}, bf16[288,768]{1,0:T(8,128)(2,1)S(1)}, u32[]{:S(2)}, u32[]{:S(2)}) collective-permute-start(bf16[288,768]{1,0:T(8,128)(2,1)S(1)} %constant_dynamic-update-slice_fusion.3.r0), channel_id=1, source_target_pairs={{0,32},{32,64},{64,96},{96,0},{1,33},{33,65},{65,97},{97,1},{2,34}... | collective-permute-start | bytes 1327112 | tf_op jit(solution)/shard_map/ppermute | solution.py:30
  68.2 11.8 %collective-permute-start.11 = (bf16[256,768]{1,0:T(8,128)(2,1)S(1)}, bf16[256,768]{1,0:T(8,128)(2,1)S(1)}, u32[]{:S(2)}, u32[]{:S(2)}) collective-permute-start(bf16[256,768]{1,0:T(8,128)(2,1)S(1)} %get-tuple-element.43.hidden_ref.hidden_hbm), channel_id=1, source_target_pairs={{0,128},{128,0},{1,129},{129,1},{2,130},{130,2},{3,131},{131,3},{4... | collective-permute-start | bytes 1179656 | tf_op jit(solution)/shard_map/ppermute | solution.py:30
  84.5 11.8 %collective-permute-start.19 = (bf16[3,256,384]{2,1,0:T(8,128)(2,1)}, bf16[3,256,384]{2,1,0:T(8,128)(2,1)S(1)}, u32[]{:S(2)}, u32[]{:S(2)}) collective-permute-start(bf16[3,256,384]{2,1,0:T(8,128)(2,1)} %get-tuple-element.46), channel_id=1, source_target_pairs={{0,128},{128,0},{1,129},{129,1},{2,130},{130,2},{3,131},{131,3},{4... | collective-permute-start | bytes 1769480 | tf_op jit(solution)/shard_map/ppermute | solution.py:30
  100.2 29.1 %all-to-all-start = ((bf16[8,256,384]{2,1,0:T(8,128)(2,1)}), bf16[8,256,384]{2,1,0:T(8,128)(2,1)S(1)}, u32[]{:S(2)}, u32[]{:S(2)}) async-start(bf16[8,256,384]{2,1,0:T(8,128)(2,1)} %bitcast_dynamic-update-slice_fusion), calls=%async_computation | async-start | bytes 3145728 | tf_op jit(solution)/shard_map/all_to_all | solution.py:80
  132.0 24.7 %all-to-all-start.1 = ((bf16[8,256,384]{2,1,0:T(8,128)(2,1)}), bf16[8,256,384]{2,1,0:T(8,128)(2,1)S(1)}, u32[]{:S(2)}, u32[]{:S(2)}) async-start(bf16[8,256,384]{2,1,0:T(8,128)(2,1)} %get-tuple-element.49), calls=%async_computation.1 | async-start | bytes 3145728 | tf_op jit(solution)/shard_map/all_to_all | solution.py:80
  195.9 23.9 %all-to-all-start.3 = ((bf16[8,256,384]{2,1,0:T(8,128)(2,1)}), bf16[8,256,384]{2,1,0:T(8,128)(2,1)S(1)}, u32[]{:S(2)}, u32[]{:S(2)}) async-start(bf16[8,256,384]{2,1,0:T(8,128)(2,1)} %get-tuple-element.51), calls=%async_computation.3 | async-start | bytes 3145728 | tf_op jit(solution)/shard_map/all_to_all | solution.py:80
  232.3 10.0 %collective-permute-start.33 = (bf16[192,768]{1,0:T(8,128)(2,1)S(1)}, bf16[192,768]{1,0:T(8,128)(2,1)S(1)}, u32[]{:S(2)}, u32[]{:S(2)}) collective-permute-start(bf16[192,768]{1,0:T(8,128)(2,1)S(1)} %get-tuple-element.66), channel_id=1, source_target_pairs={{0,32},{32,64},{64,96},{96,0},{1,33},{33,65},{65,97},{97,1},{2,34}... | collective-permute-start | bytes 884744 | tf_op jit(solution)/shard_map/ppermute | solution.py:30
  232.7 9.9 %collective-permute-start.34 = (bf16[192,768]{1,0:T(8,128)(2,1)S(1)}, bf16[192,768]{1,0:T(8,128)(2,1)S(1)}, u32[]{:S(2)}, u32[]{:S(2)}) collective-permute-start(bf16[192,768]{1,0:T(8,128)(2,1)S(1)} %get-tuple-element.67), channel_id=1, source_target_pairs={{0,96},{32,0},{64,32},{96,64},{1,97},{33,1},{65,33},{97,65},{2,98}... | collective-permute-start | bytes 884744 | tf_op jit(solution)/shard_map/ppermute | solution.py:30
  236.5 12.1 %collective-permute-start.26 = (bf16[192,768]{1,0:T(8,128)(2,1)S(1)}, bf16[192,768]{1,0:T(8,128)(2,1)S(1)}, u32[]{:S(2)}, u32[]{:S(2)}) collective-permute-start(bf16[192,768]{1,0:T(8,128)(2,1)S(1)} %get-tuple-element.57), channel_id=1, source_target_pairs={{0,32},{32,64},{64,96},{96,0},{1,33},{33,65},{65,97},{97,1},{2,34}... | collective-permute-start | bytes 884744 | tf_op jit(solution)/shard_map/ppermute | solution.py:30
  236.9 12.0 %collective-permute-start.27 = (bf16[192,768]{1,0:T(8,128)(2,1)S(1)}, bf16[192,768]{1,0:T(8,128)(2,1)S(1)}, u32[]{:S(2)}, u32[]{:S(2)}) collective-permute-start(bf16[192,768]{1,0:T(8,128)(2,1)S(1)} %get-tuple-element.58), channel_id=1, source_target_pairs={{0,96},{32,0},{64,32},{96,64},{1,97},{33,1},{65,33},{97,65},{2,98}... | collective-permute-start | bytes 884744 | tf_op jit(solution)/shard_map/ppermute | solution.py:30
  242.8 18.4 %collective-permute-start.35 = (bf16[384,768]{1,0:T(8,128)(2,1)S(1)}, bf16[384,768]{1,0:T(8,128)(2,1)S(1)}, u32[]{:S(2)}, u32[]{:S(2)}) collective-permute-start(bf16[384,768]{1,0:T(8,128)(2,1)S(1)} %get-tuple-element.68), channel_id=1, source_target_pairs={{0,32},{32,64},{64,96},{96,0},{1,33},{33,65},{65,97},{97,1},{2,34}... | collective-permute-start | bytes 1769480 | tf_op jit(solution)/shard_map/ppermute | solution.py:30
  244.7 17.4 %collective-permute-start.36 = (bf16[384,768]{1,0:T(8,128)(2,1)S(1)}, bf16[384,768]{1,0:T(8,128)(2,1)S(1)}, u32[]{:S(2)}, u32[]{:S(2)}) collective-permute-start(bf16[384,768]{1,0:T(8,128)(2,1)S(1)} %get-tuple-element.69), channel_id=1, source_target_pairs={{0,96},{32,0},{64,32},{96,64},{1,97},{33,1},{65,33},{97,65},{2,98}... | collective-permute-start | bytes 1769480 | tf_op jit(solution)/shard_map/ppermute | solution.py:30
  249.1 24.2 %collective-permute-start.28 = (bf16[384,768]{1,0:T(8,128)(2,1)S(1)}, bf16[384,768]{1,0:T(8,128)(2,1)S(1)}, u32[]{:S(2)}, u32[]{:S(2)}) collective-permute-start(bf16[384,768]{1,0:T(8,128)(2,1)S(1)} %get-tuple-element.59), channel_id=1, source_target_pairs={{0,32},{32,64},{64,96},{96,0},{1,33},{33,65},{65,97},{97,1},{2,34}... | collective-permute-start | bytes 1769480 | tf_op jit(solution)/shard_map/ppermute | solution.py:30
  251.0 22.6 %collective-permute-start.29 = (bf16[384,768]{1,0:T(8,128)(2,1)S(1)}, bf16[384,768]{1,0:T(8,128)(2,1)S(1)}, u32[]{:S(2)}, u32[]{:S(2)}) collective-permute-start(bf16[384,768]{1,0:T(8,128)(2,1)S(1)} %get-tuple-element.60), channel_id=1, source_target_pairs={{0,96},{32,0},{64,32},{96,64},{1,97},{33,1},{65,33},{97,65},{2,98}... | collective-permute-start | bytes 1769480 | tf_op jit(solution)/shard_map/ppermute | solution.py:30
  263.0 15.7 %collective-permute-start.37 = (bf16[96,768]{1,0:T(8,128)(2,1)S(1)}, bf16[96,768]{1,0:T(8,128)(2,1)S(1)}, u32[]{:S(2)}, u32[]{:S(2)}) collective-permute-start(bf16[96,768]{1,0:T(8,128)(2,1)S(1)} %get-tuple-element.71), channel_id=1, source_target_pairs={{0,8},{8,16},{16,24},{24,0},{1,9},{9,17},{17,25},{25,1},{2,10},{10... | collective-permute-start | bytes 442376 | tf_op jit(solution)/shard_map/ppermute | solution.py:30
  263.3 19.8 %collective-permute-start.38 = (bf16[96,768]{1,0:T(8,128)(2,1)S(1)}, bf16[96,768]{1,0:T(8,128)(2,1)S(1)}, u32[]{:S(2)}, u32[]{:S(2)}) collective-permute-start(bf16[96,768]{1,0:T(8,128)(2,1)S(1)} %get-tuple-element.72), channel_id=1, source_target_pairs={{0,24},{8,0},{16,8},{24,16},{1,25},{9,1},{17,9},{25,17},{2,26},{10... | collective-permute-start | bytes 442376 | tf_op jit(solution)/shard_map/ppermute | solution.py:30
  267.2 16.0 %collective-permute-start.39 = (bf16[96,768]{1,0:T(8,128)(2,1)S(1)}, bf16[96,768]{1,0:T(8,128)(2,1)S(1)}, u32[]{:S(2)}, u32[]{:S(2)}) collective-permute-start(bf16[96,768]{1,0:T(8,128)(2,1)S(1)} %get-tuple-element.73), channel_id=1, source_target_pairs={{0,16},{8,24},{16,0},{24,8},{1,17},{9,25},{17,1},{25,9},{2,18},{10... | collective-permute-start | bytes 442376 | tf_op jit(solution)/shard_map/ppermute | solution.py:30
  274.5 10.2 %collective-permute-start.30 = (bf16[96,768]{1,0:T(8,128)(2,1)S(1)}, bf16[96,768]{1,0:T(8,128)(2,1)S(1)}, u32[]{:S(2)}, u32[]{:S(2)}) collective-permute-start(bf16[96,768]{1,0:T(8,128)(2,1)S(1)} %get-tuple-element.62), channel_id=1, source_target_pairs={{0,8},{8,16},{16,24},{24,0},{1,9},{9,17},{17,25},{25,1},{2,10},{10... | collective-permute-start | bytes 442376 | tf_op jit(solution)/shard_map/ppermute | solution.py:30
  274.9 16.7 %collective-permute-start.31 = (bf16[96,768]{1,0:T(8,128)(2,1)S(1)}, bf16[96,768]{1,0:T(8,128)(2,1)S(1)}, u32[]{:S(2)}, u32[]{:S(2)}) collective-permute-start(bf16[96,768]{1,0:T(8,128)(2,1)S(1)} %get-tuple-element.63), channel_id=1, source_target_pairs={{0,24},{8,0},{16,8},{24,16},{1,25},{9,1},{17,9},{25,17},{2,26},{10... | collective-permute-start | bytes 442376 | tf_op jit(solution)/shard_map/ppermute | solution.py:30
  278.7 14.7 %collective-permute-start.32 = (bf16[96,768]{1,0:T(8,128)(2,1)S(1)}, bf16[96,768]{1,0:T(8,128)(2,1)S(1)}, u32[]{:S(2)}, u32[]{:S(2)}) collective-permute-start(bf16[96,768]{1,0:T(8,128)(2,1)S(1)} %get-tuple-element.64), channel_id=1, source_target_pairs={{0,16},{8,24},{16,0},{24,8},{1,17},{9,25},{17,1},{25,9},{2,18},{10... | collective-permute-start | bytes 442376 | tf_op jit(solution)/shard_map/ppermute | solution.py:30
  (20 other events, 122.1 us)
